TPU v7x, 32 devices: a whole 2x2x4 slice. The times are simulated.
32 devices in a mesh: groups: 2 (over y), space: 4 (over z), ckpt: 2 (over x), rep: 2 (over core).
Axes of the slice: x: 2, y: 2, z: 4, core: 2. Of those that a mesh axis runs over, the one named last changes fastest.
Arguments:
- adj_disp: bfloat16 [320, 96, 768], P(('groups', 'space', 'rep'), None, 'ckpt'), parts along dimension 0, may hold values from -6 to 6
- adj_vel: bfloat16 [320, 96, 768], P(('groups', 'space', 'rep'), None, 'ckpt'), parts along dimension 0, may hold values from -6 to 6
- tangent_blocks: bfloat16 [320, 96, 768], P(('groups', 'space', 'rep')), parts along dimension 0, may hold values from -0.21875 to 0.21875
- block_cols: int32 [320, 8], P(('groups', 'space', 'rep')), parts along dimension 0, may hold values from 0 to 159, as said below
- inv_mass: float32 [320, 96], P(('groups', 'space', 'rep')), parts along dimension 0, may hold values from 0.25 to 1
- joint_stiff: float32 [320, 96], P(('groups', 'space', 'rep')), parts along dimension 0, may hold values from 0.2 to 1
- contact: int32 [3, 320], P(None, ('groups', 'space', 'rep')), parts along dimension 1, may hold values 0 or 1
- states: float32 [3, 320, 96], P(None, ('groups', 'space', 'rep'), 'ckpt'), parts along dimension 1, may hold values from -4 to 4
Outputs:
- disp_out: float32 [320, 96, 768], P(('groups', 'space', 'rep'), None, 'ckpt'), parts along dimension 0
- vel_out: float32 [320, 96, 768], P(('groups', 'space', 'rep'), None, 'ckpt'), parts along dimension 0
There are 2 independent parts, one for each index of `groups`. A program takes and returns all parts, laid end to end along the dimension named above; each array names one. Nothing has to cross between parts.
Inputs may be any that keep to these rules, and one draw needn't show every extreme that they name: `block_cols`: every block column lies within 4 block rows of its own block row, counted cyclically over the 160 block rows; each block row lists itself and the rows exactly 4 before and after it.
All inputs are finite; a program needn't handle non-finite values. No bound on the sum of `contact` on one device may be relied on, other than what follows from the above.
Results may differ from a plain program's by a relative error of at most 0.015.
Values may be sent and summed in bfloat16 or wider, within the bound.
No kernel may reach another device: no remote copies, remote signals or barrier semaphores. Data moves between devices by JAX's collectives and lax.ppermute only.
A program may use at most 128 MiB of HBM per device.

v0:
```python
import jax
import jax.numpy as jnp
from jax import lax
from jax.sharding import PartitionSpec as P

HB = 4
WINDOW = 3


def passed_along(array, axis, by):
    length = lax.axis_size(axis)
    return lax.ppermute(array, axis, [(i, (i + by) % length) for i in range(length)])


def body(adj_disp, adj_vel, tangent_blocks, block_cols, inv_mass, joint_stiff, contact, states):
    rows = tangent_blocks.shape[0]
    width = tangent_blocks.shape[1]
    slots = block_cols.shape[1]
    total_rows = rows * lax.axis_size(("space", "rep"))
    first = lax.axis_index(("space", "rep")) * rows
    local = jnp.arange(rows, dtype=jnp.int32)
    offset = jnp.mod(block_cols - (first + local)[:, None] + HB, total_rows) - HB
    position = local[:, None] + HB + offset
    disp = adj_disp.astype(jnp.float32)
    vel = adj_vel.astype(jnp.float32)
    accel = jnp.zeros(disp.shape, jnp.float32)
    for back in range(WINDOW):
        step = WINDOW - 1 - back
        state_now = lax.all_gather(states[step], "ckpt", axis=1, tiled=True)
        total = accel + 0.5 * vel
        packed = (inv_mass[:, :, None] * total).astype(jnp.bfloat16)
        coeff = (
            3.0 * joint_stiff * contact[step].astype(jnp.float32)[:, None] * state_now * state_now
        )
        lower = passed_along(packed[rows - HB :], ("space", "rep"), 1)
        upper = passed_along(packed[:HB], ("space", "rep"), -1)
        extended = jnp.concatenate([lower, packed, upper], axis=0)
        picked = extended[position].reshape(rows, slots * width, packed.shape[2])
        product = jnp.einsum(
            "bik,bkr->bir", tangent_blocks, picked, preferred_element_type=jnp.float32
        )
        image = product + coeff[:, :, None] * packed.astype(jnp.float32)
        disp = disp - image
        accel = 0.5 * disp + 0.5 * vel
        vel = vel + disp
    return (disp, vel)


def solution(mesh):
    placed = (
        P(("groups", "space", "rep"), None, "ckpt"),
        P(("groups", "space", "rep"), None, "ckpt"),
        P(("groups", "space", "rep"), None, None),
        P(("groups", "space", "rep"), None),
        P(("groups", "space", "rep"), None),
        P(("groups", "space", "rep"), None),
        P(None, ("groups", "space", "rep")),
        P(None, ("groups", "space", "rep"), "ckpt"),
    )
    return jax.shard_map(
        body,
        mesh=mesh,
        in_specs=placed,
        out_specs=(
            P(("groups", "space", "rep"), None, "ckpt"),
            P(("groups", "space", "rep"), None, "ckpt"),
        ),
        check_vma=False,
    )
```

profile of v0, /device:TPU:0, one launch (start us, length us, event | category | flops | bytes accessed | tf_op | source)
XLA Modules:
  0.0 129.3 jit_solution(14847695931026815950)
XLA Ops:
  0.7 0.9 broadcast_multiply_fusion
  1.5 1.7 %fusion = bf16[20,96,384]{2,1,0:T(8,128)(2,1)S(1)} fusion(bf16[20,96,384]{2,1,0:T(8,128)(2,1)} %param.9, f32[20,96]{1,0:T(8,128)S(1)} %broadcast_multiply_fusion), kind=kLoop, calls=%fused_computation.5 | loop fusion | flops 2211840 | bytes 2956800 | tf_op jit(solution)/shard_map/convert_element_type | solution.py:31
  3.3 1.1 copy-done.3
  4.4 0.9 fusion.10
  5.7 4.0 %collective-permute-start.1 = (bf16[4,96,384]{2,1,0:T(8,128)(2,1)}, bf16[4,96,384]{2,1,0:T(8,128)(2,1)S(1)}, u32[]{:S(2)}, u32[]{:S(2)}) collective-permute-start(bf16[4,96,384]{2,1,0:T(8,128)(2,1)} %get-tuple-element.7), channel_id=1, source_target_pairs={{0,13},{1,0},{4,1},{5,4},{8,5},{9,8},{12,9},{13,12},{2,15},{3,2},{... | collective-permute-start | bytes 884744 | tf_op jit(solution)/shard_map/ppermute | solution.py:12
  10.3 0.7 compare_select_fusion
  11.1 0.7 copy.21
  11.7 1.4 %reshape.55 = s32[160]{0:T(256)} reshape(s32[20,8]{1,0:T(8,128)} %copy.21) | data formatting | bytes 1280 | tf_op jit(solution)/shard_map/broadcast_in_dim | solution.py:38
  13.1 1.4 %fusion.11 = (f32[1,20,48]{2,1,0:T(8,128)}, f32[1,20,48]{2,1,0:T(8,128)}, f32[1,20,48]{2,1,0:T(8,128)}) fusion(f32[3,20,48]{2,1,0:T(8,128)} %param.15), kind=kLoop, calls=%fused_computation.37 | loop fusion | bytes 23040 | tf_op jit(solution)/shard_map/slice | solution.py:29
  14.5 1.4 %copy.30 = f32[1,20,48]{1,0,2:T(1,128)} copy(f32[1,20,48]{2,1,0:T(8,128)} %get-tuple-element.8) | data formatting | bytes 7680
  15.9 6.1 %all-gather.2 = f32[1,20,96]{1,0,2:T(1,128)} all-gather(f32[1,20,48]{1,0,2:T(1,128)} %copy.30), channel_id=4, replica_groups=mesh['groups'=2,'space'=4,'ckpt'=2,'rep'=2] {'ckpt'}, dimensions={2}, use_global_device_ids=true | all-gather | bytes 11520 | tf_op jit(solution)/shard_map/all_gather | solution.py:29
  21.9 1.5 %copy.27 = f32[1,20,96]{2,1,0:T(8,128)} copy(f32[1,20,96]{1,0,2:T(1,128)} %all-gather.2) | data formatting | bytes 15360 | tf_op jit(solution)/shard_map/all_gather | solution.py:29
  23.4 1.4 %copy.29 = f32[1,20,48]{1,0,2:T(1,128)} copy(f32[1,20,48]{2,1,0:T(8,128)} %get-tuple-element.9) | data formatting | bytes 7680
  24.8 4.8 %all-gather.1 = f32[1,20,96]{1,0,2:T(1,128)} all-gather(f32[1,20,48]{1,0,2:T(1,128)} %copy.29), channel_id=3, replica_groups=mesh['groups'=2,'space'=4,'ckpt'=2,'rep'=2] {'ckpt'}, dimensions={2}, use_global_device_ids=true | all-gather | bytes 11520 | tf_op jit(solution)/shard_map/all_gather | solution.py:29
  29.6 1.5 %copy.25 = f32[1,20,96]{2,1,0:T(8,128)} copy(f32[1,20,96]{1,0,2:T(1,128)} %all-gather.1) | data formatting | bytes 15360 | tf_op jit(solution)/shard_map/all_gather | solution.py:29
  31.1 1.4 %copy.28 = f32[1,20,48]{1,0,2:T(1,128)} copy(f32[1,20,48]{2,1,0:T(8,128)} %get-tuple-element.10) | data formatting | bytes 7680
  32.5 5.4 %all-gather = f32[1,20,96]{1,0,2:T(1,128)} all-gather(f32[1,20,48]{1,0,2:T(1,128)} %copy.28), channel_id=2, replica_groups=mesh['groups'=2,'space'=4,'ckpt'=2,'rep'=2] {'ckpt'}, dimensions={2}, use_global_device_ids=true | all-gather | bytes 11520 | tf_op jit(solution)/shard_map/all_gather | solution.py:29
  37.9 1.5 %copy.23 = f32[1,20,96]{2,1,0:T(8,128)} copy(f32[1,20,96]{1,0,2:T(1,128)} %all-gather) | data formatting | bytes 15360 | tf_op jit(solution)/shard_map/all_gather | solution.py:29
  40.0 1.5 %multiply_multiply_fusion = (f32[20,96]{1,0:T(8,128)}, f32[20,96]{1,0:T(8,128)}, f32[20,96]{1,0:T(8,128)}) fusion(f32[1,20,96]{2,1,0:T(8,128)} %copy.27, f32[20,96]{1,0:T(8,128)} %param.13, f32[20]{0:T(128)} %get-tuple-element.14, f32[1,20,96]{2,1,0:T(8,128)} %copy.23, f32[20]{0:T(128)} %get-tuple-element.15, f32[1,20,96]{2,1,0:T(8,128)} %copy.25, ...), kind=kLoop, calls=%fused_computation.19 | loop fusion | flops 17280 | bytes 54000 | tf_op jit(solution)/shard_map/mul | solution.py:33
  41.5 3.0 %pad_maximum_fusion = bf16[28,96,384]{2,1,0:T(8,128)(2,1)} fusion(bf16[4,96,384]{2,1,0:T(8,128)(2,1)S(1)} %collective-permute-done.1, bf16[20,96,384]{2,1,0:T(8,128)(2,1)} %copy-done.3, bf16[4,96,384]{2,1,0:T(8,128)(2,1)S(1)} %collective-permute-done), kind=kLoop, calls=%fused_computation.14 | loop fusion | flops 2064384 | bytes 4128768 | tf_op jit(solution)/shard_map/concatenate | solution.py:37
  44.5 10.3 %gather_fusion = bf16[160,96,384]{2,1,0:T(8,128)(2,1)} fusion(bf16[28,96,384]{2,1,0:T(8,128)(2,1)} %pad_maximum_fusion, s32[1024]{0:T(1024)S(1)} %pad_clamp_fusion), kind=kCustom, calls=%fused_computation | custom fusion | bytes 23593600 | tf_op jit(solution)/shard_map/gather | solution.py:38
  54.8 7.6 %multiply_convert_fusion.1 = (bf16[20,96,384]{2,1,0:T(8,128)(2,1)S(1)}, f32[20,96,384]{2,1,0:T(8,128)}) fusion(f32[20,96]{1,0:T(8,128)S(1)} %copy-done.4, bf16[20,96,384]{2,1,0:T(8,128)(2,1)} %param.9, f32[20,96]{1,0:T(8,128)S(1)} %copy-done.6, bf16[20,96,768]{2,1,0:T(8,128)(2,1)S(1)} %copy-done, bf16[20,768,384]{2,1,0:T(8,128)(2,1)} %bitcast.34, ...), kind=kOutput, calls=%fused_computation.13 | convolution fusion | flops 1142046720 | bytes 22141440 | tf_op jit(solution)/shard_map/bik,bkr->bir/dot_general | solution.py:39
  62.5 3.5 %collective-permute-start.3 = (bf16[4,96,384]{2,1,0:T(8,128)(2,1)S(1)}, bf16[4,96,384]{2,1,0:T(8,128)(2,1)S(1)}, u32[]{:S(2)}, u32[]{:S(2)}) collective-permute-start(bf16[4,96,384]{2,1,0:T(8,128)(2,1)S(1)} %get-tuple-element.5), channel_id=1, source_target_pairs={{0,13},{1,0},{4,1},{5,4},{8,5},{9,8},{12,9},{13,12},{2,15},{3,2},{... | collective-permute-start | bytes 884744 | tf_op jit(solution)/shard_map/ppermute | solution.py:12
  66.0 7.3 %collective-permute-done.2 = bf16[4,96,384]{2,1,0:T(8,128)(2,1)S(1)} collective-permute-done((bf16[4,96,384]{2,1,0:T(8,128)(2,1)S(1)}, bf16[4,96,384]{2,1,0:T(8,128)(2,1)S(1)}, u32[]{:S(2)}, u32[]{:S(2)}) %collective-permute-start.2) | collective-permute-done | bytes 294944 | tf_op jit(solution)/shard_map/ppermute | solution.py:12
  73.3 1.6 %pad_maximum_fusion.1 = bf16[28,96,384]{2,1,0:T(8,128)(2,1)} fusion(bf16[4,96,384]{2,1,0:T(8,128)(2,1)S(1)} %collective-permute-done.3, bf16[20,96,384]{2,1,0:T(8,128)(2,1)S(1)} %get-tuple-element.17, bf16[4,96,384]{2,1,0:T(8,128)(2,1)S(1)} %collective-permute-done.2), kind=kLoop, calls=%fused_computation.15 | loop fusion | flops 2064384 | bytes 4128768 | tf_op jit(solution)/shard_map/concatenate | solution.py:37
  74.9 10.3 %gather_fusion.1 = bf16[160,96,384]{2,1,0:T(8,128)(2,1)} fusion(bf16[28,96,384]{2,1,0:T(8,128)(2,1)} %pad_maximum_fusion.1, s32[1024]{0:T(1024)S(1)} %pad_clamp_fusion), kind=kCustom, calls=%fused_computation.1 | custom fusion | bytes 23593600 | tf_op jit(solution)/shard_map/gather | solution.py:38
  85.2 10.4 %multiply_convert_fusion = (bf16[20,96,384]{2,1,0:T(8,128)(2,1)S(1)}, f32[20,96,384]{2,1,0:T(8,128)}) fusion(f32[20,96]{1,0:T(8,128)S(1)} %copy-done.4, f32[20,96,384]{2,1,0:T(8,128)} %get-tuple-element.18, bf16[20,96,384]{2,1,0:T(8,128)(2,1)} %param.9, bf16[20,96,384]{2,1,0:T(8,128)(2,1)} %copy-done.1, f32[20,96]{1,0:T(8,128)S(1)} %copy-done.5, ...), kind=kOutput, calls=%fused_computation.12 | convolution fusion | flops 1142784000 | bytes 25082880 | tf_op jit(solution)/shard_map/bik,bkr->bir/dot_general | solution.py:39
  95.7 3.5 %collective-permute-start.5 = (bf16[4,96,384]{2,1,0:T(8,128)(2,1)S(1)}, bf16[4,96,384]{2,1,0:T(8,128)(2,1)S(1)}, u32[]{:S(2)}, u32[]{:S(2)}) collective-permute-start(bf16[4,96,384]{2,1,0:T(8,128)(2,1)S(1)} %get-tuple-element.3), channel_id=1, source_target_pairs={{0,13},{1,0},{4,1},{5,4},{8,5},{9,8},{12,9},{13,12},{2,15},{3,2},{... | collective-permute-start | bytes 884744 | tf_op jit(solution)/shard_map/ppermute | solution.py:12
  99.2 6.3 %collective-permute-done.4 = bf16[4,96,384]{2,1,0:T(8,128)(2,1)S(1)} collective-permute-done((bf16[4,96,384]{2,1,0:T(8,128)(2,1)S(1)}, bf16[4,96,384]{2,1,0:T(8,128)(2,1)S(1)}, u32[]{:S(2)}, u32[]{:S(2)}) %collective-permute-start.4) | collective-permute-done | bytes 294944 | tf_op jit(solution)/shard_map/ppermute | solution.py:12
  105.5 1.7 %pad_maximum_fusion.2 = bf16[28,96,384]{2,1,0:T(8,128)(2,1)} fusion(bf16[4,96,384]{2,1,0:T(8,128)(2,1)S(1)} %collective-permute-done.5, bf16[20,96,384]{2,1,0:T(8,128)(2,1)S(1)} %get-tuple-element.19, bf16[4,96,384]{2,1,0:T(8,128)(2,1)S(1)} %collective-permute-done.4), kind=kLoop, calls=%fused_computation.16 | loop fusion | flops 2064384 | bytes 4128768 | tf_op jit(solution)/shard_map/concatenate | solution.py:37
  107.2 10.3 %gather_fusion.2 = bf16[160,96,384]{2,1,0:T(8,128)(2,1)} fusion(bf16[28,96,384]{2,1,0:T(8,128)(2,1)} %pad_maximum_fusion.2, s32[1024]{0:T(1024)S(1)} %pad_clamp_fusion), kind=kCustom, calls=%fused_computation.2 | custom fusion | bytes 23593600 | tf_op jit(solution)/shard_map/gather | solution.py:38
  117.5 11.8 %fusion.5 = (f32[20,96,384]{2,1,0:T(8,128)}, f32[20,96,384]{2,1,0:T(8,128)}) fusion(f32[20,96,384]{2,1,0:T(8,128)} %get-tuple-element.20, f32[20,96,384]{2,1,0:T(8,128)} %get-tuple-element.18, bf16[20,96,384]{2,1,0:T(8,128)(2,1)} %param.9, bf16[20,96,384]{2,1,0:T(8,128)(2,1)} %copy-done.2, f32[20,96]{1,0:T(8,128)S(1)} %copy-done.7, ...), kind=kOutput, calls=%fused_computation.18 | convolution fusion | flops 1138360320 | bytes 29498880 | tf_op jit(solution)/shard_map/bik,bkr->bir/dot_general | solution.py:39
  (29 shorter events, 2.0 us)
Async XLA Ops:
  0.6 54.2 %copy-start = (bf16[20,96,768]{2,1,0:T(8,128)(2,1)S(1)}, bf16[20,96,768]{2,1,0:T(8,128)(2,1)}, u32[]{:S(2)}) copy-start(bf16[20,96,768]{2,1,0:T(8,128)(2,1)} %param.10) | copy-start | bytes 8847364
  0.6 9.1 %copy-start.8 = (s32[3,20]{1,0:T(4,128)S(1)}, s32[3,20]{1,0:T(4,128)}, u32[]{:S(2)}) copy-start(s32[3,20]{1,0:T(4,128)} %param.14) | copy-start | bytes 724
  3.3 1.1 copy-start.3
  5.2 36.2 %collective-permute-start = (bf16[4,96,384]{2,1,0:T(8,128)(2,1)}, bf16[4,96,384]{2,1,0:T(8,128)(2,1)S(1)}, u32[]{:S(2)}, u32[]{:S(2)}) collective-permute-start(bf16[4,96,384]{2,1,0:T(8,128)(2,1)} %get-tuple-element.6), channel_id=1, source_target_pairs={{0,1},{1,4},{4,5},{5,8},{8,9},{9,12},{12,13},{13,0},{2,3},{3,6},{6... | collective-permute-start | bytes 884744 | tf_op jit(solution)/shard_map/ppermute | solution.py:12
  5.7 35.8 %collective-permute-start.1 = (bf16[4,96,384]{2,1,0:T(8,128)(2,1)}, bf16[4,96,384]{2,1,0:T(8,128)(2,1)S(1)}, u32[]{:S(2)}, u32[]{:S(2)}) collective-permute-start(bf16[4,96,384]{2,1,0:T(8,128)(2,1)} %get-tuple-element.7), channel_id=1, source_target_pairs={{0,13},{1,0},{4,1},{5,4},{8,5},{9,8},{12,9},{13,12},{2,15},{3,2},{... | collective-permute-start | bytes 884744 | tf_op jit(solution)/shard_map/ppermute | solution.py:12
  44.5 10.3 %copy-start.4 = (f32[20,96]{1,0:T(8,128)S(1)}, f32[20,96]{1,0:T(8,128)}, u32[]{:S(2)}) copy-start(f32[20,96]{1,0:T(8,128)} %param.12) | copy-start | bytes 23044
  44.5 10.3 %copy-start.6 = (f32[20,96]{1,0:T(8,128)S(1)}, f32[20,96]{1,0:T(8,128)}, u32[]{:S(2)}) copy-start(f32[20,96]{1,0:T(8,128)} %get-tuple-element.12) | copy-start | bytes 23044
  62.3 10.9 %copy-start.1 = (bf16[20,96,384]{2,1,0:T(8,128)(2,1)}, bf16[20,96,384]{2,1,0:T(8,128)(2,1)S(1)}, u32[]{:S(2)}) copy-start(bf16[20,96,384]{2,1,0:T(8,128)(2,1)S(1)} %get-tuple-element.17) | copy-start | bytes 4423684
  62.4 10.9 %collective-permute-start.2 = (bf16[4,96,384]{2,1,0:T(8,128)(2,1)S(1)}, bf16[4,96,384]{2,1,0:T(8,128)(2,1)S(1)}, u32[]{:S(2)}, u32[]{:S(2)}) collective-permute-start(bf16[4,96,384]{2,1,0:T(8,128)(2,1)S(1)} %get-tuple-element.4), channel_id=1, source_target_pairs={{0,1},{1,4},{4,5},{5,8},{8,9},{9,12},{12,13},{13,0},{2,3},{3,6},{6... | collective-permute-start | bytes 884744 | tf_op jit(solution)/shard_map/ppermute | solution.py:12
  62.5 10.8 %collective-permute-start.3 = (bf16[4,96,384]{2,1,0:T(8,128)(2,1)S(1)}, bf16[4,96,384]{2,1,0:T(8,128)(2,1)S(1)}, u32[]{:S(2)}, u32[]{:S(2)}) collective-permute-start(bf16[4,96,384]{2,1,0:T(8,128)(2,1)S(1)} %get-tuple-element.5), channel_id=1, source_target_pairs={{0,13},{1,0},{4,1},{5,4},{8,5},{9,8},{12,9},{13,12},{2,15},{3,2},{... | collective-permute-start | bytes 884744 | tf_op jit(solution)/shard_map/ppermute | solution.py:12
  74.9 10.3 %copy-start.5 = (f32[20,96]{1,0:T(8,128)S(1)}, f32[20,96]{1,0:T(8,128)}, u32[]{:S(2)}) copy-start(f32[20,96]{1,0:T(8,128)} %get-tuple-element.13) | copy-start | bytes 23044
  95.6 10.0 %copy-start.2 = (bf16[20,96,384]{2,1,0:T(8,128)(2,1)}, bf16[20,96,384]{2,1,0:T(8,128)(2,1)S(1)}, u32[]{:S(2)}) copy-start(bf16[20,96,384]{2,1,0:T(8,128)(2,1)S(1)} %get-tuple-element.19) | copy-start | bytes 4423684
  95.6 9.9 %collective-permute-start.4 = (bf16[4,96,384]{2,1,0:T(8,128)(2,1)S(1)}, bf16[4,96,384]{2,1,0:T(8,128)(2,1)S(1)}, u32[]{:S(2)}, u32[]{:S(2)}) collective-permute-start(bf16[4,96,384]{2,1,0:T(8,128)(2,1)S(1)} %get-tuple-element.2), channel_id=1, source_target_pairs={{0,1},{1,4},{4,5},{5,8},{8,9},{9,12},{12,13},{13,0},{2,3},{3,6},{6... | collective-permute-start | bytes 884744 | tf_op jit(solution)/shard_map/ppermute | solution.py:12
  95.7 9.8 %collective-permute-start.5 = (bf16[4,96,384]{2,1,0:T(8,128)(2,1)S(1)}, bf16[4,96,384]{2,1,0:T(8,128)(2,1)S(1)}, u32[]{:S(2)}, u32[]{:S(2)}) collective-permute-start(bf16[4,96,384]{2,1,0:T(8,128)(2,1)S(1)} %get-tuple-element.3), channel_id=1, source_target_pairs={{0,13},{1,0},{4,1},{5,4},{8,5},{9,8},{12,9},{13,12},{2,15},{3,2},{... | collective-permute-start | bytes 884744 | tf_op jit(solution)/shard_map/ppermute | solution.py:12
  107.2 10.3 %copy-start.7 = (f32[20,96]{1,0:T(8,128)S(1)}, f32[20,96]{1,0:T(8,128)}, u32[]{:S(2)}) copy-start(f32[20,96]{1,0:T(8,128)} %get-tuple-element.11) | copy-start | bytes 23044
where the time goes:
time: 130 us; the launch traced here: 129 us
  local copies, waits for them, and re-layouts  45 us (35%)
  matrix products  29.8 us (23%)
  blocking collectives  16.3 us (13%)
  waiting for transfers between devices  13.6 us (10%)
  other arithmetic  12.3 us (9%)
  starting transfers between devices  11.7 us (9%)
    gather x3, local copies, waits for them, and re-layouts, body(): picked = extended[position].reshape(rows, slots * width, packed.shape[2])  30.9 us
    dot_general x3, matrix products, body(): jnp.einsum('bik,bkr->bir', tangent_blocks, picked, preferred_element_type...  29.8 us
    all_gather x3, blocking collectives, body(): state_now = lax.all_gather(states[step], 'ckpt', axis=1, tiled=True)  16.3 us
    ppermute x6, waiting for transfers between devices, passed_along(): lax.ppermute(array, axis, [(i, (i + by) % length) for i in range(length)])  13.6 us
    ppermute x6, starting transfers between devices, passed_along(): lax.ppermute(array, axis, [(i, (i + by) % length) for i in range(length)])  11.7 us
    concatenate x3, other arithmetic, body(): extended = jnp.concatenate([lower, packed, upper], axis=0)  6.24 us
    unnamed x21, local copies, waits for them, and re-layouts  5.3 us
    all_gather x3, local copies, waits for them, and re-layouts, body(): state_now = lax.all_gather(states[step], 'ckpt', axis=1, tiled=True)  4.42 us
  transfers between devices with their start and end apart: 6, of which 2 were waited for; matrix products, arithmetic and copies ran while one was open for 12% of the time, Pallas kernels for 0%

commit v1 on v0

v1 whole, which is shorter than its diff:
```python
import functools
import jax
import jax.numpy as jnp
from jax import lax
from jax.experimental import pallas as pl
from jax.experimental.pallas import tpu as pltpu
from jax.sharding import PartitionSpec as P

HB = 4
WINDOW = 3
RING = ("space", "rep")
VMEM_LIMIT = 24 * 1024 * 1024


def ring_pairs(ring):
    inner = [(i, i ^ 1) for i in range(ring)]
    outer = [(i, (i + 1) % ring) for i in range(1, ring, 2)]
    outer = outer + [(b, a) for a, b in outer]
    return inner, outer


def slots_of(cols, r, first, total):
    out = []
    for k in range(cols.shape[1]):
        off = cols[r, k] - (first + r)
        off = jnp.where(off > HB, off - total, off)
        off = jnp.where(off < -HB, off + total, off)
        out.append(r + HB + off)
    return out


def product(blocks, packed, cols, r, first, total):
    picked = jnp.concatenate([packed[p] for p in slots_of(cols, r, first, total)], axis=0)
    return jnp.dot(blocks[r], picked, preferred_element_type=jnp.float32)


def tiled(column, lanes):
    return jnp.concatenate([column] * (lanes // 128), axis=1)


def advance(r, first, total, blocks, packed, cols, coeff, disp_old, vel_old):
    lanes = packed.shape[2]
    image = product(blocks, packed, cols, r, first, total)
    image = image + tiled(coeff[r], lanes) * packed[r + HB].astype(jnp.float32)
    disp = disp_old[r].astype(jnp.float32) - image
    vel = vel_old[r].astype(jnp.float32) + disp
    return disp, vel


def head(vel0, inv_mass, _v, out_b, out_a):
    rows, _, lanes = vel0.shape
    rep = lax.axis_index("rep")
    mass = inv_mass[...].T
    for j in range(HB):
        def packed(r):
            m = jnp.broadcast_to(mass[:, r : r + 1], (mass.shape[0], lanes))
            return m * (0.5 * vel0[r].astype(jnp.float32))
        low, high = packed(j), packed(rows - HB + j)
        out_b[j] = jnp.where(rep == 0, low, high).astype(jnp.bfloat16)
        out_a[j] = jnp.where(rep == 0, high, low).astype(jnp.bfloat16)


def main_first(
    total, pieces, blocks, vel0, disp0, halo, cols, contact, inv_mass, stiff, *rest
):
    shards, rest = rest[:pieces], rest[pieces:]
    _b, _h, now, later, disp, vel, mass_b, coeff, out_a, turned = rest
    rows, _, lanes = vel0.shape
    rep = lax.axis_index("rep")
    me = lax.axis_index("ckpt")
    first = (lax.axis_index("space") * 2 + rep) * rows
    width = shards[0].shape[2]
    mass = inv_mass[...].T
    for r in range(rows):
        m = jnp.broadcast_to(mass[:, r : r + 1], (mass.shape[0], 128))
        mass_b[r] = m
        now[r + HB] = (tiled(m, lanes) * (0.5 * vel0[r].astype(jnp.float32))).astype(
            jnp.bfloat16
        )
    bent = 3.0 * stiff[...].T
    for s in range(WINDOW):
        for j in range(pieces):
            source = lax.rem(me + j, pieces)
            turned[pl.ds(pl.multiple_of(source * width, 8), width), :] = shards[j][s].T
        state = turned[...]
        full = bent * state * state
        for r in range(rows):
            flag = contact[s, r].astype(jnp.float32)
            coeff[s, r] = jnp.broadcast_to(full[:, r : r + 1], (full.shape[0], 128)) * flag
    at_a = (rows + HB) * (1 - rep)
    for j in range(HB):
        now[at_a + j] = halo[j]
    b_start = (rows - HB) * rep
    for j in range(HB):
        disp[b_start + j] = disp0[b_start + j].astype(jnp.float32)
        vel[b_start + j] = vel0[b_start + j].astype(jnp.float32)
    start = HB * (1 - rep)

    def one(i, carry):
        r = start + i
        d, v = advance(r, first, total, blocks, now, cols, coeff.at[WINDOW - 1], disp0, vel0)
        disp[r] = d
        vel[r] = v
        later[r + HB] = (tiled(mass_b[r], lanes) * v).astype(jnp.bfloat16)
        return carry

    lax.fori_loop(0, rows - HB, one, 0, unroll=2)
    a_start = (rows - HB) * (1 - rep)
    for j in range(HB):
        out_a[j] = later[a_start + HB + j]


def middle(total, step, edge, *refs):
    cols = refs[8]
    blocks, now, later, disp, vel, mass_b, coeff, halo, out = refs[9:]
    rows, _, lanes = disp.shape
    rep = lax.axis_index("rep")
    first = (lax.axis_index("space") * 2 + rep) * rows
    side = rep if edge else 1 - rep
    for j in range(HB):
        now[(rows + HB) * side + j] = halo[j]
    if edge:
        start, count = (rows - HB) * rep, HB
    else:
        start, count = HB * (1 - rep), rows - HB

    def one(i, carry):
        r = start + i
        d, v = advance(r, first, total, blocks, now, cols, coeff.at[step], disp, vel)
        disp[r] = d
        vel[r] = v
        p = (tiled(mass_b[r], lanes) * v).astype(jnp.bfloat16)
        later[r + HB] = p
        if edge:
            out[i] = p
        return carry

    lax.fori_loop(0, count, one, 0, unroll=2)
    if not edge:
        for j in range(HB):
            out[j] = later[(rows - HB) * side + HB + j]


def final(total, step, edge, *refs):
    if edge:
        cols = refs[8]
        blocks, now, disp, vel, coeff, halo, disp_out, vel_out, sem = refs[9:]
    else:
        cols = refs[6]
        blocks, now, disp, vel, coeff, halo, disp_out, vel_out, sem = refs[7:]
    rows = disp.shape[0]
    rep = lax.axis_index("rep")
    first = (lax.axis_index("space") * 2 + rep) * rows
    side = rep if edge else 1 - rep
    for j in range(HB):
        now[(rows + HB) * side + j] = halo[j]
    if edge:
        start, count, group = (rows - HB) * rep, HB, 1
    else:
        start, count, group = HB * (1 - rep), rows - HB, HB

    def copies(g):
        at = pl.ds(start + g * group, group)
        return (
            pltpu.make_async_copy(disp.at[at], disp_out.at[at], sem.at[0, g]),
            pltpu.make_async_copy(vel.at[at], vel_out.at[at], sem.at[1, g]),
        )

    for g in range(count // group):
        def one(i, carry):
            r = start + g * group + i
            d, v = advance(r, first, total, blocks, now, cols, coeff.at[step], disp, vel)
            disp[r] = d
            vel[r] = v
            return carry

        lax.fori_loop(0, group, one, 0, unroll=True)
        for c in copies(g):
            c.start()
    for g in range(count // group):
        for c in copies(g):
            c.wait()


def body(adj_disp, adj_vel, tangent_blocks, block_cols, inv_mass, joint_stiff, contact, states):
    rows, width, lanes = adj_disp.shape
    ring = lax.axis_size(RING)
    total = rows * ring
    inner, outer = ring_pairs(ring)
    pieces = lax.axis_size("ckpt")
    f32, bf16 = jnp.float32, jnp.bfloat16
    vm = pl.BlockSpec(memory_space=pltpu.VMEM)
    sm = pl.BlockSpec(memory_space=pltpu.SMEM)
    anyspec = pl.BlockSpec(memory_space=pl.ANY)
    params = pltpu.CompilerParams(vmem_limit_bytes=VMEM_LIMIT)
    like = lambda a: pltpu.VMEM(a.shape, a.dtype)
    edge_t = pltpu.VMEM((HB, width, lanes), bf16)

    shards = [states] + [
        lax.ppermute(states, "ckpt", [((i + j) % pieces, i) for i in range(pieces)])
        for j in range(1, pieces)
    ]

    vel0, out_b, out_a = pl.pallas_call(
        head,
        name="head",
        out_shape=(like(adj_vel), edge_t, edge_t),
        in_specs=[vm] * 2,
        out_specs=(vm,) * 3,
        input_output_aliases={0: 0},
        compiler_params=params,
    )(adj_vel, inv_mass)

    halo_b = lax.ppermute(out_b, RING, outer)
    halo_a = lax.ppermute(out_a, RING, inner)

    ext = pltpu.VMEM((rows + 2 * HB, width, lanes), bf16)
    full = pltpu.VMEM((rows, width, lanes), f32)
    flops = 2 * (rows - HB) * width * tangent_blocks.shape[2] * lanes
    big = pl.CostEstimate(flops=flops, bytes_accessed=6_000_000, transcendentals=0)
    small = pl.CostEstimate(flops=flops * HB // (rows - HB), bytes_accessed=1_000_000, transcendentals=0)
    blocks, _, now, later, disp, vel, mass_b, coeff, out_a = pl.pallas_call(
        functools.partial(main_first, total, pieces),
        name="main_first",
        out_shape=(
            like(tangent_blocks), edge_t, ext, ext, full, full,
            pltpu.VMEM((rows, width, 128), f32),
            pltpu.VMEM((WINDOW, rows, width, 128), f32),
            edge_t,
        ),
        in_specs=[vm] * 4 + [sm] * 2 + [vm] * (2 + pieces),
        out_specs=(vm,) * 9,
        scratch_shapes=[pltpu.VMEM((width, rows), f32)],
        input_output_aliases={0: 0, 3: 1},
        compiler_params=params,
        cost_estimate=big,
    )(tangent_blocks, vel0, adj_disp, halo_a, block_cols, contact, inv_mass, joint_stiff, *shards)

    def run_middle(step, edge, held, halo):
        return pl.pallas_call(
            functools.partial(middle, total, step, edge),
            name=("edge" if edge else "main") + str(step),
            out_shape=tuple(like(a) for a in held) + (edge_t, edge_t),
            in_specs=[vm] * 8 + [sm],
            out_specs=(vm,) * 9,
            input_output_aliases={i: i for i in range(8)},
            compiler_params=params,
            cost_estimate=small if edge else big,
        )(*held, halo, block_cols)

    step = WINDOW - 1
    held = [blocks, now, later, disp, vel, mass_b, coeff]
    while step > 0:
        next_a = lax.ppermute(out_a, RING, inner)
        *held, _, out_b = run_middle(step, True, held, halo_b)
        halo_b = lax.ppermute(out_b, RING, outer)
        halo_a = next_a
        step -= 1
        held[1], held[2] = held[2], held[1]
        if step > 0:
            *held, _, out_a = run_middle(step, False, held, halo_a)

    blocks, now, later, disp, vel, mass_b, coeff = held
    shape = jax.ShapeDtypeStruct((rows, width, lanes), f32)
    held = [blocks, now, disp, vel, coeff]
    *held, _, disp_out, vel_out = pl.pallas_call(
        functools.partial(final, total, 0, False),
        name="main_last",
        out_shape=tuple(like(a) for a in held) + (edge_t, shape, shape),
        in_specs=[vm] * 6 + [sm],
        out_specs=(vm,) * 6 + (anyspec,) * 2,
        scratch_shapes=[pltpu.SemaphoreType.DMA((2, rows // HB - 1))],
        input_output_aliases={i: i for i in range(6)},
        compiler_params=params,
        cost_estimate=big,
    )(*held, halo_a, block_cols)
    out = pl.pallas_call(
        functools.partial(final, total, 0, True),
        name="edge_last",
        out_shape=tuple(like(a) for a in held) + (edge_t, shape, shape),
        in_specs=[vm] * 6 + [anyspec] * 2 + [sm],
        out_specs=(vm,) * 6 + (anyspec,) * 2,
        scratch_shapes=[pltpu.SemaphoreType.DMA((2, HB))],
        input_output_aliases={i: i for i in range(8)},
        compiler_params=params,
        cost_estimate=small,
    )(*held, halo_b, disp_out, vel_out, block_cols)
    return out[-2], out[-1]


def solution(mesh):
    placed = (
        P(("groups", "space", "rep"), None, "ckpt"),
        P(("groups", "space", "rep"), None, "ckpt"),
        P(("groups", "space", "rep"), None, None),
        P(("groups", "space", "rep"), None),
        P(("groups", "space", "rep"), None),
        P(("groups", "space", "rep"), None),
        P(None, ("groups", "space", "rep")),
        P(None, ("groups", "space", "rep"), "ckpt"),
    )
    return jax.shard_map(
        body,
        mesh=mesh,
        in_specs=placed,
        out_specs=(
            P(("groups", "space", "rep"), None, "ckpt"),
            P(("groups", "space", "rep"), None, "ckpt"),
        ),
        check_vma=False,
    )
```

time: 130 us -> 48.9 us (0.38)
  the two profiles are of different devices: /device:TPU:0 before, /device:TPU:1 now
where the time goes in v1:
time: 48.9 us; the launch traced here: 48.5 us
  Pallas kernels  18.7 us (38%)
  waiting for transfers between devices  11.7 us (24%)
  local copies, waits for them, and re-layouts  9.01 us (18%)
  starting transfers between devices  8.37 us (17%)
  between operations  0.73 us (1%)
    ppermute x3, waiting for transfers between devices, body(): halo_b = lax.ppermute(out_b, RING, outer)  10.6 us
    unnamed x19, local copies, waits for them, and re-layouts  9.01 us
    pallas_call x3, Pallas kernels, run_middle(): pl.pallas_call(functools.partial(middle, total, step, edge), name=('edge'...  6.66 us
    pallas_call x1, Pallas kernels, body(): pl.pallas_call(functools.partial(main_first, total, pieces), name='main_f...  5.1 us
    ppermute x2, starting transfers between devices, body(): next_a = lax.ppermute(out_a, RING, inner)  4.32 us
    pallas_call x1, Pallas kernels, body(): pl.pallas_call(functools.partial(final, total, 0, False), name='main_last...  3.7 us
    ppermute x3, starting transfers between devices, body(): halo_b = lax.ppermute(out_b, RING, outer)  2.77 us
    pallas_call x1, Pallas kernels, body(): pl.pallas_call(functools.partial(final, total, 0, True), name='edge_last'...  2.12 us
  transfers between devices with their start and end apart: 7, of which 3 were waited for; matrix products, arithmetic and copies ran while one was open for 2% of the time, Pallas kernels for 32%

profile of v1, /device:TPU:1, one launch (start us, length us, event | category | flops | bytes accessed | tf_op | source)
XLA Modules:
  0.0 48.5 jit_solution(7308763234044278764)
XLA Ops:
  0.6 0.0 copy-start.7
  0.6 1.5 %copy.100.vel0 = bf16[20,96,384]{2,1,0:T(8,128)(2,1)S(1)} copy(bf16[20,96,384]{2,1,0:T(8,128)(2,1)} %param.9) | data formatting | bytes 2949120
  2.2 0.7 %copy-done.7 = bf16[20,96,768]{2,1,0:T(8,128)(2,1)S(1)} copy-done((bf16[20,96,768]{2,1,0:T(8,128)(2,1)S(1)}, bf16[20,96,768]{2,1,0:T(8,128)(2,1)}, u32[]{:S(2)}) %copy-start.7) | copy-done | bytes 2949144
  2.9 0.2 copy.101.blocks
  3.1 0.5 %copy-done.3 = f32[20,96]{1,0:T(8,128)S(1)} copy-done((f32[20,96]{1,0:T(8,128)S(1)}, f32[20,96]{1,0:T(8,128)}, u32[]{:S(2)}) %copy-start.3) | copy-done | bytes 7704
  3.6 1.1 %head.1 = (bf16[20,96,384]{2,1,0:T(8,128)(2,1)S(1)}, bf16[4,96,384]{2,1,0:T(8,128)(2,1)}, bf16[4,96,384]{2,1,0:T(8,128)(2,1)}) custom-call(bf16[20,96,384]{2,1,0:T(8,128)(2,1)S(1)} %copy.100.vel0, f32[20,96]{1,0:T(8,128)S(1)} %copy-done.3), custom_call_target="tpu_custom_call", output_to_operand_aliasing={{0}: (0, {})} | custom-call | tf_op jit(solution)/shard_map/head/pallas_call | solution.py:204
  4.7 1.1 %copy-done = bf16[20,96,384]{2,1,0:T(8,128)(2,1)} copy-done((bf16[20,96,384]{2,1,0:T(8,128)(2,1)}, bf16[20,96,384]{2,1,0:T(8,128)(2,1)S(1)}, u32[]{:S(2)}) %copy-start) | copy-done | bytes 1474584
  5.8 0.1 collective-permute-start
  5.9 2.6 %collective-permute-start.2 = (bf16[4,96,384]{2,1,0:T(8,128)(2,1)}, bf16[4,96,384]{2,1,0:T(8,128)(2,1)S(1)}, u32[]{:S(2)}, u32[]{:S(2)}) collective-permute-start(bf16[4,96,384]{2,1,0:T(8,128)(2,1)} %get-tuple-element.53), channel_id=1, source_target_pairs={{1,4},{5,8},{9,12},{13,0},{4,1},{8,5},{12,9},{0,13},{3,6},{7,10},{... | collective-permute-start | bytes 884744 | tf_op jit(solution)/shard_map/ppermute | solution.py:214
  8.5 1.2 %collective-permute-start.1 = (f32[3,20,48]{2,1,0:T(8,128)}, f32[3,20,48]{2,1,0:T(8,128)}, u32[]{:S(2)}, u32[]{:S(2)}) collective-permute-start(f32[3,20,48]{2,1,0:T(8,128)} %rest_0_.1), channel_id=1, source_target_pairs={{2,0},{0,2},{3,1},{1,3},{6,4},{4,6},{7,5},{5,7},{10,8},{8,10},{11,... | collective-permute-start | bytes 34568 | tf_op jit(solution)/shard_map/ppermute | solution.py:200
  9.7 0.8 %copy.51.cols.refs_8_.refs_6_ = s32[20,8]{1,0:T(8,128)S(1)} copy(s32[20,8]{0,1:T(8,128)} %param.11) | data formatting | bytes 1280 | tf_op args[3]
  10.5 1.1 %collective-permute-done.1.rest_1_ = f32[3,20,48]{2,1,0:T(8,128)} collective-permute-done((f32[3,20,48]{2,1,0:T(8,128)}, f32[3,20,48]{2,1,0:T(8,128)}, u32[]{:S(2)}, u32[]{:S(2)}) %collective-permute-start.1) | collective-permute-done | bytes 11552 | tf_op jit(solution)/shard_map/ppermute | solution.py:200
  11.6 0.0 collective-permute-done.halo
  11.7 1.4 %copy-done.1 = bf16[20,96,384]{2,1,0:T(8,128)(2,1)S(1)} copy-done((bf16[20,96,384]{2,1,0:T(8,128)(2,1)S(1)}, bf16[20,96,384]{2,1,0:T(8,128)(2,1)}, u32[]{:S(2)}) %copy-start.1) | copy-done | bytes 1474584
  13.0 1.4 %copy-done.2 = bf16[20,96,384]{2,1,0:T(8,128)(2,1)S(1)} copy-done((bf16[20,96,384]{2,1,0:T(8,128)(2,1)S(1)}, bf16[20,96,384]{2,1,0:T(8,128)(2,1)}, u32[]{:S(2)}) %copy-start.2) | copy-done | bytes 1474584
  14.4 0.7 %copy-done.4 = f32[20,96]{1,0:T(8,128)S(1)} copy-done((f32[20,96]{1,0:T(8,128)S(1)}, f32[20,96]{1,0:T(8,128)}, u32[]{:S(2)}) %copy-start.4) | copy-done | bytes 7704
  15.1 0.7 %copy-done.5 = f32[20,96]{1,0:T(8,128)S(1)} copy-done((f32[20,96]{1,0:T(8,128)S(1)}, f32[20,96]{1,0:T(8,128)}, u32[]{:S(2)}) %copy-start.5) | copy-done | bytes 7704
  15.8 5.1 %main_first.1 = (bf16[20,96,768]{2,1,0:T(8,128)(2,1)S(1)}, bf16[4,96,384]{2,1,0:T(8,128)(2,1)S(1)}, bf16[28,96,384]{2,1,0:T(8,128)(2,1)S(1)}, bf16[28,96,384]{2,...) custom-call(bf16[20,96,768]{2,1,0:T(8,128)(2,1)S(1)} %copy.101.block, ...), custom_call_target="tpu_custom_call", output_to_operand_aliasing={{0}: (0, {}), {1}: (3, {})} | custom-call | flops 905969664 | bytes 6000000 | tf_op jit(solution)/shard_map/main_first/pallas_call | solution.py:222
  20.9 3.7 %collective-permute-start.3 = (bf16[4,96,384]{2,1,0:T(8,128)(2,1)S(1)}, bf16[4,96,384]{2,1,0:T(8,128)(2,1)S(1)}, u32[]{:S(2)}, u32[]{:S(2)}) collective-permute-start(bf16[4,96,384]{2,1,0:T(8,128)(2,1)S(1)} %get-tuple-element.61), channel_id=1, source_target_pairs={{0,1},{1,0},{4,5},{5,4},{8,9},{9,8},{12,13},{13,12},{2,3},{3,2},{6... | collective-permute-start | bytes 884744 | tf_op jit(solution)/shard_map/ppermute | solution.py:254
  24.7 0.0 collective-permute-done.2.refs_7_
  24.7 1.5 %edge2.1 = (bf16[20,96,768]{2,1,0:T(8,128)(2,1)S(1)}, bf16[28,96,384]{2,1,0:T(8,128)(2,1)S(1)}, bf16[28,96,384]{2,1,0:T(8,128)(2,1)S(1)}, f32[20,96,384]{2,1,0:T...) custom-call(bf16[20,96,768]{2,1,0:T(8,128)(2,1)S(1)} %get-tuple-elem, ...), custom_call_target="tpu_custom_call", output_to_operand_aliasing={{0}: (0, {}), {1}: (1, {}), {2}: (2, {}), {3}: (3, {}), {4}... | custom-call | flops 226492416 | bytes 1000000 | tf_op jit(solution)/shard_map/edge2/pallas_call | solution.py:240
  26.2 0.1 collective-permute-start.4
  26.2 0.0 collective-permute-done.3.refs_7_
  26.2 3.7 %main1.1 = (bf16[20,96,768]{2,1,0:T(8,128)(2,1)S(1)}, bf16[28,96,384]{2,1,0:T(8,128)(2,1)S(1)}, bf16[28,96,384]{2,1,0:T(8,128)(2,1)S(1)}, f32[20,96,384]{2,1,0:T...) custom-call(bf16[20,96,768]{2,1,0:T(8,128)(2,1)S(1)} %get-tuple-elem, ...), custom_call_target="tpu_custom_call", output_to_operand_aliasing={{0}: (0, {}), {1}: (1, {}), {2}: (2, {}), {3}: (3, {}), {4}... | custom-call | flops 905969664 | bytes 6000000 | tf_op jit(solution)/shard_map/main1/pallas_call | solution.py:240
  29.9 0.6 %collective-permute-start.5 = (bf16[4,96,384]{2,1,0:T(8,128)(2,1)S(1)}, bf16[4,96,384]{2,1,0:T(8,128)(2,1)S(1)}, u32[]{:S(2)}, u32[]{:S(2)}) collective-permute-start(bf16[4,96,384]{2,1,0:T(8,128)(2,1)S(1)} %get-tuple-element.75), channel_id=1, source_target_pairs={{0,1},{1,0},{4,5},{5,4},{8,9},{9,8},{12,13},{13,12},{2,3},{3,2},{6... | collective-permute-start | bytes 884744 | tf_op jit(solution)/shard_map/ppermute | solution.py:254
  30.5 5.0 %collective-permute-done.4.refs_7_ = bf16[4,96,384]{2,1,0:T(8,128)(2,1)S(1)} collective-permute-done((bf16[4,96,384]{2,1,0:T(8,128)(2,1)S(1)}, bf16[4,96,384]{2,1,0:T(8,128)(2,1)S(1)}, u32[]{:S(2)}, u32[]{:S(2)}) %collective-permute-start.4) | collective-permute-done | bytes 294944 | tf_op jit(solution)/shard_map/ppermute | solution.py:256
  35.5 1.5 %edge1.1 = (bf16[20,96,768]{2,1,0:T(8,128)(2,1)S(1)}, bf16[28,96,384]{2,1,0:T(8,128)(2,1)S(1)}, bf16[28,96,384]{2,1,0:T(8,128)(2,1)S(1)}, f32[20,96,384]{2,1,0:T...) custom-call(bf16[20,96,768]{2,1,0:T(8,128)(2,1)S(1)} %get-tuple-elem, ...), custom_call_target="tpu_custom_call", output_to_operand_aliasing={{0}: (0, {}), {1}: (1, {}), {2}: (2, {}), {3}: (3, {}), {4}... | custom-call | flops 226492416 | bytes 1000000 | tf_op jit(solution)/shard_map/edge1/pallas_call | solution.py:240
  37.0 0.1 collective-permute-start.6
  37.1 0.0 collective-permute-done.5.refs_5_
  37.1 3.7 %main_last.1 = (bf16[20,96,768]{2,1,0:T(8,128)(2,1)S(1)}, bf16[28,96,384]{2,1,0:T(8,128)(2,1)S(1)}, f32[20,96,384]{2,1,0:T(8,128)S(1)}, f32[20,96,384]{2,1,0:T(8...) custom-call(bf16[20,96,768]{2,1,0:T(8,128)(2,1)S(1)} %get-tuple-elem, ...), custom_call_target="tpu_custom_call", output_to_operand_aliasing={{0}: (0, {}), {1}: (1, {}), {2}: (2, {}), {3}: (3, {}), {4}... | custom-call | flops 905969664 | bytes 6000000 | tf_op jit(solution)/shard_map/main_last/pallas_call | solution.py:266
  40.8 5.6 %collective-permute-done.6.refs_5_ = bf16[4,96,384]{2,1,0:T(8,128)(2,1)S(1)} collective-permute-done((bf16[4,96,384]{2,1,0:T(8,128)(2,1)S(1)}, bf16[4,96,384]{2,1,0:T(8,128)(2,1)S(1)}, u32[]{:S(2)}, u32[]{:S(2)}) %collective-permute-start.6) | collective-permute-done | bytes 294944 | tf_op jit(solution)/shard_map/ppermute | solution.py:256
  46.4 2.1 %edge_last.1 = (bf16[20,96,768]{2,1,0:T(8,128)(2,1)S(1)}, bf16[28,96,384]{2,1,0:T(8,128)(2,1)S(1)}, f32[20,96,384]{2,1,0:T(8,128)S(1)}, f32[20,96,384]{2,1,0:T(8...) custom-call(bf16[20,96,768]{2,1,0:T(8,128)(2,1)S(1)} %get-tuple-elem, ...), custom_call_target="tpu_custom_call", output_to_operand_aliasing={{0}: (0, {}), {1}: (1, {}), {2}: (2, {}), {3}: (3, {}), {4}... | custom-call | flops 226492416 | bytes 1000000 | tf_op jit(solution)/shard_map/edge_last/pallas_call | solution.py:277
  (8 shorter events, 0.0 us)
Async XLA Ops:
  0.6 2.3 %copy-start.7 = (bf16[20,96,768]{2,1,0:T(8,128)(2,1)S(1)}, bf16[20,96,768]{2,1,0:T(8,128)(2,1)}, u32[]{:S(2)}) copy-start(bf16[20,96,768]{2,1,0:T(8,128)(2,1)} %param.10) | copy-start | bytes 8847364
  2.9 0.7 %copy-start.3 = (f32[20,96]{1,0:T(8,128)S(1)}, f32[20,96]{1,0:T(8,128)}, u32[]{:S(2)}) copy-start(f32[20,96]{1,0:T(8,128)} %inv_mass.3) | copy-start | bytes 23044
  2.9 8.7 %copy-start.6 = (s32[3,20]{1,0:T(4,128)S(1)}, s32[3,20]{1,0:T(4,128)}, u32[]{:S(2)}) copy-start(s32[3,20]{1,0:T(4,128)} %contact.1) | copy-start | bytes 724
  4.7 1.1 %copy-start = (bf16[20,96,384]{2,1,0:T(8,128)(2,1)}, bf16[20,96,384]{2,1,0:T(8,128)(2,1)S(1)}, u32[]{:S(2)}) copy-start(bf16[20,96,384]{2,1,0:T(8,128)(2,1)S(1)} %get-tuple-element.44.vel0) | copy-start | bytes 4423684
  5.8 5.8 %collective-permute-start = (bf16[4,96,384]{2,1,0:T(8,128)(2,1)}, bf16[4,96,384]{2,1,0:T(8,128)(2,1)S(1)}, u32[]{:S(2)}, u32[]{:S(2)}) collective-permute-start(bf16[4,96,384]{2,1,0:T(8,128)(2,1)} %get-tuple-element.45), channel_id=1, source_target_pairs={{0,1},{1,0},{4,5},{5,4},{8,9},{9,8},{12,13},{13,12},{2,3},{3,2},{6... | collective-permute-start | bytes 884744 | tf_op jit(solution)/shard_map/ppermute | solution.py:215
  5.9 18.8 %collective-permute-start.2 = (bf16[4,96,384]{2,1,0:T(8,128)(2,1)}, bf16[4,96,384]{2,1,0:T(8,128)(2,1)S(1)}, u32[]{:S(2)}, u32[]{:S(2)}) collective-permute-start(bf16[4,96,384]{2,1,0:T(8,128)(2,1)} %get-tuple-element.53), channel_id=1, source_target_pairs={{1,4},{5,8},{9,12},{13,0},{4,1},{8,5},{12,9},{0,13},{3,6},{7,10},{... | collective-permute-start | bytes 884744 | tf_op jit(solution)/shard_map/ppermute | solution.py:214
  8.5 3.1 %collective-permute-start.1 = (f32[3,20,48]{2,1,0:T(8,128)}, f32[3,20,48]{2,1,0:T(8,128)}, u32[]{:S(2)}, u32[]{:S(2)}) collective-permute-start(f32[3,20,48]{2,1,0:T(8,128)} %rest_0_.1), channel_id=1, source_target_pairs={{2,0},{0,2},{3,1},{1,3},{6,4},{4,6},{7,5},{5,7},{10,8},{8,10},{11,... | collective-permute-start | bytes 34568 | tf_op jit(solution)/shard_map/ppermute | solution.py:200
  11.7 1.4 %copy-start.1 = (bf16[20,96,384]{2,1,0:T(8,128)(2,1)S(1)}, bf16[20,96,384]{2,1,0:T(8,128)(2,1)}, u32[]{:S(2)}) copy-start(bf16[20,96,384]{2,1,0:T(8,128)(2,1)} %copy-done) | copy-start | bytes 4423684
  13.0 1.4 %copy-start.2 = (bf16[20,96,384]{2,1,0:T(8,128)(2,1)S(1)}, bf16[20,96,384]{2,1,0:T(8,128)(2,1)}, u32[]{:S(2)}) copy-start(bf16[20,96,384]{2,1,0:T(8,128)(2,1)} %disp0.1) | copy-start | bytes 4423684
  14.4 0.7 %copy-start.4 = (f32[20,96]{1,0:T(8,128)S(1)}, f32[20,96]{1,0:T(8,128)}, u32[]{:S(2)}) copy-start(f32[20,96]{1,0:T(8,128)} %inv_mass.3) | copy-start | bytes 23044
  15.1 0.7 %copy-start.5 = (f32[20,96]{1,0:T(8,128)S(1)}, f32[20,96]{1,0:T(8,128)}, u32[]{:S(2)}) copy-start(f32[20,96]{1,0:T(8,128)} %stiff.1) | copy-start | bytes 23044
  20.9 5.3 %collective-permute-start.3 = (bf16[4,96,384]{2,1,0:T(8,128)(2,1)S(1)}, bf16[4,96,384]{2,1,0:T(8,128)(2,1)S(1)}, u32[]{:S(2)}, u32[]{:S(2)}) collective-permute-start(bf16[4,96,384]{2,1,0:T(8,128)(2,1)S(1)} %get-tuple-element.61), channel_id=1, source_target_pairs={{0,1},{1,0},{4,5},{5,4},{8,9},{9,8},{12,13},{13,12},{2,3},{3,2},{6... | collective-permute-start | bytes 884744 | tf_op jit(solution)/shard_map/ppermute | solution.py:254
  26.2 9.4 %collective-permute-start.4 = (bf16[4,96,384]{2,1,0:T(8,128)(2,1)S(1)}, bf16[4,96,384]{2,1,0:T(8,128)(2,1)S(1)}, u32[]{:S(2)}, u32[]{:S(2)}) collective-permute-start(bf16[4,96,384]{2,1,0:T(8,128)(2,1)S(1)} %get-tuple-element.69), channel_id=1, source_target_pairs={{1,4},{5,8},{9,12},{13,0},{4,1},{8,5},{12,9},{0,13},{3,6},{7,10},{... | collective-permute-start | bytes 884744 | tf_op jit(solution)/shard_map/ppermute | solution.py:256
  29.9 7.2 %collective-permute-start.5 = (bf16[4,96,384]{2,1,0:T(8,128)(2,1)S(1)}, bf16[4,96,384]{2,1,0:T(8,128)(2,1)S(1)}, u32[]{:S(2)}, u32[]{:S(2)}) collective-permute-start(bf16[4,96,384]{2,1,0:T(8,128)(2,1)S(1)} %get-tuple-element.75), channel_id=1, source_target_pairs={{0,1},{1,0},{4,5},{5,4},{8,9},{9,8},{12,13},{13,12},{2,3},{3,2},{6... | collective-permute-start | bytes 884744 | tf_op jit(solution)/shard_map/ppermute | solution.py:254
  37.0 9.4 %collective-permute-start.6 = (bf16[4,96,384]{2,1,0:T(8,128)(2,1)S(1)}, bf16[4,96,384]{2,1,0:T(8,128)(2,1)S(1)}, u32[]{:S(2)}, u32[]{:S(2)}) collective-permute-start(bf16[4,96,384]{2,1,0:T(8,128)(2,1)S(1)} %get-tuple-element.81), channel_id=1, source_target_pairs={{1,4},{5,8},{9,12},{13,0},{4,1},{8,5},{12,9},{0,13},{3,6},{7,10},{... | collective-permute-start | bytes 884744 | tf_op jit(solution)/shard_map/ppermute | solution.py:256

commit v2 on v0

v2 whole, which is shorter than its diff:
```python
import functools
import jax
import jax.numpy as jnp
from jax import lax
from jax.experimental import pallas as pl
from jax.experimental.pallas import tpu as pltpu
from jax.sharding import PartitionSpec as P

HB = 4
WINDOW = 3
RING = ("space", "rep")
VMEM_LIMIT = 24 * 1024 * 1024


def ring_pairs(ring):
    inner = [(i, i ^ 1) for i in range(ring)]
    outer = [(i, (i + 1) % ring) for i in range(1, ring, 2)]
    outer = outer + [(b, a) for a, b in outer]
    return inner, outer


def product(blocks, packed, place, r):
    slots = blocks.shape[2] // blocks.shape[1]
    picked = jnp.concatenate([packed[place[k, r]] for k in range(slots)], axis=0)
    return jnp.dot(blocks[r], picked, preferred_element_type=jnp.float32)


def tiled(column, lanes):
    return jnp.concatenate([column] * (lanes // 128), axis=1)


def spread(matrix, r, lanes):
    return jnp.broadcast_to(matrix[:, r : r + 1], (matrix.shape[0], lanes))


def each(count, one):
    def run(i, carry):
        one(i)
        return carry

    lax.fori_loop(0, count, run, 0, unroll=True)


def begin(copies):
    for c in copies:
        c.start()
    return copies


def end(copies):
    for c in copies:
        c.wait()


def head(vel0, inv_mass, out_b, out_a, low, high, mass, sem):
    rows, _, lanes = vel0.shape
    end(
        begin(
            [
                pltpu.make_async_copy(inv_mass, mass, sem.at[0]),
                pltpu.make_async_copy(vel0.at[pl.ds(0, HB)], low, sem.at[1]),
                pltpu.make_async_copy(vel0.at[pl.ds(rows - HB, HB)], high, sem.at[2]),
            ]
        )
    )
    rep = lax.axis_index("rep")
    turned = mass[...].T
    for j in range(HB):
        p = spread(turned, j, lanes) * (0.5 * low[j].astype(jnp.float32))
        q = spread(turned, rows - HB + j, lanes) * (0.5 * high[j].astype(jnp.float32))
        out_b[j] = jnp.where(rep == 0, p, q).astype(jnp.bfloat16)
        out_a[j] = jnp.where(rep == 0, q, p).astype(jnp.bfloat16)


def first_products(
    total, blocks_in, vel0_in, disp0_in, inv_mass, halo, cols,
    blocks, now, disp, vel, mass_b, place, vel0, disp0, mass, sem,
):
    rows, _, lanes = vel0.shape
    slots = cols.shape[0]
    begin(
        [
            pltpu.make_async_copy(inv_mass, mass, sem.at[0]),
            pltpu.make_async_copy(vel0_in, vel0, sem.at[1]),
            pltpu.make_async_copy(disp0_in, disp0, sem.at[2]),
            pltpu.make_async_copy(blocks_in, blocks, sem.at[3]),
        ]
    )
    rep = lax.axis_index("rep")
    first = (lax.axis_index("space") * 2 + rep) * rows
    for r in range(rows):
        for k in range(slots):
            off = cols[k, r] - (first + r)
            off = jnp.where(off > HB, off - total, off)
            off = jnp.where(off < -HB, off + total, off)
            place[k, r] = r + HB + off
    pltpu.make_async_copy(inv_mass, mass, sem.at[0]).wait()
    turned = mass[...].T
    for r in range(rows):
        mass_b[r] = spread(turned, r, 128)
    pltpu.make_async_copy(vel0_in, vel0, sem.at[1]).wait()
    for r in range(rows):
        v = vel0[r].astype(jnp.float32)
        vel[r] = v
        now[r + HB] = (tiled(mass_b[r], lanes) * (0.5 * v)).astype(jnp.bfloat16)
    at_a = (rows + HB) * (1 - rep)
    for j in range(HB):
        now[at_a + j] = halo[j]
    pltpu.make_async_copy(disp0_in, disp0, sem.at[2]).wait()
    b_start = (rows - HB) * rep
    for j in range(HB):
        disp[b_start + j] = disp0[b_start + j].astype(jnp.float32)
    pltpu.make_async_copy(blocks_in, blocks, sem.at[3]).wait()
    start = HB * (1 - rep)

    def one(i):
        r = start + i
        disp[r] = disp0[r].astype(jnp.float32) - product(blocks, now, place, r)

    each(rows - HB, one)


def first_rows(start, count, now, later, disp, vel, mass_b, coeff):
    lanes = disp.shape[2]

    def one(i):
        r = start + i
        d = disp[r] - tiled(coeff[WINDOW - 1, r], lanes) * now[r + HB].astype(jnp.float32)
        v = vel[r] + d
        disp[r] = d
        vel[r] = v
        later[r + HB] = (tiled(mass_b[r], lanes) * v).astype(jnp.bfloat16)

    each(count, one)


def coefficients(pieces, *refs):
    stiff_in, contact_in, mine = refs[4:7]
    now, disp, vel, mass_b, *others = refs[6 + pieces : 9 + 2 * pieces]
    later, coeff, out_a, stiff, contact, shard, turned, sem = refs[9 + 2 * pieces :]
    rows, width = stiff.shape
    part = width // pieces
    end(
        begin(
            [
                pltpu.make_async_copy(stiff_in, stiff, sem.at[0]),
                pltpu.make_async_copy(contact_in, contact, sem.at[1]),
                pltpu.make_async_copy(mine, shard, sem.at[2]),
            ]
        )
    )
    me = lax.axis_index("ckpt")
    bent = 3.0 * stiff[...].T
    for s in range(WINDOW):
        for j, piece in enumerate((shard,) + tuple(others)):
            source = lax.rem(me + j, pieces)
            turned[s, pl.ds(pl.multiple_of(source * part, 8), part), :] = piece[s].T
        state = turned[s]
        full = bent * state * state
        for r in range(rows):
            coeff[s, r] = spread(full, r, 128) * contact[s, r].astype(jnp.float32)
    start = (rows - HB) * (1 - lax.axis_index("rep"))
    first_rows(start, HB, now, later, disp, vel, mass_b, coeff)
    for j in range(HB):
        out_a[j] = later[start + HB + j]


def first_update(*refs):
    now, later, disp, vel, mass_b, coeff = refs[6:]
    first_rows(HB, disp.shape[0] - 2 * HB, now, later, disp, vel, mass_b, coeff)


def advance(step, r, blocks, now, place, coeff, disp, vel):
    lanes = now.shape[2]
    image = product(blocks, now, place, r)
    image = image + tiled(coeff[step, r], lanes) * now[r + HB].astype(jnp.float32)
    d = disp[r] - image
    v = vel[r] + d
    disp[r] = d
    vel[r] = v
    return v


def extent(rows, edge, rep):
    if edge:
        return rep, (rows - HB) * rep, HB
    return 1 - rep, HB * (1 - rep), rows - HB


def middle(step, edge, *refs):
    place, blocks, now, disp, vel, mass_b, coeff, halo, later, out = refs[-10:]
    rows, _, lanes = disp.shape
    side, start, count = extent(rows, edge, lax.axis_index("rep"))
    for j in range(HB):
        now[(rows + HB) * side + j] = halo[j]

    def one(i):
        r = start + i
        v = advance(step, r, blocks, now, place, coeff, disp, vel)
        p = (tiled(mass_b[r], lanes) * v).astype(jnp.bfloat16)
        later[r + HB] = p
        if edge:
            out[i] = p

    each(count, one)
    if not edge:
        for j in range(HB):
            out[j] = later[(rows - HB) * side + HB + j]


def final(step, edge, *refs):
    place = refs[8 if edge else 6]
    blocks, now, disp, vel, coeff, halo, disp_out, vel_out, sem = refs[(9 if edge else 7) :]
    rows = disp.shape[0]
    side, start, count = extent(rows, edge, lax.axis_index("rep"))
    group = 1 if edge else HB
    for j in range(HB):
        now[(rows + HB) * side + j] = halo[j]

    def copies(g):
        at = pl.ds(start + g * group, group)
        return [
            pltpu.make_async_copy(disp.at[at], disp_out.at[at], sem.at[0, g]),
            pltpu.make_async_copy(vel.at[at], vel_out.at[at], sem.at[1, g]),
        ]

    for g in range(count // group):
        each(group, lambda i: advance(step, start + g * group + i, blocks, now, place, coeff, disp, vel))
        begin(copies(g))
    for g in range(count // group):
        end(copies(g))


def body(adj_disp, adj_vel, tangent_blocks, block_cols, inv_mass, joint_stiff, contact, states):
    rows, width, lanes = adj_disp.shape
    ring = lax.axis_size(RING)
    total = rows * ring
    inner, outer = ring_pairs(ring)
    pieces = lax.axis_size("ckpt")
    f32, bf16 = jnp.float32, jnp.bfloat16
    vm = pl.BlockSpec(memory_space=pltpu.VMEM)
    sm = pl.BlockSpec(memory_space=pltpu.SMEM)
    hbm = pl.BlockSpec(memory_space=pltpu.HBM)
    params = pltpu.CompilerParams(vmem_limit_bytes=VMEM_LIMIT)
    like = lambda a: pltpu.VMEM(a.shape, a.dtype)
    edge_t = pltpu.VMEM((HB, width, lanes), bf16)
    ext = pltpu.VMEM((rows + 2 * HB, width, lanes), bf16)
    full = pltpu.VMEM((rows, width, lanes), f32)
    dma = pltpu.SemaphoreType.DMA
    flops = 2 * (rows - HB) * width * tangent_blocks.shape[2] * lanes
    big = pl.CostEstimate(flops=flops // 64, bytes_accessed=100_000, transcendentals=0)
    small = pl.CostEstimate(flops=flops // 256, bytes_accessed=25_000, transcendentals=0)
    adj_disp, adj_vel, tangent_blocks, cols, inv_mass, joint_stiff, contact, mine = (
        pltpu.with_memory_space_constraint(a, pltpu.HBM)
        for a in (
            adj_disp, adj_vel, tangent_blocks, block_cols.T, inv_mass, joint_stiff, contact, states
        )
    )

    out_b, out_a = pl.pallas_call(
        head,
        name="head",
        out_shape=(edge_t, edge_t),
        in_specs=[hbm] * 2,
        out_specs=(vm,) * 2,
        scratch_shapes=[edge_t, edge_t, pltpu.VMEM((rows, width), f32), dma((3,))],
        compiler_params=params,
    )(adj_vel, inv_mass)

    states_late, out_a = lax.optimization_barrier((states, out_a))
    halo_a = lax.ppermute(out_a, RING, inner)
    halo_b = lax.ppermute(out_b, RING, outer)
    shards = [mine] + [
        lax.ppermute(states_late, "ckpt", [((i + j) % pieces, i) for i in range(pieces)])
        for j in range(1, pieces)
    ]

    blocks, now, disp, vel, mass_b, place = pl.pallas_call(
        functools.partial(first_products, total),
        name="first_products",
        out_shape=(
            like(tangent_blocks), ext, full, full,
            pltpu.VMEM((rows, width, 128), f32),
            jax.ShapeDtypeStruct(cols.shape, jnp.int32),
        ),
        in_specs=[hbm] * 4 + [vm, sm],
        out_specs=(vm,) * 5 + (sm,),
        scratch_shapes=[like(adj_vel), like(adj_disp), pltpu.VMEM((rows, width), f32), dma((4,))],
        compiler_params=params,
        cost_estimate=big,
    )(tangent_blocks, adj_vel, adj_disp, inv_mass, halo_a, cols)

    now, disp, vel, mass_b, *_, later, coeff, out_a = pl.pallas_call(
        functools.partial(coefficients, pieces),
        name="coefficients",
        out_shape=(like(now), like(disp), like(vel), like(mass_b))
        + tuple(like(a) for a in shards[1:])
        + (ext, pltpu.VMEM((WINDOW, rows, width, 128), f32), edge_t),
        in_specs=[vm] * 4 + [hbm] * 3 + [vm] * (pieces - 1),
        out_specs=(vm,) * (pieces + 6),
        input_output_aliases={i: i for i in range(4)} | {6 + j: 3 + j for j in range(1, pieces)},
        scratch_shapes=[
            pltpu.VMEM((rows, width), f32),
            pltpu.SMEM(contact.shape, jnp.int32),
            pltpu.VMEM(states.shape, f32),
            pltpu.VMEM((WINDOW, width, rows), f32),
            dma((3,)),
        ],
        compiler_params=params,
        cost_estimate=small,
    )(now, disp, vel, mass_b, joint_stiff, contact, *shards)

    def run_middle(step, edge, held, halo, later):
        given = list(held) + [halo, later]
        *out, edge_rows = pl.pallas_call(
            functools.partial(middle, step, edge),
            name=("edge" if edge else "main") + str(step),
            out_shape=tuple(like(a) for a in held) + (edge_t, ext, edge_t),
            in_specs=[vm] * len(given) + [sm],
            out_specs=(vm,) * 9,
            input_output_aliases={i: i for i in range(len(given))},
            compiler_params=params,
            cost_estimate=small if edge else big,
        )(*given, place)
        return out[:6], out[7], edge_rows

    held = [blocks, now, disp, vel, mass_b, coeff]
    step = WINDOW - 1
    halo_a = lax.ppermute(out_a, RING, inner)
    held, later, out_b = run_middle(step, True, held, halo_b, later)
    halo_b = lax.ppermute(out_b, RING, outer)
    blocks, now, disp, vel, mass_b, coeff = held
    now, later, disp, vel, mass_b, coeff = pl.pallas_call(
        first_update,
        name="first_update",
        out_shape=(ext, ext, full, full, like(mass_b), like(coeff)),
        in_specs=[vm] * 6,
        out_specs=(vm,) * 6,
        input_output_aliases={i: i for i in range(6)},
        compiler_params=params,
        cost_estimate=small,
    )(now, later, disp, vel, mass_b, coeff)

    step -= 1
    while step > 0:
        held = [blocks, later, disp, vel, mass_b, coeff]
        held, later, out_a = run_middle(step, False, held, halo_a, now)
        halo_a = lax.ppermute(out_a, RING, inner)
        held, later, out_b = run_middle(step, True, held, halo_b, later)
        halo_b = lax.ppermute(out_b, RING, outer)
        blocks, now, disp, vel, mass_b, coeff = held
        step -= 1

    shape = jax.ShapeDtypeStruct((rows, width, lanes), f32)
    held = [blocks, later, disp, vel, coeff]
    *held, _, disp_out, vel_out = pl.pallas_call(
        functools.partial(final, 0, False),
        name="main_last",
        out_shape=tuple(like(a) for a in held) + (edge_t, shape, shape),
        in_specs=[vm] * 6 + [sm],
        out_specs=(vm,) * 6 + (hbm,) * 2,
        scratch_shapes=[dma((2, rows // HB - 1))],
        input_output_aliases={i: i for i in range(6)},
        compiler_params=params,
        cost_estimate=big,
    )(*held, halo_a, place)
    out = pl.pallas_call(
        functools.partial(final, 0, True),
        name="edge_last",
        out_shape=tuple(like(a) for a in held) + (edge_t, shape, shape),
        in_specs=[vm] * 6 + [hbm] * 2 + [sm],
        out_specs=(vm,) * 6 + (hbm,) * 2,
        scratch_shapes=[dma((2, HB))],
        input_output_aliases={i: i for i in range(8)},
        compiler_params=params,
        cost_estimate=small,
    )(*held, halo_b, disp_out, vel_out, place)
    return out[-2], out[-1]


def solution(mesh):
    placed = (
        P(("groups", "space", "rep"), None, "ckpt"),
        P(("groups", "space", "rep"), None, "ckpt"),
        P(("groups", "space", "rep"), None, None),
        P(("groups", "space", "rep"), None),
        P(("groups", "space", "rep"), None),
        P(("groups", "space", "rep"), None),
        P(None, ("groups", "space", "rep")),
        P(None, ("groups", "space", "rep"), "ckpt"),
    )
    return jax.shard_map(
        body,
        mesh=mesh,
        in_specs=placed,
        out_specs=(
            P(("groups", "space", "rep"), None, "ckpt"),
            P(("groups", "space", "rep"), None, "ckpt"),
        ),
        check_vma=False,
    )
```

time: 130 us -> 40.2 us (0.31)
  the two profiles are of different devices: /device:TPU:0 before, /device:TPU:1 now
where the time goes in v2:
time: 40.2 us; the launch traced here: 39.8 us
  Pallas kernels  20.2 us (50%)
  waiting for transfers between devices  11.3 us (28%)
  starting transfers between devices  7.59 us (19%)
  between operations  0.73 us (2%)
    ppermute x3, waiting for transfers between devices, body(): halo_b = lax.ppermute(out_b, RING, outer)  11.3 us
    pallas_call x1, Pallas kernels, body(): pl.pallas_call(functools.partial(first_products, total), name='first_prod...  5.7 us
    pallas_call x3, Pallas kernels, run_middle(): pl.pallas_call(functools.partial(middle, step, edge), name=('edge' if edg...  5.09 us
    pallas_call x1, Pallas kernels, body(): pl.pallas_call(functools.partial(final, 0, False), name='main_last', out_...  3.59 us
    ppermute x3, starting transfers between devices, body(): halo_a = lax.ppermute(out_a, RING, inner)  3.53 us
    ppermute x3, starting transfers between devices, body(): halo_b = lax.ppermute(out_b, RING, outer)  2.85 us
    pallas_call x1, Pallas kernels, body(): pl.pallas_call(functools.partial(coefficients, pieces), name='coefficient...  2.06 us
    pallas_call x1, Pallas kernels, body(): pl.pallas_call(functools.partial(final, 0, True), name='edge_last', out_s...  2 us
  transfers between devices with their start and end apart: 7, of which 2 were waited for; matrix products, arithmetic and copies ran while one was open for 0% of the time, Pallas kernels for 42%

profile of v2, /device:TPU:1, one launch (start us, length us, event | category | flops | bytes accessed | tf_op | source)
XLA Modules:
  0.0 39.8 jit_solution(14384514401657525506)
XLA Ops:
  0.6 1.4 %head.1 = (bf16[4,96,384]{2,1,0:T(8,128)(2,1)S(1)}, bf16[4,96,384]{2,1,0:T(8,128)(2,1)S(1)}) custom-call(bf16[20,96,384]{2,1,0:T(8,128)(2,1)} %vel0_in.1, f32[20,96]{1,0:T(8,128)} %inv_mass.3), custom_call_target="tpu_custom_call" | custom-call | tf_op jit(solution)/shard_map/head/pallas_call | solution.py:260
  2.0 0.1 collective-permute-start
  2.2 2.7 %collective-permute-start.2 = (bf16[4,96,384]{2,1,0:T(8,128)(2,1)S(1)}, bf16[4,96,384]{2,1,0:T(8,128)(2,1)S(1)}, u32[]{:S(2)}, u32[]{:S(2)}) collective-permute-start(bf16[4,96,384]{2,1,0:T(8,128)(2,1)S(1)} %get-tuple-element.69), channel_id=1, source_target_pairs={{1,4},{5,8},{9,12},{13,0},{4,1},{8,5},{12,9},{0,13},{3,6},{7,10},{... | collective-permute-start | bytes 884744 | tf_op jit(solution)/shard_map/ppermute | solution.py:272
  4.9 1.2 %collective-permute-start.1 = (f32[3,20,48]{2,1,0:T(8,128)}, f32[3,20,48]{2,1,0:T(8,128)S(1)}, u32[]{:S(2)}, u32[]{:S(2)}) collective-permute-start(f32[3,20,48]{2,1,0:T(8,128)} %refs_6_.1), channel_id=1, source_target_pairs={{2,0},{0,2},{3,1},{1,3},{6,4},{4,6},{7,5},{5,7},{10,8},{8,10},{11,... | collective-permute-start | bytes 34568 | tf_op jit(solution)/shard_map/ppermute | solution.py:274
  6.1 0.0 collective-permute-done.halo
  6.1 5.7 %first_products.1 = (bf16[20,96,768]{2,1,0:T(8,128)(2,1)S(1)}, bf16[28,96,384]{2,1,0:T(8,128)(2,1)S(1)}, f32[20,96,384]{2,1,0:T(8,128)S(1)}, f32[20,96,384]{2,1,...) custom-call(bf16[20,96,768]{2,1,0:T(8,128)(2,1)} %blocks_in.1, bf16[20,96,384]{2,1,0:T(8,128)(2,1)} %vel0_in.1, ...), custom_call_target="tpu_custom_call" | custom-call | flops 14155776 | bytes 100000 | tf_op jit(solution)/shard_map/first_products/pallas_call | solution.py:278
  11.8 0.0 collective-permute-done.1.refs_7_
  11.8 2.1 %coefficients.1 = (bf16[28,96,384]{2,1,0:T(8,128)(2,1)S(1)}, f32[20,96,384]{2,1,0:T(8,128)S(1)}, f32[20,96,384]{2,1,0:T(8,128)S(1)}, f32[20,96,128]{2,1,0:T(8,12...) custom-call(bf16[28,96,384]{2,1,0:T(8,128)(2,1)S(1)} %get-tuple-elem, ...), custom_call_target="tpu_custom_call", output_to_operand_aliasing={{0}: (0, {}), {1}: (1, {}), {2}: (2, {}), {3}: (3, {}), {4}... | custom-call | flops 3538944 | bytes 25000 | tf_op jit(solution)/shard_map/coefficients/pallas_call | solution.py:293
  13.9 2.8 %collective-permute-start.3 = (bf16[4,96,384]{2,1,0:T(8,128)(2,1)S(1)}, bf16[4,96,384]{2,1,0:T(8,128)(2,1)S(1)}, u32[]{:S(2)}, u32[]{:S(2)}) collective-permute-start(bf16[4,96,384]{2,1,0:T(8,128)(2,1)S(1)} %get-tuple-element.84), channel_id=1, source_target_pairs={{0,1},{1,0},{4,5},{5,4},{8,9},{9,8},{12,13},{13,12},{2,3},{3,2},{6... | collective-permute-start | bytes 884744 | tf_op jit(solution)/shard_map/ppermute | solution.py:329
  16.7 0.0 collective-permute-done.2.refs_6_
  16.7 1.2 %edge2.1 = (bf16[20,96,768]{2,1,0:T(8,128)(2,1)S(1)}, bf16[28,96,384]{2,1,0:T(8,128)(2,1)S(1)}, f32[20,96,384]{2,1,0:T(8,128)S(1)}, f32[20,96,384]{2,1,0:T(8,128...) custom-call(bf16[20,96,768]{2,1,0:T(8,128)(2,1)S(1)} %get-tuple-elem, ...), custom_call_target="tpu_custom_call", output_to_operand_aliasing={{0}: (0, {}), {1}: (1, {}), {2}: (2, {}), {3}: (3, {}), {4}... | custom-call | flops 3538944 | bytes 25000 | tf_op jit(solution)/shard_map/edge2/pallas_call | solution.py:315
  17.9 0.1 collective-permute-start.4
  18.0 0.4 first_update.1
  18.4 0.0 collective-permute-done.3.refs_6_
  18.4 2.7 %main1.1 = (bf16[20,96,768]{2,1,0:T(8,128)(2,1)S(1)}, bf16[28,96,384]{2,1,0:T(8,128)(2,1)S(1)}, f32[20,96,384]{2,1,0:T(8,128)S(1)}, f32[20,96,384]{2,1,0:T(8,128...) custom-call(bf16[20,96,768]{2,1,0:T(8,128)(2,1)S(1)} %get-tuple-elem, ...), custom_call_target="tpu_custom_call", output_to_operand_aliasing={{0}: (0, {}), {1}: (1, {}), {2}: (2, {}), {3}: (3, {}), {4}... | custom-call | flops 14155776 | bytes 100000 | tf_op jit(solution)/shard_map/main1/pallas_call | solution.py:315
  21.0 0.6 %collective-permute-start.5 = (bf16[4,96,384]{2,1,0:T(8,128)(2,1)S(1)}, bf16[4,96,384]{2,1,0:T(8,128)(2,1)S(1)}, u32[]{:S(2)}, u32[]{:S(2)}) collective-permute-start(bf16[4,96,384]{2,1,0:T(8,128)(2,1)S(1)} %get-tuple-element.99), channel_id=1, source_target_pairs={{0,1},{1,0},{4,5},{5,4},{8,9},{9,8},{12,13},{13,12},{2,3},{3,2},{6... | collective-permute-start | bytes 884744 | tf_op jit(solution)/shard_map/ppermute | solution.py:348
  21.7 5.6 %collective-permute-done.4.refs_6_ = bf16[4,96,384]{2,1,0:T(8,128)(2,1)S(1)} collective-permute-done((bf16[4,96,384]{2,1,0:T(8,128)(2,1)S(1)}, bf16[4,96,384]{2,1,0:T(8,128)(2,1)S(1)}, u32[]{:S(2)}, u32[]{:S(2)}) %collective-permute-start.4) | collective-permute-done | bytes 294944 | tf_op jit(solution)/shard_map/ppermute | solution.py:331
  27.3 1.2 %edge1.1 = (bf16[20,96,768]{2,1,0:T(8,128)(2,1)S(1)}, bf16[28,96,384]{2,1,0:T(8,128)(2,1)S(1)}, f32[20,96,384]{2,1,0:T(8,128)S(1)}, f32[20,96,384]{2,1,0:T(8,128...) custom-call(bf16[20,96,768]{2,1,0:T(8,128)(2,1)S(1)} %get-tuple-elem, ...), custom_call_target="tpu_custom_call", output_to_operand_aliasing={{0}: (0, {}), {1}: (1, {}), {2}: (2, {}), {3}: (3, {}), {4}... | custom-call | flops 3538944 | bytes 25000 | tf_op jit(solution)/shard_map/edge1/pallas_call | solution.py:315
  28.5 0.1 collective-permute-start.6
  28.6 0.0 collective-permute-done.5.refs_5_
  28.6 3.6 %main_last.1 = (bf16[20,96,768]{2,1,0:T(8,128)(2,1)S(1)}, bf16[28,96,384]{2,1,0:T(8,128)(2,1)S(1)}, f32[20,96,384]{2,1,0:T(8,128)S(1)}, f32[20,96,384]{2,1,0:T(8...) custom-call(bf16[20,96,768]{2,1,0:T(8,128)(2,1)S(1)} %get-tuple-elem, ...), custom_call_target="tpu_custom_call", output_to_operand_aliasing={{0}: (0, {}), {1}: (1, {}), {2}: (2, {}), {3}: (3, {}), {4}... | custom-call | flops 14155776 | bytes 100000 | tf_op jit(solution)/shard_map/main_last/pallas_call | solution.py:356
  32.2 5.7 %collective-permute-done.6.refs_5_ = bf16[4,96,384]{2,1,0:T(8,128)(2,1)S(1)} collective-permute-done((bf16[4,96,384]{2,1,0:T(8,128)(2,1)S(1)}, bf16[4,96,384]{2,1,0:T(8,128)(2,1)S(1)}, u32[]{:S(2)}, u32[]{:S(2)}) %collective-permute-start.6) | collective-permute-done | bytes 294944 | tf_op jit(solution)/shard_map/ppermute | solution.py:350
  37.8 2.0 %edge_last.1 = (bf16[20,96,768]{2,1,0:T(8,128)(2,1)S(1)}, bf16[28,96,384]{2,1,0:T(8,128)(2,1)S(1)}, f32[20,96,384]{2,1,0:T(8,128)S(1)}, f32[20,96,384]{2,1,0:T(8...) custom-call(bf16[20,96,768]{2,1,0:T(8,128)(2,1)S(1)} %get-tuple-elem, ...), custom_call_target="tpu_custom_call", output_to_operand_aliasing={{0}: (0, {}), {1}: (1, {}), {2}: (2, {}), {3}: (3, {}), {4}... | custom-call | flops 3538944 | bytes 25000 | tf_op jit(solution)/shard_map/edge_last/pallas_call | solution.py:367
Async XLA Ops:
  2.0 4.0 %collective-permute-start = (bf16[4,96,384]{2,1,0:T(8,128)(2,1)S(1)}, bf16[4,96,384]{2,1,0:T(8,128)(2,1)S(1)}, u32[]{:S(2)}, u32[]{:S(2)}) collective-permute-start(bf16[4,96,384]{2,1,0:T(8,128)(2,1)S(1)} %get-tuple-element.57), channel_id=1, source_target_pairs={{0,1},{1,0},{4,5},{5,4},{8,9},{9,8},{12,13},{13,12},{2,3},{3,2},{6... | collective-permute-start | bytes 884744 | tf_op jit(solution)/shard_map/ppermute | solution.py:271
  2.2 14.5 %collective-permute-start.2 = (bf16[4,96,384]{2,1,0:T(8,128)(2,1)S(1)}, bf16[4,96,384]{2,1,0:T(8,128)(2,1)S(1)}, u32[]{:S(2)}, u32[]{:S(2)}) collective-permute-start(bf16[4,96,384]{2,1,0:T(8,128)(2,1)S(1)} %get-tuple-element.69), channel_id=1, source_target_pairs={{1,4},{5,8},{9,12},{13,0},{4,1},{8,5},{12,9},{0,13},{3,6},{7,10},{... | collective-permute-start | bytes 884744 | tf_op jit(solution)/shard_map/ppermute | solution.py:272
  4.9 6.9 %collective-permute-start.1 = (f32[3,20,48]{2,1,0:T(8,128)}, f32[3,20,48]{2,1,0:T(8,128)S(1)}, u32[]{:S(2)}, u32[]{:S(2)}) collective-permute-start(f32[3,20,48]{2,1,0:T(8,128)} %refs_6_.1), channel_id=1, source_target_pairs={{2,0},{0,2},{3,1},{1,3},{6,4},{4,6},{7,5},{5,7},{10,8},{8,10},{11,... | collective-permute-start | bytes 34568 | tf_op jit(solution)/shard_map/ppermute | solution.py:274
  13.9 4.5 %collective-permute-start.3 = (bf16[4,96,384]{2,1,0:T(8,128)(2,1)S(1)}, bf16[4,96,384]{2,1,0:T(8,128)(2,1)S(1)}, u32[]{:S(2)}, u32[]{:S(2)}) collective-permute-start(bf16[4,96,384]{2,1,0:T(8,128)(2,1)S(1)} %get-tuple-element.84), channel_id=1, source_target_pairs={{0,1},{1,0},{4,5},{5,4},{8,9},{9,8},{12,13},{13,12},{2,3},{3,2},{6... | collective-permute-start | bytes 884744 | tf_op jit(solution)/shard_map/ppermute | solution.py:329
  17.9 9.4 %collective-permute-start.4 = (bf16[4,96,384]{2,1,0:T(8,128)(2,1)S(1)}, bf16[4,96,384]{2,1,0:T(8,128)(2,1)S(1)}, u32[]{:S(2)}, u32[]{:S(2)}) collective-permute-start(bf16[4,96,384]{2,1,0:T(8,128)(2,1)S(1)} %get-tuple-element.92), channel_id=1, source_target_pairs={{1,4},{5,8},{9,12},{13,0},{4,1},{8,5},{12,9},{0,13},{3,6},{7,10},{... | collective-permute-start | bytes 884744 | tf_op jit(solution)/shard_map/ppermute | solution.py:331
  21.0 7.5 %collective-permute-start.5 = (bf16[4,96,384]{2,1,0:T(8,128)(2,1)S(1)}, bf16[4,96,384]{2,1,0:T(8,128)(2,1)S(1)}, u32[]{:S(2)}, u32[]{:S(2)}) collective-permute-start(bf16[4,96,384]{2,1,0:T(8,128)(2,1)S(1)} %get-tuple-element.99), channel_id=1, source_target_pairs={{0,1},{1,0},{4,5},{5,4},{8,9},{9,8},{12,13},{13,12},{2,3},{3,2},{6... | collective-permute-start | bytes 884744 | tf_op jit(solution)/shard_map/ppermute | solution.py:348
  28.5 9.4 %collective-permute-start.6 = (bf16[4,96,384]{2,1,0:T(8,128)(2,1)S(1)}, bf16[4,96,384]{2,1,0:T(8,128)(2,1)S(1)}, u32[]{:S(2)}, u32[]{:S(2)}) collective-permute-start(bf16[4,96,384]{2,1,0:T(8,128)(2,1)S(1)} %get-tuple-element.105), channel_id=1, source_target_pairs={{1,4},{5,8},{9,12},{13,0},{4,1},{8,5},{12,9},{0,13},{3,6},{7,10},{... | collective-permute-start | bytes 884744 | tf_op jit(solution)/shard_map/ppermute | solution.py:350

commit v3 on v0

v3 whole, which is shorter than its diff:
```python
import functools
import jax
import jax.numpy as jnp
from jax import lax
from jax.experimental import pallas as pl
from jax.experimental.pallas import tpu as pltpu
from jax.sharding import PartitionSpec as P

HB = 4
WINDOW = 3
RING = ("space", "rep")
VMEM_LIMIT = 24 * 1024 * 1024


def ring_pairs(ring):
    inner = [(i, i ^ 1) for i in range(ring)]
    outer = [(i, (i + 1) % ring) for i in range(1, ring, 2)]
    outer = outer + [(b, a) for a, b in outer]
    return inner, outer


def product(blocks, packed, place, r):
    slots = blocks.shape[2] // blocks.shape[1]
    picked = jnp.concatenate([packed[place[k, r]] for k in range(slots)], axis=0)
    return jnp.dot(blocks[r], picked, preferred_element_type=jnp.float32)


def tiled(column, lanes):
    return jnp.concatenate([column] * (lanes // 128), axis=1)


def spread(matrix, r, lanes):
    return jnp.broadcast_to(matrix[:, r : r + 1], (matrix.shape[0], lanes))


def each(count, one):
    def run(i, carry):
        one(i)
        return carry

    lax.fori_loop(0, count, run, 0, unroll=True)


def begin(copies):
    for c in copies:
        c.start()
    return copies


def end(copies):
    for c in copies:
        c.wait()


def head(vel0, inv_mass, out_b, out_a, low, high, mass, sem):
    rows, _, lanes = vel0.shape
    end(
        begin(
            [
                pltpu.make_async_copy(inv_mass, mass, sem.at[0]),
                pltpu.make_async_copy(vel0.at[pl.ds(0, HB)], low, sem.at[1]),
                pltpu.make_async_copy(vel0.at[pl.ds(rows - HB, HB)], high, sem.at[2]),
            ]
        )
    )
    rep = lax.axis_index("rep")
    turned = mass[...].T
    for j in range(HB):
        p = spread(turned, j, lanes) * (0.5 * low[j].astype(jnp.float32))
        q = spread(turned, rows - HB + j, lanes) * (0.5 * high[j].astype(jnp.float32))
        out_b[j] = jnp.where(rep == 0, p, q).astype(jnp.bfloat16)
        out_a[j] = jnp.where(rep == 0, q, p).astype(jnp.bfloat16)


def load_all(
    total, pieces, blocks_in, vel0_in, disp0_in, inv_mass, stiff_in, contact_in, mine, halo, cols,
    blocks, disp0, now, disp, vel, mass_b, bent, turned, place, vel0, mass, stiff, contact, shard, sem,
):
    rows, _, lanes = vel0.shape
    slots = cols.shape[0]
    rep = lax.axis_index("rep")
    a_start = (rows - HB) * (1 - rep)
    b_start = (rows - HB) * rep
    at = pl.ds(a_start, HB)
    small = begin(
        [
            pltpu.make_async_copy(inv_mass, mass, sem.at[0]),
            pltpu.make_async_copy(stiff_in, stiff, sem.at[1]),
            pltpu.make_async_copy(contact_in, contact, sem.at[2]),
            pltpu.make_async_copy(mine, shard, sem.at[3]),
        ]
    )
    get_vel = begin([pltpu.make_async_copy(vel0_in, vel0, sem.at[4])])
    get_rest = begin(
        [
            pltpu.make_async_copy(blocks_in, blocks, sem.at[5]),
            pltpu.make_async_copy(disp0_in, disp0, sem.at[6]),
        ]
    )
    first = (lax.axis_index("space") * 2 + rep) * rows
    for r in range(rows):
        for k in range(slots):
            off = cols[k, r] - (first + r)
            off = jnp.where(off > HB, off - total, off)
            off = jnp.where(off < -HB, off + total, off)
            place[k, r] = r + HB + off
    now[rows + 2 * HB] = jnp.zeros(now.shape[1:], now.dtype)
    side = (rows + HB) * (1 - rep)
    for j in range(HB):
        now[side + j] = halo[j]
    end(small)
    upright = mass[...].T
    for r in range(rows):
        mass_b[r] = spread(upright, r, 128)
    part = shard.shape[2]
    home = pl.ds(pl.multiple_of(lax.axis_index("ckpt") * part, 8), part)
    stiff3 = 3.0 * stiff[...].T
    for s in range(WINDOW):
        bent[s] = stiff3 * contact[s : s + 1, :].astype(jnp.float32)
        turned[s, home, :] = shard[s].T
    end(get_vel)
    for r in range(rows):
        v = vel0[r].astype(jnp.float32)
        vel[r] = v
        now[r + HB] = (tiled(mass_b[r], lanes) * (0.5 * v)).astype(jnp.bfloat16)
    end(get_rest)
    for j in range(HB):
        disp[b_start + j] = disp0[b_start + j].astype(jnp.float32)

    def one(i):
        r = a_start + i
        disp[r] = disp0[r].astype(jnp.float32) - product(blocks, now, place, r)

    each(HB, one)


def finish_row(r, image, now, later, disp, vel, mass_b):
    d = disp[r] - image
    v = vel[r] + d
    disp[r] = d
    vel[r] = v
    if later is not None:
        p = (tiled(mass_b[r], disp.shape[2]) * v).astype(jnp.bfloat16)
        later[r + HB] = p
        return p


def joint(step, r, now, coeff):
    return tiled(coeff[step, r], now.shape[2]) * now[r + HB].astype(jnp.float32)


def coefficients(pieces, *refs):
    now, disp, vel, mass_b, bent, turned, *others = refs[5 + pieces : 10 + 2 * pieces]
    later, coeff, out_a = refs[10 + 2 * pieces :]
    rows, _, lanes = disp.shape
    part = turned.shape[1] // pieces
    me = lax.axis_index("ckpt")
    last = WINDOW - 1
    for s in range(WINDOW):
        for j, piece in enumerate(others):
            source = lax.rem(me + 1 + j, pieces)
            turned[s, pl.ds(pl.multiple_of(source * part, 8), part), :] = piece[s].T
        turned[s] = bent[s] * turned[s] * turned[s]
    full = turned[last]
    for r in range(rows):
        coeff[last, r] = spread(full, r, 128)
    later[rows + 2 * HB] = jnp.zeros(later.shape[1:], later.dtype)
    start = (rows - HB) * (1 - lax.axis_index("rep"))

    def one(i):
        r = start + i
        out_a[i] = finish_row(r, joint(last, r, now, coeff), now, later, disp, vel, mass_b)

    each(HB, one)


def first_edge(*refs):
    place, blocks, now, disp, vel, mass_b, coeff, halo, later, out = refs[-10:]
    rows = disp.shape[0]
    rep = lax.axis_index("rep")
    for j in range(HB):
        now[(rows + HB) * rep + j] = halo[j]
    start = (rows - HB) * rep

    def one(i):
        r = start + i
        image = product(blocks, now, place, r) + joint(WINDOW - 1, r, now, coeff)
        out[i] = finish_row(r, image, now, later, disp, vel, mass_b)

    each(HB, one)


def first_interior(*refs):
    place, blocks, disp0, now, later, disp, vel, mass_b, turned, coeff, dense, wide = refs[-12:]
    rows, width, lanes = disp.shape
    slots = blocks.shape[2] // width

    def one(i):
        r = HB + i
        disp[r] = disp0[r].astype(jnp.float32)
        image = product(blocks, now, place, r) + joint(WINDOW - 1, r, now, coeff)
        finish_row(r, image, now, later, disp, vel, mass_b)

    each(rows - 2 * HB, one)
    for s in range(WINDOW - 1):
        full = turned[s]
        for r in range(rows):
            coeff[s, r] = spread(full, r, 128)
    rep = lax.axis_index("rep")
    wide[...] = jnp.zeros_like(wide)
    for i in range(HB):
        r = (rows - HB) * rep + i
        block = blocks[r].astype(jnp.float32)
        for k in range(slots):
            j = place[k, r] - (rows + HB) * rep
            inside = jnp.logical_and(j >= 0, j < HB)

            @pl.when(inside)
            def _():
                at = pl.ds(i * width, width)
                wide[j, at, pl.ds(0, width)] += block[:, k * width : (k + 1) * width]

    dense[...] = jnp.concatenate([wide[j, :, :width] for j in range(HB)], axis=1).astype(
        jnp.bfloat16
    )


def near_part(step, i, blocks, now, place, coeff, disp):
    rows = disp.shape[0]
    rep = lax.axis_index("rep")
    r = (rows - HB) * rep + i
    low = (rows + HB) * rep
    slots = blocks.shape[2] // blocks.shape[1]
    picked = []
    for k in range(slots):
        p = place[k, r]
        inside = jnp.logical_and(p >= low, p < low + HB)
        picked.append(now[jnp.where(inside, rows + 2 * HB, p)])
    image = jnp.dot(
        blocks[r], jnp.concatenate(picked, axis=0), preferred_element_type=jnp.float32
    )
    disp[r] = disp[r] - (image + joint(step, r, now, coeff))


def main_rows(step, *refs):
    place, blocks, now, disp, vel, mass_b, coeff, halo, later, out = refs[-10:]
    rows = disp.shape[0]
    side = 1 - lax.axis_index("rep")
    for j in range(HB):
        now[(rows + HB) * side + j] = halo[j]
    start = HB * side

    def one(i):
        r = start + i
        image = product(blocks, now, place, r) + joint(step, r, now, coeff)
        finish_row(r, image, now, later, disp, vel, mass_b)

    each(rows - HB, one)
    for j in range(HB):
        out[j] = later[(rows - HB) * side + HB + j]
    each(HB, lambda i: near_part(step, i, blocks, now, place, coeff, disp))


def far_part(dense, halo):
    rows, width, lanes = halo.shape
    return jnp.dot(
        dense[...], halo[...].reshape(rows * width, lanes), preferred_element_type=jnp.float32
    )


def edge_rows(*refs):
    dense, disp, vel, mass_b, halo, later, out = refs[-7:]
    rows, width, _ = disp.shape
    image = far_part(dense, halo)
    start = (rows - HB) * lax.axis_index("rep")
    for i in range(HB):
        part = image[i * width : (i + 1) * width]
        out[i] = finish_row(start + i, part, None, later, disp, vel, mass_b)


def row_copies(disp, vel, disp_out, vel_out, sem, start, count, g):
    at = pl.ds(start, count)
    return [
        pltpu.make_async_copy(disp.at[at], disp_out.at[at], sem.at[0, g]),
        pltpu.make_async_copy(vel.at[at], vel_out.at[at], sem.at[1, g]),
    ]


def main_last(*refs):
    place, blocks, now, disp, vel, coeff, halo, disp_out, vel_out, sem = refs[-10:]
    rows = disp.shape[0]
    side = 1 - lax.axis_index("rep")
    for j in range(HB):
        now[(rows + HB) * side + j] = halo[j]
    sent = []
    for g in range(rows // HB - 1):
        start = HB * side + g * HB

        def one(i):
            r = start + i
            image = product(blocks, now, place, r) + joint(0, r, now, coeff)
            finish_row(r, image, now, None, disp, vel, None)

        each(HB, one)
        sent += begin(row_copies(disp, vel, disp_out, vel_out, sem, start, HB, g))
    each(HB, lambda i: near_part(0, i, blocks, now, place, coeff, disp))
    end(sent)


def edge_last(*refs):
    dense, disp, vel, halo, disp_out, vel_out, sem = refs[-7:]
    rows, width, _ = disp.shape
    image = far_part(dense, halo)
    start = (rows - HB) * lax.axis_index("rep")
    sent = []
    for i in range(HB):
        finish_row(start + i, image[i * width : (i + 1) * width], None, None, disp, vel, None)
        sent += begin(row_copies(disp, vel, disp_out, vel_out, sem, start + i, 1, i))
    end(sent)


def body(adj_disp, adj_vel, tangent_blocks, block_cols, inv_mass, joint_stiff, contact, states):
    rows, width, lanes = adj_disp.shape
    ring = lax.axis_size(RING)
    total = rows * ring
    inner, outer = ring_pairs(ring)
    pieces = lax.axis_size("ckpt")
    f32, bf16 = jnp.float32, jnp.bfloat16
    vm = pl.BlockSpec(memory_space=pltpu.VMEM)
    sm = pl.BlockSpec(memory_space=pltpu.SMEM)
    hbm = pl.BlockSpec(memory_space=pltpu.HBM)
    like = lambda a: pltpu.VMEM(a.shape, a.dtype)
    edge_t = pltpu.VMEM((HB, width, lanes), bf16)
    ext = pltpu.VMEM((rows + 2 * HB + 1, width, lanes), bf16)
    full = pltpu.VMEM((rows, width, lanes), f32)
    table = pltpu.VMEM((rows, width), f32)
    upright = pltpu.VMEM((WINDOW, width, rows), f32)
    dma = pltpu.SemaphoreType.DMA
    flops = 2 * (rows - HB) * width * tangent_blocks.shape[2] * lanes
    big = pl.CostEstimate(flops=flops // 64, bytes_accessed=100_000, transcendentals=0)
    small = pl.CostEstimate(flops=flops // 256, bytes_accessed=25_000, transcendentals=0)
    adj_disp, adj_vel, tangent_blocks, cols, inv_mass, joint_stiff, contact, mine = (
        pltpu.with_memory_space_constraint(a, pltpu.HBM)
        for a in (
            adj_disp, adj_vel, tangent_blocks, block_cols.T, inv_mass, joint_stiff, contact, states
        )
    )

    def call(kernel, name, held, given, specs, made, made_specs, scratch=(), cost=small):
        return pl.pallas_call(
            kernel,
            name=name,
            out_shape=tuple(like(a) for a in held) + tuple(made),
            in_specs=[vm] * len(held) + list(specs),
            out_specs=(vm,) * len(held) + tuple(made_specs),
            input_output_aliases={i: i for i in range(len(held))},
            scratch_shapes=list(scratch),
            compiler_params=pltpu.CompilerParams(vmem_limit_bytes=VMEM_LIMIT),
            cost_estimate=cost,
        )(*held, *given)

    out_b, out_a = call(
        head, "head", [], [adj_vel, inv_mass], [hbm] * 2, [edge_t] * 2, [vm] * 2,
        [edge_t, edge_t, table, dma((3,))],
    )
    states_late, out_a = lax.optimization_barrier((states, out_a))
    halo_a = lax.ppermute(out_a, RING, inner)
    halo_b = lax.ppermute(out_b, RING, outer)
    others = [
        lax.ppermute(states_late, "ckpt", [((i + j) % pieces, i) for i in range(pieces)])
        for j in range(1, pieces)
    ]

    _, blocks, disp0, now, disp, vel, mass_b, bent, turned, place = pl.pallas_call(
        lambda *refs: load_all(
            total, pieces, *refs[1:8], refs[0], refs[8], *refs[10:]
        ),
        name="load_all",
        out_shape=(
            edge_t, like(tangent_blocks), like(adj_disp), ext, full, full,
            pltpu.VMEM((rows, width, 128), f32), upright, upright,
            jax.ShapeDtypeStruct(cols.shape, jnp.int32),
        ),
        in_specs=[vm] + [hbm] * 7 + [sm],
        out_specs=(vm,) * 9 + (sm,),
        input_output_aliases={0: 0},
        scratch_shapes=[
            like(adj_vel), table, table, pltpu.VMEM(contact.shape, jnp.int32),
            pltpu.VMEM(states.shape, f32), dma((7,)),
        ],
        compiler_params=pltpu.CompilerParams(vmem_limit_bytes=VMEM_LIMIT),
        cost_estimate=big,
    )(halo_a, tangent_blocks, adj_vel, adj_disp, inv_mass, joint_stiff, contact, mine, cols)

    now, disp, vel, mass_b, _, turned, *_, later, coeff, out_a = call(
        functools.partial(coefficients, pieces), "coefficients",
        [now, disp, vel, mass_b, bent, turned] + others, [], [],
        [ext, pltpu.VMEM((WINDOW, rows, width, 128), f32), edge_t], [vm] * 3,
    )
    halo_a = lax.ppermute(out_a, RING, inner)
    blocks, now, disp, vel, mass_b, coeff, _, later, out_b = call(
        first_edge, "first_edge",
        [blocks, now, disp, vel, mass_b, coeff, halo_b, later], [place], [sm], [edge_t], [vm],
    )
    halo_b = lax.ppermute(out_b, RING, outer)
    blocks, _, now, later, disp, vel, mass_b, _, coeff, dense = call(
        first_interior, "first_interior",
        [blocks, disp0, now, later, disp, vel, mass_b, turned, coeff], [place], [sm],
        [pltpu.VMEM((HB * width, HB * width), bf16)], [vm],
        [pltpu.VMEM((HB, HB * width, 128), f32)], big,
    )
    for step in range(WINDOW - 2, 0, -1):
        blocks, later, disp, vel, mass_b, coeff, _, now, out_a = call(
            functools.partial(main_rows, step), "main_rows",
            [blocks, later, disp, vel, mass_b, coeff, halo_a, now], [place], [sm],
            [edge_t], [vm], (), big,
        )
        now, later = later, now
        halo_a = lax.ppermute(out_a, RING, inner)
        dense, disp, vel, mass_b, _, later, out_b = call(
            edge_rows, "edge_rows", [dense, disp, vel, mass_b, halo_b, later], [], [],
            [edge_t], [vm],
        )
        halo_b = lax.ppermute(out_b, RING, outer)

    shape = jax.ShapeDtypeStruct((rows, width, lanes), f32)
    *_, disp, vel, _, _, disp_out, vel_out = call(
        main_last, "main_last", [blocks, later, disp, vel, coeff, halo_a], [place], [sm],
        [shape] * 2, [hbm] * 2, [dma((2, rows // HB - 1))], big,
    )
    return pl.pallas_call(
        edge_last,
        name="edge_last",
        out_shape=tuple(like(a) for a in (dense, disp, vel, halo_b)) + (shape,) * 2,
        in_specs=[vm] * 4 + [hbm] * 2,
        out_specs=(vm,) * 4 + (hbm,) * 2,
        input_output_aliases={i: i for i in range(6)},
        scratch_shapes=[dma((2, HB))],
        compiler_params=pltpu.CompilerParams(vmem_limit_bytes=VMEM_LIMIT),
        cost_estimate=small,
    )(dense, disp, vel, halo_b, disp_out, vel_out)[-2:]


def solution(mesh):
    placed = (
        P(("groups", "space", "rep"), None, "ckpt"),
        P(("groups", "space", "rep"), None, "ckpt"),
        P(("groups", "space", "rep"), None, None),
        P(("groups", "space", "rep"), None),
        P(("groups", "space", "rep"), None),
        P(("groups", "space", "rep"), None),
        P(None, ("groups", "space", "rep")),
        P(None, ("groups", "space", "rep"), "ckpt"),
    )
    return jax.shard_map(
        body,
        mesh=mesh,
        in_specs=placed,
        out_specs=(
            P(("groups", "space", "rep"), None, "ckpt"),
            P(("groups", "space", "rep"), None, "ckpt"),
        ),
        check_vma=False,
    )
```

time: 130 us -> 37.1 us (0.29)
  local copies, waits for them, and re-layouts: 45 us -> 0 us
  matrix products: 29.8 us -> 0 us
  Pallas kernels: 0 us -> 19.7 us
  blocking collectives: 16.3 us -> 0 us
  other arithmetic: 12.3 us -> 0 us
  waiting for transfers between devices: 13.6 us -> 6.94 us
  starting transfers between devices: 11.7 us -> 9.4 us
    gather x3 -> x0, local copies, waits for them, and re-layouts: 30.9 us -> none  [body(): picked = extended[position].reshape(rows, slots * width, packed.shape[2])]
    dot_general x3 -> x0, matrix products: 29.8 us -> none  [body(): jnp.einsum('bik,bkr->bir', tangent_blocks, picked, preferred_element_type...]
    pallas_call x0 -> x9, Pallas kernels: none -> 19.7 us  [the longest x7 13.8 us: call(): pl.pallas_call(kernel, name=name, out_shape=tuple((like(a) for a in held)...]
    all_gather x3 -> x0, blocking collectives: 16.3 us -> none  [body(): state_now = lax.all_gather(states[step], 'ckpt', axis=1, tiled=True)]
    ppermute x6 -> x7, waiting for transfers between devices: 13.6 us -> 6.94 us  [the longest x3 6.92 us: body(): halo_b = lax.ppermute(out_b, RING, outer)]
    concatenate x3 -> x0, other arithmetic: 6.24 us -> none  [body(): extended = jnp.concatenate([lower, packed, upper], axis=0)]
    unnamed x21 -> x0, local copies, waits for them, and re-layouts: 5.3 us -> none
    all_gather x3 -> x0, local copies, waits for them, and re-layouts: 4.42 us -> none  [body(): state_now = lax.all_gather(states[step], 'ckpt', axis=1, tiled=True)]
  transfers between devices with their start and end apart: 6 -> 7, of which waited for: 2 -> 3; matrix products, arithmetic and copies ran while one was open for 12% -> 0% of each run, Pallas kernels for 0% -> 46%
where the time goes in v3:
time: 37.1 us; the launch traced here: 36.8 us
  Pallas kernels  19.7 us (53%)
  starting transfers between devices  9.4 us (25%)
  waiting for transfers between devices  6.94 us (19%)
  between operations  0.73 us (2%)
    pallas_call x7, Pallas kernels, call(): pl.pallas_call(kernel, name=name, out_shape=tuple((like(a) for a in held)...  13.8 us
    ppermute x3, starting transfers between devices, body(): halo_b = lax.ppermute(out_b, RING, outer)  7.25 us
    ppermute x3, waiting for transfers between devices, body(): halo_b = lax.ppermute(out_b, RING, outer)  6.92 us
    pallas_call x1, Pallas kernels, body(): pl.pallas_call(lambda *refs: load_all(total, pieces, *refs[1:8], refs[0],...  4.54 us
    ppermute x1, starting transfers between devices, body(): lax.ppermute(states_late, 'ckpt', [((i + j) % pieces, i) for i in range(p...  1.49 us
    pallas_call x1, Pallas kernels, body(): pl.pallas_call(edge_last, name='edge_last', out_shape=tuple((like(a) for...  1.37 us
  transfers between devices with their start and end apart: 7, of which 3 were waited for; matrix products, arithmetic and copies ran while one was open for 0% of the time, Pallas kernels for 46%

profile of v3, /device:TPU:0, one launch (start us, length us, event | category | flops | bytes accessed | tf_op | source)
XLA Modules:
  0.0 36.8 jit_solution(5342638234296020502)
XLA Ops:
  0.6 1.4 %head.1 = (bf16[4,96,384]{2,1,0:T(8,128)(2,1)S(1)}, bf16[4,96,384]{2,1,0:T(8,128)(2,1)S(1)}) custom-call(bf16[20,96,384]{2,1,0:T(8,128)(2,1)} %refs_2_.1, f32[20,96]{1,0:T(8,128)} %refs_4_.1), custom_call_target="tpu_custom_call" | custom-call | flops 3538944 | bytes 25000 | tf_op jit(solution)/shard_map/head/pallas_call | solution.py:350
  2.0 0.5 %collective-permute-start = (bf16[4,96,384]{2,1,0:T(8,128)(2,1)S(1)}, bf16[4,96,384]{2,1,0:T(8,128)(2,1)S(1)}, u32[]{:S(2)}, u32[]{:S(2)}) collective-permute-start(bf16[4,96,384]{2,1,0:T(8,128)(2,1)S(1)} %get-tuple-element.58), channel_id=1, source_target_pairs={{0,1},{1,0},{4,5},{5,4},{8,9},{9,8},{12,13},{13,12},{2,3},{3,2},{6... | collective-permute-start | bytes 884744 | tf_op jit(solution)/shard_map/ppermute | solution.py:367
  2.6 4.7 %collective-permute-start.2 = (bf16[4,96,384]{2,1,0:T(8,128)(2,1)S(1)}, bf16[4,96,384]{2,1,0:T(8,128)(2,1)S(1)}, u32[]{:S(2)}, u32[]{:S(2)}) collective-permute-start(bf16[4,96,384]{2,1,0:T(8,128)(2,1)S(1)} %get-tuple-element.72), channel_id=1, source_target_pairs={{1,4},{5,8},{9,12},{13,0},{4,1},{8,5},{12,9},{0,13},{3,6},{7,10},{... | collective-permute-start | bytes 884744 | tf_op jit(solution)/shard_map/ppermute | solution.py:368
  7.3 1.5 %collective-permute-start.1 = (f32[3,20,48]{2,1,0:T(8,128)}, f32[3,20,48]{2,1,0:T(8,128)S(1)}, u32[]{:S(2)}, u32[]{:S(2)}) collective-permute-start(f32[3,20,48]{2,1,0:T(8,128)} %refs_7_.1), channel_id=1, source_target_pairs={{2,0},{0,2},{3,1},{1,3},{6,4},{4,6},{7,5},{5,7},{10,8},{8,10},{11,... | collective-permute-start | bytes 34568 | tf_op jit(solution)/shard_map/ppermute | solution.py:370
  8.8 0.0 collective-permute-done.refs_0_
  8.8 4.5 %load_all.1 = (bf16[4,96,384]{2,1,0:T(8,128)(2,1)S(1)}, bf16[20,96,768]{2,1,0:T(8,128)(2,1)S(1)}, bf16[20,96,384]{2,1,0:T(8,128)(2,1)S(1)}, bf16[29,96,384]{2,1,...) custom-call(bf16[4,96,384]{2,1,0:T(8,128)(2,1)S(1)} %collective-perm, ...), custom_call_target="tpu_custom_call", output_to_operand_aliasing={{0}: (0, {})} | custom-call | flops 14155776 | bytes 100000 | tf_op jit(solution)/shard_map/load_all/pallas_call | solution.py:374
  13.3 0.0 collective-permute-done.1.refs_6_
  13.3 0.6 %coefficients.1 = (bf16[29,96,384]{2,1,0:T(8,128)(2,1)S(1)}, f32[20,96,384]{2,1,0:T(8,128)S(1)}, f32[20,96,384]{2,1,0:T(8,128)S(1)}, f32[20,96,128]{2,1,0:T(8,12...) custom-call(bf16[29,96,384]{2,1,0:T(8,128)(2,1)S(1)} %get-tuple-elem, ...), custom_call_target="tpu_custom_call", output_to_operand_aliasing={{0}: (0, {}), {1}: (1, {}), {2}: (2, {}), {3}: (3, {}), {4}... | custom-call | flops 3538944 | bytes 25000 | tf_op jit(solution)/shard_map/coefficients/pallas_call | solution.py:350
  13.9 0.1 collective-permute-start.3
  14.0 0.1 collective-permute-done.2.refs_6_
  14.1 1.2 %first_edge.1 = (bf16[20,96,768]{2,1,0:T(8,128)(2,1)S(1)}, bf16[29,96,384]{2,1,0:T(8,128)(2,1)S(1)}, f32[20,96,384]{2,1,0:T(8,128)S(1)}, f32[20,96,384]{2,1,0:T(...) custom-call(bf16[20,96,768]{2,1,0:T(8,128)(2,1)S(1)} %get-tuple-elem, ...), custom_call_target="tpu_custom_call", output_to_operand_aliasing={{0}: (0, {}), {1}: (1, {}), {2}: (2, {}), {3}: (3, {}), {4}... | custom-call | flops 3538944 | bytes 25000 | tf_op jit(solution)/shard_map/first_edge/pallas_call | solution.py:350
  15.3 1.8 %collective-permute-start.4 = (bf16[4,96,384]{2,1,0:T(8,128)(2,1)S(1)}, bf16[4,96,384]{2,1,0:T(8,128)(2,1)S(1)}, u32[]{:S(2)}, u32[]{:S(2)}) collective-permute-start(bf16[4,96,384]{2,1,0:T(8,128)(2,1)S(1)} %get-tuple-element.96), channel_id=1, source_target_pairs={{1,4},{5,8},{9,12},{13,0},{4,1},{8,5},{12,9},{0,13},{3,6},{7,10},{... | collective-permute-start | bytes 884744 | tf_op jit(solution)/shard_map/ppermute | solution.py:405
  17.2 3.4 %first_interior.1 = (bf16[20,96,768]{2,1,0:T(8,128)(2,1)S(1)}, bf16[20,96,384]{2,1,0:T(8,128)(2,1)S(1)}, bf16[29,96,384]{2,1,0:T(8,128)(2,1)S(1)}, bf16[29,96,38...) custom-call(bf16[20,96,768]{2,1,0:T(8,128)(2,1)S(1)} %get-tuple-elem, ...), custom_call_target="tpu_custom_call", output_to_operand_aliasing={{0}: (0, {}), {1}: (1, {}), {2}: (2, {}), {3}: (3, {}), {4}... | custom-call | flops 14155776 | bytes 100000 | tf_op jit(solution)/shard_map/first_interior/pallas_call | solution.py:350
  20.6 0.0 collective-permute-done.3.refs_6_
  20.6 3.1 %main_rows.1 = (bf16[20,96,768]{2,1,0:T(8,128)(2,1)S(1)}, bf16[29,96,384]{2,1,0:T(8,128)(2,1)S(1)}, f32[20,96,384]{2,1,0:T(8,128)S(1)}, f32[20,96,384]{2,1,0:T(8...) custom-call(bf16[20,96,768]{2,1,0:T(8,128)(2,1)S(1)} %get-tuple-elem, ...), custom_call_target="tpu_custom_call", output_to_operand_aliasing={{0}: (0, {}), {1}: (1, {}), {2}: (2, {}), {3}: (3, {}), {4}... | custom-call | flops 14155776 | bytes 100000 | tf_op jit(solution)/shard_map/main_rows/pallas_call | solution.py:350
  23.7 0.1 collective-permute-start.5
  23.8 1.9 %collective-permute-done.4.refs_4_ = bf16[4,96,384]{2,1,0:T(8,128)(2,1)S(1)} collective-permute-done((bf16[4,96,384]{2,1,0:T(8,128)(2,1)S(1)}, bf16[4,96,384]{2,1,0:T(8,128)(2,1)S(1)}, u32[]{:S(2)}, u32[]{:S(2)}) %collective-permute-start.4) | collective-permute-done | bytes 294944 | tf_op jit(solution)/shard_map/ppermute | solution.py:405
  25.7 0.4 %edge_rows.1 = (bf16[384,384]{1,0:T(8,128)(2,1)S(1)}, f32[20,96,384]{2,1,0:T(8,128)S(1)}, f32[20,96,384]{2,1,0:T(8,128)S(1)}, f32[20,96,128]{2,1,0:T(8,128)S(1)}...) custom-call(bf16[384,384]{1,0:T(8,128)(2,1)S(1)} %get-tuple-element., ...), custom_call_target="tpu_custom_call", output_to_operand_aliasing={{0}: (0, {}), {1}: (1, {}), {2}: (2, {}), {3}: (3, {}), {4}... | custom-call | flops 3538944 | bytes 25000 | tf_op jit(solution)/shard_map/edge_rows/pallas_call | solution.py:350
  26.1 0.7 %collective-permute-start.6 = (bf16[4,96,384]{2,1,0:T(8,128)(2,1)S(1)}, bf16[4,96,384]{2,1,0:T(8,128)(2,1)S(1)}, u32[]{:S(2)}, u32[]{:S(2)}) collective-permute-start(bf16[4,96,384]{2,1,0:T(8,128)(2,1)S(1)} %get-tuple-element.107), channel_id=1, source_target_pairs={{1,4},{5,8},{9,12},{13,0},{4,1},{8,5},{12,9},{0,13},{3,6},{7,10},{... | collective-permute-start | bytes 884744 | tf_op jit(solution)/shard_map/ppermute | solution.py:424
  26.8 0.0 collective-permute-done.5.refs_5_
  26.8 3.7 %main_last.1 = (bf16[20,96,768]{2,1,0:T(8,128)(2,1)S(1)}, bf16[29,96,384]{2,1,0:T(8,128)(2,1)S(1)}, f32[20,96,384]{2,1,0:T(8,128)S(1)}, f32[20,96,384]{2,1,0:T(8...) custom-call(bf16[20,96,768]{2,1,0:T(8,128)(2,1)S(1)} %get-tuple-elem, ...), custom_call_target="tpu_custom_call", output_to_operand_aliasing={{0}: (0, {}), {1}: (1, {}), {2}: (2, {}), {3}: (3, {}), {4}... | custom-call | flops 14155776 | bytes 100000 | tf_op jit(solution)/shard_map/main_last/pallas_call | solution.py:350
  30.6 4.9 %collective-permute-done.6.refs_3_ = bf16[4,96,384]{2,1,0:T(8,128)(2,1)S(1)} collective-permute-done((bf16[4,96,384]{2,1,0:T(8,128)(2,1)S(1)}, bf16[4,96,384]{2,1,0:T(8,128)(2,1)S(1)}, u32[]{:S(2)}, u32[]{:S(2)}) %collective-permute-start.6) | collective-permute-done | bytes 294944 | tf_op jit(solution)/shard_map/ppermute | solution.py:424
  35.4 1.4 %edge_last.1 = (bf16[384,384]{1,0:T(8,128)(2,1)S(1)}, f32[20,96,384]{2,1,0:T(8,128)S(1)}, f32[20,96,384]{2,1,0:T(8,128)S(1)}, bf16[4,96,384]{2,1,0:T(8,128)(2,1)...) custom-call(bf16[384,384]{1,0:T(8,128)(2,1)S(1)} %get-tuple-element., ...), custom_call_target="tpu_custom_call", output_to_operand_aliasing={{0}: (0, {}), {1}: (1, {}), {2}: (2, {}), {3}: (3, {}), {4}... | custom-call | flops 3538944 | bytes 25000 | tf_op jit(solution)/shard_map/edge_last/pallas_call | solution.py:431
Async XLA Ops:
  2.0 6.7 %collective-permute-start = (bf16[4,96,384]{2,1,0:T(8,128)(2,1)S(1)}, bf16[4,96,384]{2,1,0:T(8,128)(2,1)S(1)}, u32[]{:S(2)}, u32[]{:S(2)}) collective-permute-start(bf16[4,96,384]{2,1,0:T(8,128)(2,1)S(1)} %get-tuple-element.58), channel_id=1, source_target_pairs={{0,1},{1,0},{4,5},{5,4},{8,9},{9,8},{12,13},{13,12},{2,3},{3,2},{6... | collective-permute-start | bytes 884744 | tf_op jit(solution)/shard_map/ppermute | solution.py:367
  2.6 11.6 %collective-permute-start.2 = (bf16[4,96,384]{2,1,0:T(8,128)(2,1)S(1)}, bf16[4,96,384]{2,1,0:T(8,128)(2,1)S(1)}, u32[]{:S(2)}, u32[]{:S(2)}) collective-permute-start(bf16[4,96,384]{2,1,0:T(8,128)(2,1)S(1)} %get-tuple-element.72), channel_id=1, source_target_pairs={{1,4},{5,8},{9,12},{13,0},{4,1},{8,5},{12,9},{0,13},{3,6},{7,10},{... | collective-permute-start | bytes 884744 | tf_op jit(solution)/shard_map/ppermute | solution.py:368
  7.3 6.0 %collective-permute-start.1 = (f32[3,20,48]{2,1,0:T(8,128)}, f32[3,20,48]{2,1,0:T(8,128)S(1)}, u32[]{:S(2)}, u32[]{:S(2)}) collective-permute-start(f32[3,20,48]{2,1,0:T(8,128)} %refs_7_.1), channel_id=1, source_target_pairs={{2,0},{0,2},{3,1},{1,3},{6,4},{4,6},{7,5},{5,7},{10,8},{8,10},{11,... | collective-permute-start | bytes 34568 | tf_op jit(solution)/shard_map/ppermute | solution.py:370
  13.9 6.7 %collective-permute-start.3 = (bf16[4,96,384]{2,1,0:T(8,128)(2,1)S(1)}, bf16[4,96,384]{2,1,0:T(8,128)(2,1)S(1)}, u32[]{:S(2)}, u32[]{:S(2)}) collective-permute-start(bf16[4,96,384]{2,1,0:T(8,128)(2,1)S(1)} %get-tuple-element.91), channel_id=1, source_target_pairs={{0,1},{1,0},{4,5},{5,4},{8,9},{9,8},{12,13},{13,12},{2,3},{3,2},{6... | collective-permute-start | bytes 884744 | tf_op jit(solution)/shard_map/ppermute | solution.py:400
  15.3 10.4 %collective-permute-start.4 = (bf16[4,96,384]{2,1,0:T(8,128)(2,1)S(1)}, bf16[4,96,384]{2,1,0:T(8,128)(2,1)S(1)}, u32[]{:S(2)}, u32[]{:S(2)}) collective-permute-start(bf16[4,96,384]{2,1,0:T(8,128)(2,1)S(1)} %get-tuple-element.96), channel_id=1, source_target_pairs={{1,4},{5,8},{9,12},{13,0},{4,1},{8,5},{12,9},{0,13},{3,6},{7,10},{... | collective-permute-start | bytes 884744 | tf_op jit(solution)/shard_map/ppermute | solution.py:405
  23.7 3.1 %collective-permute-start.5 = (bf16[4,96,384]{2,1,0:T(8,128)(2,1)S(1)}, bf16[4,96,384]{2,1,0:T(8,128)(2,1)S(1)}, u32[]{:S(2)}, u32[]{:S(2)}) collective-permute-start(bf16[4,96,384]{2,1,0:T(8,128)(2,1)S(1)} %get-tuple-element.104), channel_id=1, source_target_pairs={{0,1},{1,0},{4,5},{5,4},{8,9},{9,8},{12,13},{13,12},{2,3},{3,2},{6... | collective-permute-start | bytes 884744 | tf_op jit(solution)/shard_map/ppermute | solution.py:419
  26.1 9.3 %collective-permute-start.6 = (bf16[4,96,384]{2,1,0:T(8,128)(2,1)S(1)}, bf16[4,96,384]{2,1,0:T(8,128)(2,1)S(1)}, u32[]{:S(2)}, u32[]{:S(2)}) collective-permute-start(bf16[4,96,384]{2,1,0:T(8,128)(2,1)S(1)} %get-tuple-element.107), channel_id=1, source_target_pairs={{1,4},{5,8},{9,12},{13,0},{4,1},{8,5},{12,9},{0,13},{3,6},{7,10},{... | collective-permute-start | bytes 884744 | tf_op jit(solution)/shard_map/ppermute | solution.py:424

commit v4 on v3

v4 whole, which is shorter than its diff:
```python
import functools
import jax
import jax.numpy as jnp
from jax import lax
from jax.experimental import pallas as pl
from jax.experimental.pallas import tpu as pltpu
from jax.sharding import PartitionSpec as P

HB = 4
WINDOW = 3
RING = ("space", "rep")
VMEM_LIMIT = 24 * 1024 * 1024


def ring_pairs(ring):
    inner = [(i, i ^ 1) for i in range(ring)]
    outer = [(i, (i + 1) % ring) for i in range(1, ring, 2)]
    outer = outer + [(b, a) for a, b in outer]
    return inner, outer


def windows_of(lanes):
    tiles = lanes // 128
    if tiles < 2:
        return [(0, lanes)]
    cut = 128 * ((tiles + 1) // 2)
    return [(0, cut), (cut, lanes - cut)]


def product(blocks, packed, place, r, window=None):
    slots = blocks.shape[2] // blocks.shape[1]
    at = slice(None) if window is None else pl.ds(*window)
    picked = jnp.concatenate([packed[place[k, r], :, at] for k in range(slots)], axis=0)
    return jnp.dot(blocks[r], picked, preferred_element_type=jnp.float32)


def tiled(column, lanes):
    return jnp.concatenate([column] * (lanes // 128), axis=1)


def spread(matrix, r, lanes):
    return jnp.broadcast_to(matrix[:, r : r + 1], (matrix.shape[0], lanes))


def each(count, one):
    def run(i, carry):
        one(i)
        return carry

    lax.fori_loop(0, count, run, 0, unroll=True)


def begin(copies):
    for c in copies:
        c.start()
    return copies


def end(copies):
    for c in copies:
        c.wait()


def head(vel0, inv_mass, *refs):
    *out_b, out_a, low, high, mass, sem = refs
    rows, _, lanes = vel0.shape
    end(
        begin(
            [
                pltpu.make_async_copy(inv_mass, mass, sem.at[0]),
                pltpu.make_async_copy(vel0.at[pl.ds(0, HB)], low, sem.at[1]),
                pltpu.make_async_copy(vel0.at[pl.ds(rows - HB, HB)], high, sem.at[2]),
            ]
        )
    )
    rep = lax.axis_index("rep")
    upright = mass[...].T
    for j in range(HB):
        p = spread(upright, j, lanes) * (0.5 * low[j].astype(jnp.float32))
        q = spread(upright, rows - HB + j, lanes) * (0.5 * high[j].astype(jnp.float32))
        b = jnp.where(rep == 0, p, q).astype(jnp.bfloat16)
        for ref, (at, size) in zip(out_b, windows_of(lanes)):
            ref[j] = b[:, at : at + size]
        out_a[j] = jnp.where(rep == 0, q, p).astype(jnp.bfloat16)


def load_all(total, blocks_in, vel0_in, disp0_in, inv_mass, stiff_in, contact_in, mine, cols_in, *refs):
    halo, blocks, now, disp, vel, mass_b, bent, turned, place_out = refs[:9]
    vel0, edges, cols, place, mass, stiff, contact, shard, sem = refs[9:]
    rows, _, lanes = vel0.shape
    rep = lax.axis_index("rep")
    a_start = (rows - HB) * (1 - rep)
    b_start = (rows - HB) * rep
    sides = (pl.ds(a_start, HB), pl.ds(b_start, HB))
    get_cols = begin([pltpu.make_async_copy(cols_in, cols, sem.at[0])])
    small = begin(
        [
            pltpu.make_async_copy(inv_mass, mass, sem.at[1]),
            pltpu.make_async_copy(stiff_in, stiff, sem.at[2]),
            pltpu.make_async_copy(contact_in, contact, sem.at[3]),
            pltpu.make_async_copy(mine, shard, sem.at[4]),
        ]
    )
    get_vel = begin([pltpu.make_async_copy(vel0_in, vel0, sem.at[5])])
    get_rest = begin(
        [
            pltpu.make_async_copy(blocks_in.at[at], blocks.at[at], sem.at[6 + n])
            for n, at in enumerate(sides)
        ]
        + [
            pltpu.make_async_copy(disp0_in.at[at], edges.at[n], sem.at[8 + n])
            for n, at in enumerate(sides)
        ]
    )
    now[rows + 2 * HB] = jnp.zeros(now.shape[1:], now.dtype)
    side = (rows + HB) * (1 - rep)
    for j in range(HB):
        now[side + j] = halo[j]
    end(get_cols)
    first = (lax.axis_index("space") * 2 + rep) * rows
    row = lax.broadcasted_iota(jnp.int32, cols.shape, 1)
    off = cols[...] - (first + row)
    off = jnp.where(off > HB, off - total, off)
    off = jnp.where(off < -HB, off + total, off)
    place_out[...] = row + HB + off
    get_place = begin([pltpu.make_async_copy(place_out, place, sem.at[0])])
    end(small)
    upright = mass[...].T
    for r in range(rows):
        mass_b[r] = spread(upright, r, 128)
    part = shard.shape[2]
    home = pl.ds(pl.multiple_of(lax.axis_index("ckpt") * part, 8), part)
    stiff3 = 3.0 * stiff[...].T
    for s in range(WINDOW):
        bent[s] = stiff3 * contact[s : s + 1, :].astype(jnp.float32)
        turned[s, home, :] = shard[s].T
    end(get_vel)
    for r in range(rows):
        v = vel0[r].astype(jnp.float32)
        vel[r] = v
        now[r + HB] = (tiled(mass_b[r], lanes) * (0.5 * v)).astype(jnp.bfloat16)
    end(get_place)
    end(get_rest)
    for j in range(HB):
        disp[b_start + j] = edges[1, j].astype(jnp.float32)

    def one(i):
        r = a_start + i
        disp[r] = edges[0, i].astype(jnp.float32) - product(blocks, now, place, r)

    each(HB, one)


def finish_row(r, image, later, disp, vel, mass_b, window=None):
    at = slice(None) if window is None else pl.ds(*window)
    d = disp[r, :, at] - image
    v = vel[r, :, at] + d
    disp[r, :, at] = d
    vel[r, :, at] = v
    if later is not None:
        p = (tiled(mass_b[r], image.shape[1]) * v).astype(jnp.bfloat16)
        later[r + HB, :, at] = p
        return p


def joint(step, r, now, coeff, window=None):
    at = slice(None) if window is None else pl.ds(*window)
    own = now[r + HB, :, at].astype(jnp.float32)
    return tiled(coeff[step, r], own.shape[1]) * own


def coefficients(pieces, *refs):
    now, disp, vel, mass_b, bent, turned, *others = refs[5 + pieces : 10 + 2 * pieces]
    later, coeff, out_a = refs[10 + 2 * pieces :]
    rows, _, lanes = disp.shape
    part = turned.shape[1] // pieces
    me = lax.axis_index("ckpt")
    last = WINDOW - 1
    for s in range(WINDOW):
        for j, piece in enumerate(others):
            source = lax.rem(me + 1 + j, pieces)
            turned[s, pl.ds(pl.multiple_of(source * part, 8), part), :] = piece[s].T
        turned[s] = bent[s] * turned[s] * turned[s]
    full = turned[last]
    for r in range(rows):
        coeff[last, r] = spread(full, r, 128)
    later[rows + 2 * HB] = jnp.zeros(later.shape[1:], later.dtype)
    start = (rows - HB) * (1 - lax.axis_index("rep"))

    def one(i):
        r = start + i
        out_a[i] = finish_row(r, joint(last, r, now, coeff), later, disp, vel, mass_b)

    each(HB, one)


def first_edge(window, *refs):
    place, blocks, now, disp, vel, mass_b, coeff, halo, later, out = refs[-10:]
    rows = disp.shape[0]
    rep = lax.axis_index("rep")
    at = pl.ds(*window)
    for j in range(HB):
        now[(rows + HB) * rep + j, :, at] = halo[j]
    start = (rows - HB) * rep

    def one(i):
        r = start + i
        image = product(blocks, now, place, r, window)
        image = image + joint(WINDOW - 1, r, now, coeff, window)
        out[i] = finish_row(r, image, later, disp, vel, mass_b, window)

    each(HB, one)


def first_interior(*refs):
    blocks_in, disp0_in, place = refs[8:11]
    blocks, now, later, disp, vel, mass_b, turned, coeff, dense, wide, disp0, sem = refs[11:]
    rows, width, lanes = disp.shape
    slots = blocks.shape[2] // width
    loads = []
    for g in range(1, rows // HB - 1):
        at = pl.ds(g * HB, HB)
        loads.append(
            begin(
                [
                    pltpu.make_async_copy(blocks_in.at[at], blocks.at[at], sem.at[0, g]),
                    pltpu.make_async_copy(disp0_in.at[at], disp0.at[at], sem.at[1, g]),
                ]
            )
        )
    for s in range(WINDOW - 1):
        full = turned[s]
        for r in range(rows):
            coeff[s, r] = spread(full, r, 128)
    rep = lax.axis_index("rep")
    wide[...] = jnp.zeros_like(wide)
    for i in range(HB):
        r = (rows - HB) * rep + i
        block = blocks[r].astype(jnp.float32)
        for k in range(slots):
            j = place[k, r] - (rows + HB) * rep
            inside = jnp.logical_and(j >= 0, j < HB)

            @pl.when(inside)
            def _():
                at = pl.ds(i * width, width)
                wide[j, at, pl.ds(0, width)] += block[:, k * width : (k + 1) * width]

    dense[...] = jnp.concatenate([wide[j, :, :width] for j in range(HB)], axis=1).astype(
        jnp.bfloat16
    )
    for g, load in enumerate(loads, 1):
        end(load)
        for r in range(g * HB, (g + 1) * HB):
            disp[r] = disp0[r].astype(jnp.float32)
            image = product(blocks, now, place, r) + joint(WINDOW - 1, r, now, coeff)
            finish_row(r, image, later, disp, vel, mass_b)


def near_part(step, i, blocks, now, place, coeff, disp):
    rows = disp.shape[0]
    rep = lax.axis_index("rep")
    r = (rows - HB) * rep + i
    low = (rows + HB) * rep
    slots = blocks.shape[2] // blocks.shape[1]
    picked = []
    for k in range(slots):
        p = place[k, r]
        inside = jnp.logical_and(p >= low, p < low + HB)
        picked.append(now[jnp.where(inside, rows + 2 * HB, p)])
    image = jnp.dot(
        blocks[r], jnp.concatenate(picked, axis=0), preferred_element_type=jnp.float32
    )
    disp[r] = disp[r] - (image + joint(step, r, now, coeff))


def main_rows(step, *refs):
    place, blocks, now, disp, vel, mass_b, coeff, halo, later, out = refs[-10:]
    rows = disp.shape[0]
    side = 1 - lax.axis_index("rep")
    for j in range(HB):
        now[(rows + HB) * side + j] = halo[j]
    start = HB * side

    def one(i):
        r = start + i
        image = product(blocks, now, place, r) + joint(step, r, now, coeff)
        finish_row(r, image, later, disp, vel, mass_b)

    each(rows - HB, one)
    for j in range(HB):
        out[j] = later[(rows - HB) * side + HB + j]
    each(HB, lambda i: near_part(step, i, blocks, now, place, coeff, disp))


def far_part(dense, halo):
    rows, width, lanes = halo.shape
    return jnp.dot(
        dense[...], halo[...].reshape(rows * width, lanes), preferred_element_type=jnp.float32
    )


def edge_rows(window, *refs):
    dense, disp, vel, mass_b, halo, later, out = refs[-7:]
    rows, width, _ = disp.shape
    image = far_part(dense, halo)
    start = (rows - HB) * lax.axis_index("rep")
    for i in range(HB):
        part = image[i * width : (i + 1) * width]
        out[i] = finish_row(start + i, part, later, disp, vel, mass_b, window)


def row_copies(disp, vel, disp_out, vel_out, sem, start, count, g, window):
    at = (pl.ds(start, count), slice(None), pl.ds(*window))
    return [
        pltpu.make_async_copy(disp.at[at], disp_out.at[at], sem.at[0, g]),
        pltpu.make_async_copy(vel.at[at], vel_out.at[at], sem.at[1, g]),
    ]


def main_last(*refs):
    place, blocks, now, disp, vel, coeff, halo, disp_out, vel_out, sem = refs[-10:]
    rows = disp.shape[0]
    side = 1 - lax.axis_index("rep")
    for j in range(HB):
        now[(rows + HB) * side + j] = halo[j]
    sent = []
    for g in range(rows // HB - 1):
        start = HB * side + g * HB

        def one(i):
            r = start + i
            image = product(blocks, now, place, r) + joint(0, r, now, coeff)
            finish_row(r, image, None, disp, vel, None)

        each(HB, one)
        copies = row_copies(disp, vel, disp_out, vel_out, sem, start, HB, g, (0, disp.shape[2]))
        sent += begin(copies)
    each(HB, lambda i: near_part(0, i, blocks, now, place, coeff, disp))
    end(sent)


def edge_last(window, *refs):
    dense, disp, vel, halo, disp_out, vel_out, sem = refs[-7:]
    rows, width, _ = disp.shape
    image = far_part(dense, halo)
    start = (rows - HB) * lax.axis_index("rep")
    sent = []
    for i in range(HB):
        part = image[i * width : (i + 1) * width]
        finish_row(start + i, part, None, disp, vel, None, window)
        sent += begin(row_copies(disp, vel, disp_out, vel_out, sem, start + i, 1, i, window))
    end(sent)


def body(adj_disp, adj_vel, tangent_blocks, block_cols, inv_mass, joint_stiff, contact, states):
    rows, width, lanes = adj_disp.shape
    ring = lax.axis_size(RING)
    total = rows * ring
    inner, outer = ring_pairs(ring)
    pieces = lax.axis_size("ckpt")
    f32, bf16 = jnp.float32, jnp.bfloat16
    vm = pl.BlockSpec(memory_space=pltpu.VMEM)
    sm = pl.BlockSpec(memory_space=pltpu.SMEM)
    hbm = pl.BlockSpec(memory_space=pltpu.HBM)
    like = lambda a: pltpu.VMEM(a.shape, a.dtype)
    edge_t = pltpu.VMEM((HB, width, lanes), bf16)
    ext = pltpu.VMEM((rows + 2 * HB + 1, width, lanes), bf16)
    full = pltpu.VMEM((rows, width, lanes), f32)
    table = pltpu.VMEM((rows, width), f32)
    upright = pltpu.VMEM((WINDOW, width, rows), f32)
    dma = pltpu.SemaphoreType.DMA
    light = pl.CostEstimate(flops=1000, bytes_accessed=1000, transcendentals=0)
    heavy = pl.CostEstimate(flops=4_000_000_000, bytes_accessed=1000, transcendentals=0)
    adj_disp, adj_vel, tangent_blocks, cols, inv_mass, joint_stiff, contact, mine = (
        pltpu.with_memory_space_constraint(a, pltpu.HBM)
        for a in (
            adj_disp, adj_vel, tangent_blocks, block_cols.T, inv_mass, joint_stiff, contact, states
        )
    )

    def call(kernel, name, held, given, specs, made, made_specs, scratch=(), cost=light):
        return pl.pallas_call(
            kernel,
            name=name,
            out_shape=tuple(like(a) for a in held) + tuple(made),
            in_specs=[vm] * len(held) + list(specs),
            out_specs=(vm,) * len(held) + tuple(made_specs),
            input_output_aliases={i: i for i in range(len(held))},
            scratch_shapes=list(scratch),
            compiler_params=pltpu.CompilerParams(vmem_limit_bytes=VMEM_LIMIT),
            cost_estimate=cost,
        )(*held, *given)

    windows = windows_of(lanes)
    edges_t = [pltpu.VMEM((HB, width, size), bf16) for _, size in windows]

    *out_b, out_a = call(
        head, "head", [], [adj_vel, inv_mass], [hbm] * 2,
        edges_t + [edge_t], [vm] * (len(windows) + 1), [edge_t, edge_t, table, dma((3,))],
    )
    states_late, out_a = lax.optimization_barrier((states, out_a))
    halo_a = lax.ppermute(out_a, RING, inner)
    halo_b = [lax.ppermute(a, RING, outer) for a in out_b]
    others = [
        lax.ppermute(states_late, "ckpt", [((i + j) % pieces, i) for i in range(pieces)])
        for j in range(1, pieces)
    ]

    _, blocks, now, disp, vel, mass_b, bent, turned, place = call(
        lambda *refs: load_all(total, *refs[1:9], refs[0], *refs[10:]), "load_all",
        [halo_a],
        [tangent_blocks, adj_vel, adj_disp, inv_mass, joint_stiff, contact, mine, cols], [hbm] * 8,
        [
            like(tangent_blocks), ext, full, full, pltpu.VMEM((rows, width, 128), f32),
            upright, upright, like(cols),
        ],
        [vm] * 8,
        [
            like(adj_vel), pltpu.VMEM((2, HB, width, lanes), bf16), like(cols),
            pltpu.SMEM(cols.shape, jnp.int32), table, table,
            pltpu.VMEM(contact.shape, jnp.int32), pltpu.VMEM(states.shape, f32), dma((10,)),
        ],
    )
    now, disp, vel, mass_b, _, turned, *_, later, coeff, out_a = call(
        functools.partial(coefficients, pieces), "coefficients",
        [now, disp, vel, mass_b, bent, turned] + others, [], [],
        [ext, pltpu.VMEM((WINDOW, rows, width, 128), f32), edge_t], [vm] * 3,
    )
    halo_a = lax.ppermute(out_a, RING, inner)
    for n, window in enumerate(windows):
        blocks, now, disp, vel, mass_b, coeff, _, later, out = call(
            functools.partial(first_edge, window), "first_edge",
            [blocks, now, disp, vel, mass_b, coeff, halo_b[n], later], [place], [sm],
            [edges_t[n]], [vm], (), heavy if n else light,
        )
        halo_b[n] = lax.ppermute(out, RING, outer)
    blocks, now, later, disp, vel, mass_b, _, coeff, dense = call(
        first_interior, "first_interior",
        [blocks, now, later, disp, vel, mass_b, turned, coeff],
        [tangent_blocks, adj_disp, place], [hbm, hbm, sm],
        [pltpu.VMEM((HB * width, HB * width), bf16)], [vm],
        [pltpu.VMEM((HB, HB * width, 128), f32), like(adj_disp), dma((2, rows // HB))],
    )
    for step in range(WINDOW - 2, 0, -1):
        blocks, later, disp, vel, mass_b, coeff, _, now, out_a = call(
            functools.partial(main_rows, step), "main_rows",
            [blocks, later, disp, vel, mass_b, coeff, halo_a, now], [place], [sm],
            [edge_t], [vm],
        )
        now, later = later, now
        halo_a = lax.ppermute(out_a, RING, inner)
        for n, window in enumerate(windows):
            dense, disp, vel, mass_b, _, later, out = call(
                functools.partial(edge_rows, window), "edge_rows",
                [dense, disp, vel, mass_b, halo_b[n], later], [], [], [edges_t[n]], [vm],
                (), heavy if n else light,
            )
            halo_b[n] = lax.ppermute(out, RING, outer)

    shape = jax.ShapeDtypeStruct((rows, width, lanes), f32)
    *_, disp, vel, _, _, disp_out, vel_out = call(
        main_last, "main_last", [blocks, later, disp, vel, coeff, halo_a], [place], [sm],
        [shape] * 2, [hbm] * 2, [dma((2, rows // HB - 1))],
    )
    for n, window in enumerate(windows):
        dense, disp, vel, _, disp_out, vel_out = pl.pallas_call(
            functools.partial(edge_last, window),
            name="edge_last",
            out_shape=tuple(like(a) for a in (dense, disp, vel, halo_b[n])) + (shape,) * 2,
            in_specs=[vm] * 4 + [hbm] * 2,
            out_specs=(vm,) * 4 + (hbm,) * 2,
            input_output_aliases={i: i for i in range(6)},
            scratch_shapes=[dma((2, HB))],
            compiler_params=pltpu.CompilerParams(vmem_limit_bytes=VMEM_LIMIT),
            cost_estimate=light,
        )(dense, disp, vel, halo_b[n], disp_out, vel_out)
    return disp_out, vel_out


def solution(mesh):
    placed = (
        P(("groups", "space", "rep"), None, "ckpt"),
        P(("groups", "space", "rep"), None, "ckpt"),
        P(("groups", "space", "rep"), None, None),
        P(("groups", "space", "rep"), None),
        P(("groups", "space", "rep"), None),
        P(("groups", "space", "rep"), None),
        P(None, ("groups", "space", "rep")),
        P(None, ("groups", "space", "rep"), "ckpt"),
    )
    return jax.shard_map(
        body,
        mesh=mesh,
        in_specs=placed,
        out_specs=(
            P(("groups", "space", "rep"), None, "ckpt"),
            P(("groups", "space", "rep"), None, "ckpt"),
        ),
        check_vma=False,
    )
```

time: 37.1 us -> 36.8 us (level)
  waiting for transfers between devices: 6.94 us -> 1.45 us
  starting transfers between devices: 9.4 us -> 14.1 us
  Pallas kernels: 19.7 us -> 20.3 us
    ppermute x3 -> x6, waiting for transfers between devices: 6.92 us -> 0.39 us  [the longest x4 0.38 us: body(): halo_b[n] = lax.ppermute(out, RING, outer)]
    ppermute x3 -> x6, starting transfers between devices: 7.25 us -> 12.1 us  [the longest x4 7.35 us: body(): halo_b[n] = lax.ppermute(out, RING, outer)]
    pallas_call x7 -> x10, Pallas kernels: 13.8 us -> 18.1 us  [call(): pl.pallas_call(kernel, name=name, out_shape=tuple((like(a) for a in held)...]
    pallas_call x2, Pallas kernels: 5.91 us -> 2.13 us  [body(): pl.pallas_call(functools.partial(edge_last, window), name='edge_last', ou...]
    ppermute x3, waiting for transfers between devices: 0.01 us -> 0.96 us  [body(): halo_a = lax.ppermute(out_a, RING, inner)]
  transfers between devices with their start and end apart: 7 -> 10, of which waited for: 3 -> 3; matrix products, arithmetic and copies ran while one was open for 0% -> 0% of each run, Pallas kernels for 46% -> 49%
where the time goes in v4:
time: 36.8 us; the launch traced here: 36.6 us
  Pallas kernels  20.3 us (55%)
  starting transfers between devices  14.1 us (38%)
  waiting for transfers between devices  1.45 us (4%)
  between operations  0.75 us (2%)
    pallas_call x10, Pallas kernels, call(): pl.pallas_call(kernel, name=name, out_shape=tuple((like(a) for a in held)...  18.1 us
    ppermute x4, starting transfers between devices, body(): halo_b[n] = lax.ppermute(out, RING, outer)  7.35 us
    ppermute x2, starting transfers between devices, body(): halo_b = [lax.ppermute(a, RING, outer) for a in out_b]  4.74 us
    pallas_call x2, Pallas kernels, body(): pl.pallas_call(functools.partial(edge_last, window), name='edge_last', ou...  2.13 us
    ppermute x1, starting transfers between devices, body(): lax.ppermute(states_late, 'ckpt', [((i + j) % pieces, i) for i in range(p...  1.49 us
    ppermute x3, waiting for transfers between devices, body(): halo_a = lax.ppermute(out_a, RING, inner)  0.96 us
  transfers between devices with their start and end apart: 10, of which 3 were waited for; matrix products, arithmetic and copies ran while one was open for 0% of the time, Pallas kernels for 49%

profile of v4, /device:TPU:0, one launch (start us, length us, event | category | flops | bytes accessed | tf_op | source)
XLA Modules:
  0.0 36.6 jit_solution(10736627653507363740)
XLA Ops:
  0.6 1.4 %head.1 = (bf16[4,96,256]{2,1,0:T(8,128)(2,1)S(1)}, bf16[4,96,128]{2,1,0:T(8,128)(2,1)S(1)}, bf16[4,96,384]{2,1,0:T(8,128)(2,1)S(1)}) custom-call(bf16[20,96,384]{2,1,0:T(8,128)(2,1)} %refs_2_.1, f32[20,96]{1,0:T(8,128)} %refs_4_.1), custom_call_target="tpu_custom_call" | custom-call | flops 1000 | bytes 1000 | tf_op jit(solution)/shard_map/head/pallas_call | solution.py:383
  2.0 0.5 %collective-permute-start = (bf16[4,96,384]{2,1,0:T(8,128)(2,1)S(1)}, bf16[4,96,384]{2,1,0:T(8,128)(2,1)S(1)}, u32[]{:S(2)}, u32[]{:S(2)}) collective-permute-start(bf16[4,96,384]{2,1,0:T(8,128)(2,1)S(1)} %get-tuple-element.77), channel_id=1, source_target_pairs={{0,1},{1,0},{4,5},{5,4},{8,9},{9,8},{12,13},{13,12},{2,3},{3,2},{6... | collective-permute-start | bytes 884744 | tf_op jit(solution)/shard_map/ppermute | solution.py:403
  2.6 4.7 %collective-permute-start.2 = (bf16[4,96,256]{2,1,0:T(8,128)(2,1)S(1)}, bf16[4,96,256]{2,1,0:T(8,128)(2,1)S(1)}, u32[]{:S(2)}, u32[]{:S(2)}) collective-permute-start(bf16[4,96,256]{2,1,0:T(8,128)(2,1)S(1)} %get-tuple-element.91), channel_id=1, source_target_pairs={{1,4},{5,8},{9,12},{13,0},{4,1},{8,5},{12,9},{0,13},{3,6},{7,10},{... | collective-permute-start | bytes 589832 | tf_op jit(solution)/shard_map/ppermute | solution.py:404
  7.3 0.0 collective-permute-start.3
  7.3 1.5 %collective-permute-start.1 = (f32[3,20,48]{2,1,0:T(8,128)}, f32[3,20,48]{2,1,0:T(8,128)S(1)}, u32[]{:S(2)}, u32[]{:S(2)}) collective-permute-start(f32[3,20,48]{2,1,0:T(8,128)} %refs_7_.1), channel_id=1, source_target_pairs={{2,0},{0,2},{3,1},{1,3},{6,4},{4,6},{7,5},{5,7},{10,8},{8,10},{11,... | collective-permute-start | bytes 34568 | tf_op jit(solution)/shard_map/ppermute | solution.py:406
  8.8 0.0 collective-permute-done.refs_0_
  8.8 2.6 %load_all.1 = (bf16[4,96,384]{2,1,0:T(8,128)(2,1)S(1)}, bf16[20,96,768]{2,1,0:T(8,128)(2,1)S(1)}, bf16[29,96,384]{2,1,0:T(8,128)(2,1)S(1)}, f32[20,96,384]{2,1,0...) custom-call(bf16[4,96,384]{2,1,0:T(8,128)(2,1)S(1)} %collective-perm, ...), custom_call_target="tpu_custom_call", output_to_operand_aliasing={{0}: (0, {})} | custom-call | flops 1000 | bytes 1000 | tf_op jit(solution)/shard_map/load_all/pallas_call | solution.py:383
  11.4 0.1 collective-permute-done.1.refs_6_
  11.5 0.6 %coefficients.1 = (bf16[29,96,384]{2,1,0:T(8,128)(2,1)S(1)}, f32[20,96,384]{2,1,0:T(8,128)S(1)}, f32[20,96,384]{2,1,0:T(8,128)S(1)}, f32[20,96,128]{2,1,0:T(8,12...) custom-call(bf16[29,96,384]{2,1,0:T(8,128)(2,1)S(1)} %get-tuple-elem, ...), custom_call_target="tpu_custom_call", output_to_operand_aliasing={{0}: (0, {}), {1}: (1, {}), {2}: (2, {}), {3}: (3, {}), {4}... | custom-call | flops 1000 | bytes 1000 | tf_op jit(solution)/shard_map/coefficients/pallas_call | solution.py:383
  12.1 0.0 collective-permute-done.2.refs_6_
  12.1 1.1 %first_edge.2 = (bf16[20,96,768]{2,1,0:T(8,128)(2,1)S(1)}, bf16[29,96,384]{2,1,0:T(8,128)(2,1)S(1)}, f32[20,96,384]{2,1,0:T(8,128)S(1)}, f32[20,96,384]{2,1,0:T(...) custom-call(bf16[20,96,768]{2,1,0:T(8,128)(2,1)S(1)} %get-tuple-elem, ...), custom_call_target="tpu_custom_call", output_to_operand_aliasing={{0}: (0, {}), {1}: (1, {}), {2}: (2, {}), {3}: (3, {}), {4}... | custom-call | flops 1000 | bytes 1000 | tf_op jit(solution)/shard_map/first_edge/pallas_call | solution.py:383
  13.1 3.2 %collective-permute-start.5 = (bf16[4,96,256]{2,1,0:T(8,128)(2,1)S(1)}, bf16[4,96,256]{2,1,0:T(8,128)(2,1)S(1)}, u32[]{:S(2)}, u32[]{:S(2)}) collective-permute-start(bf16[4,96,256]{2,1,0:T(8,128)(2,1)S(1)} %get-tuple-element.122), channel_id=1, source_target_pairs={{1,4},{5,8},{9,12},{13,0},{4,1},{8,5},{12,9},{0,13},{3,6},{7,10},{... | collective-permute-start | bytes 589832 | tf_op jit(solution)/shard_map/ppermute | solution.py:437
  16.4 0.0 collective-permute-start.4
  16.4 0.0 collective-permute-done.3.refs_6_
  16.4 1.0 %first_edge.3 = (bf16[20,96,768]{2,1,0:T(8,128)(2,1)S(1)}, bf16[29,96,384]{2,1,0:T(8,128)(2,1)S(1)}, f32[20,96,384]{2,1,0:T(8,128)S(1)}, f32[20,96,384]{2,1,0:T(...) custom-call(bf16[20,96,768]{2,1,0:T(8,128)(2,1)S(1)} %get-tuple-elem, ...), custom_call_target="tpu_custom_call", output_to_operand_aliasing={{0}: (0, {}), {1}: (1, {}), {2}: (2, {}), {3}: (3, {}), {4}... | custom-call | flops 4000000000 | bytes 1000 | tf_op jit(solution)/shard_map/first_edge/pallas_call | solution.py:383
  17.3 0.5 %collective-permute-start.6 = (bf16[4,96,128]{2,1,0:T(8,128)(2,1)S(1)}, bf16[4,96,128]{2,1,0:T(8,128)(2,1)S(1)}, u32[]{:S(2)}, u32[]{:S(2)}) collective-permute-start(bf16[4,96,128]{2,1,0:T(8,128)(2,1)S(1)} %get-tuple-element.128), channel_id=1, source_target_pairs={{1,4},{5,8},{9,12},{13,0},{4,1},{8,5},{12,9},{0,13},{3,6},{7,10},{... | collective-permute-start | bytes 294920 | tf_op jit(solution)/shard_map/ppermute | solution.py:437
  17.8 4.2 %first_interior.1 = (bf16[20,96,768]{2,1,0:T(8,128)(2,1)S(1)}, bf16[29,96,384]{2,1,0:T(8,128)(2,1)S(1)}, bf16[29,96,384]{2,1,0:T(8,128)(2,1)S(1)}, f32[20,96,384...) custom-call(bf16[20,96,768]{2,1,0:T(8,128)(2,1)S(1)} %get-tuple-elem, ...), custom_call_target="tpu_custom_call", output_to_operand_aliasing={{0}: (0, {}), {1}: (1, {}), {2}: (2, {}), {3}: (3, {}), {4}... | custom-call | flops 1000 | bytes 1000 | tf_op jit(solution)/shard_map/first_interior/pallas_call | solution.py:383
  22.0 0.0 collective-permute-done.4.refs_6_
  22.0 3.1 %main_rows.1 = (bf16[20,96,768]{2,1,0:T(8,128)(2,1)S(1)}, bf16[29,96,384]{2,1,0:T(8,128)(2,1)S(1)}, f32[20,96,384]{2,1,0:T(8,128)S(1)}, f32[20,96,384]{2,1,0:T(8...) custom-call(bf16[20,96,768]{2,1,0:T(8,128)(2,1)S(1)} %get-tuple-elem, ...), custom_call_target="tpu_custom_call", output_to_operand_aliasing={{0}: (0, {}), {1}: (1, {}), {2}: (2, {}), {3}: (3, {}), {4}... | custom-call | flops 1000 | bytes 1000 | tf_op jit(solution)/shard_map/main_rows/pallas_call | solution.py:383
  25.1 0.0 collective-permute-done.5.refs_4_
  25.1 0.3 edge_rows.2
  25.4 3.3 %collective-permute-start.8 = (bf16[4,96,256]{2,1,0:T(8,128)(2,1)S(1)}, bf16[4,96,256]{2,1,0:T(8,128)(2,1)S(1)}, u32[]{:S(2)}, u32[]{:S(2)}) collective-permute-start(bf16[4,96,256]{2,1,0:T(8,128)(2,1)S(1)} %get-tuple-element.139), channel_id=1, source_target_pairs={{1,4},{5,8},{9,12},{13,0},{4,1},{8,5},{12,9},{0,13},{3,6},{7,10},{... | collective-permute-start | bytes 589832 | tf_op jit(solution)/shard_map/ppermute | solution.py:459
  28.7 0.0 collective-permute-start.7
  28.7 0.0 collective-permute-done.6.refs_4_
  28.7 0.3 edge_rows.3
  28.9 0.4 collective-permute-start.9
  29.3 1.0 %collective-permute-done.7.refs_5_ = bf16[4,96,384]{2,1,0:T(8,128)(2,1)S(1)} collective-permute-done((bf16[4,96,384]{2,1,0:T(8,128)(2,1)S(1)}, bf16[4,96,384]{2,1,0:T(8,128)(2,1)S(1)}, u32[]{:S(2)}, u32[]{:S(2)}) %collective-permute-start.7) | collective-permute-done | bytes 294944 | tf_op jit(solution)/shard_map/ppermute | solution.py:452
  30.2 3.8 %main_last.1 = (bf16[20,96,768]{2,1,0:T(8,128)(2,1)S(1)}, bf16[29,96,384]{2,1,0:T(8,128)(2,1)S(1)}, f32[20,96,384]{2,1,0:T(8,128)S(1)}, f32[20,96,384]{2,1,0:T(8...) custom-call(bf16[20,96,768]{2,1,0:T(8,128)(2,1)S(1)} %get-tuple-elem, ...), custom_call_target="tpu_custom_call", output_to_operand_aliasing={{0}: (0, {}), {1}: (1, {}), {2}: (2, {}), {3}: (3, {}), {4}... | custom-call | flops 1000 | bytes 1000 | tf_op jit(solution)/shard_map/main_last/pallas_call | solution.py:383
  34.1 0.4 %collective-permute-done.8.refs_3_ = bf16[4,96,256]{2,1,0:T(8,128)(2,1)S(1)} collective-permute-done((bf16[4,96,256]{2,1,0:T(8,128)(2,1)S(1)}, bf16[4,96,256]{2,1,0:T(8,128)(2,1)S(1)}, u32[]{:S(2)}, u32[]{:S(2)}) %collective-permute-start.8) | collective-permute-done | bytes 196640 | tf_op jit(solution)/shard_map/ppermute | solution.py:459
  34.4 1.1 %edge_last.2 = (bf16[384,384]{1,0:T(8,128)(2,1)S(1)}, f32[20,96,384]{2,1,0:T(8,128)S(1)}, f32[20,96,384]{2,1,0:T(8,128)S(1)}, bf16[4,96,256]{2,1,0:T(8,128)(2,1)...) custom-call(bf16[384,384]{1,0:T(8,128)(2,1)S(1)} %get-tuple-element., ...), custom_call_target="tpu_custom_call", output_to_operand_aliasing={{0}: (0, {}), {1}: (1, {}), {2}: (2, {}), {3}: (3, {}), {4}... | custom-call | flops 1000 | bytes 1000 | tf_op jit(solution)/shard_map/edge_last/pallas_call | solution.py:467
  35.6 0.0 collective-permute-done.9.refs_3_
  35.6 1.0 %edge_last.3 = (bf16[384,384]{1,0:T(8,128)(2,1)S(1)}, f32[20,96,384]{2,1,0:T(8,128)S(1)}, f32[20,96,384]{2,1,0:T(8,128)S(1)}, bf16[4,96,128]{2,1,0:T(8,128)(2,1)...) custom-call(bf16[384,384]{1,0:T(8,128)(2,1)S(1)} %get-tuple-element., ...), custom_call_target="tpu_custom_call", output_to_operand_aliasing={{0}: (0, {}), {1}: (1, {}), {2}: (2, {}), {3}: (3, {}), {4}... | custom-call | flops 1000 | bytes 1000 | tf_op jit(solution)/shard_map/edge_last/pallas_call | solution.py:467
Async XLA Ops:
  2.0 6.8 %collective-permute-start = (bf16[4,96,384]{2,1,0:T(8,128)(2,1)S(1)}, bf16[4,96,384]{2,1,0:T(8,128)(2,1)S(1)}, u32[]{:S(2)}, u32[]{:S(2)}) collective-permute-start(bf16[4,96,384]{2,1,0:T(8,128)(2,1)S(1)} %get-tuple-element.77), channel_id=1, source_target_pairs={{0,1},{1,0},{4,5},{5,4},{8,9},{9,8},{12,13},{13,12},{2,3},{3,2},{6... | collective-permute-start | bytes 884744 | tf_op jit(solution)/shard_map/ppermute | solution.py:403
  2.6 9.5 %collective-permute-start.2 = (bf16[4,96,256]{2,1,0:T(8,128)(2,1)S(1)}, bf16[4,96,256]{2,1,0:T(8,128)(2,1)S(1)}, u32[]{:S(2)}, u32[]{:S(2)}) collective-permute-start(bf16[4,96,256]{2,1,0:T(8,128)(2,1)S(1)} %get-tuple-element.91), channel_id=1, source_target_pairs={{1,4},{5,8},{9,12},{13,0},{4,1},{8,5},{12,9},{0,13},{3,6},{7,10},{... | collective-permute-start | bytes 589832 | tf_op jit(solution)/shard_map/ppermute | solution.py:404
  7.3 9.1 %collective-permute-start.3 = (bf16[4,96,128]{2,1,0:T(8,128)(2,1)S(1)}, bf16[4,96,128]{2,1,0:T(8,128)(2,1)S(1)}, u32[]{:S(2)}, u32[]{:S(2)}) collective-permute-start(bf16[4,96,128]{2,1,0:T(8,128)(2,1)S(1)} %get-tuple-element.100), channel_id=1, source_target_pairs={{1,4},{5,8},{9,12},{13,0},{4,1},{8,5},{12,9},{0,13},{3,6},{7,10},{... | collective-permute-start | bytes 294920 | tf_op jit(solution)/shard_map/ppermute | solution.py:404
  7.3 4.2 %collective-permute-start.1 = (f32[3,20,48]{2,1,0:T(8,128)}, f32[3,20,48]{2,1,0:T(8,128)S(1)}, u32[]{:S(2)}, u32[]{:S(2)}) collective-permute-start(f32[3,20,48]{2,1,0:T(8,128)} %refs_7_.1), channel_id=1, source_target_pairs={{2,0},{0,2},{3,1},{1,3},{6,4},{4,6},{7,5},{5,7},{10,8},{8,10},{11,... | collective-permute-start | bytes 34568 | tf_op jit(solution)/shard_map/ppermute | solution.py:406
  13.1 11.9 %collective-permute-start.5 = (bf16[4,96,256]{2,1,0:T(8,128)(2,1)S(1)}, bf16[4,96,256]{2,1,0:T(8,128)(2,1)S(1)}, u32[]{:S(2)}, u32[]{:S(2)}) collective-permute-start(bf16[4,96,256]{2,1,0:T(8,128)(2,1)S(1)} %get-tuple-element.122), channel_id=1, source_target_pairs={{1,4},{5,8},{9,12},{13,0},{4,1},{8,5},{12,9},{0,13},{3,6},{7,10},{... | collective-permute-start | bytes 589832 | tf_op jit(solution)/shard_map/ppermute | solution.py:437
  16.4 5.6 %collective-permute-start.4 = (bf16[4,96,384]{2,1,0:T(8,128)(2,1)S(1)}, bf16[4,96,384]{2,1,0:T(8,128)(2,1)S(1)}, u32[]{:S(2)}, u32[]{:S(2)}) collective-permute-start(bf16[4,96,384]{2,1,0:T(8,128)(2,1)S(1)} %get-tuple-element.117), channel_id=1, source_target_pairs={{0,1},{1,0},{4,5},{5,4},{8,9},{9,8},{12,13},{13,12},{2,3},{3,2},{6... | collective-permute-start | bytes 884744 | tf_op jit(solution)/shard_map/ppermute | solution.py:430
  17.3 11.3 %collective-permute-start.6 = (bf16[4,96,128]{2,1,0:T(8,128)(2,1)S(1)}, bf16[4,96,128]{2,1,0:T(8,128)(2,1)S(1)}, u32[]{:S(2)}, u32[]{:S(2)}) collective-permute-start(bf16[4,96,128]{2,1,0:T(8,128)(2,1)S(1)} %get-tuple-element.128), channel_id=1, source_target_pairs={{1,4},{5,8},{9,12},{13,0},{4,1},{8,5},{12,9},{0,13},{3,6},{7,10},{... | collective-permute-start | bytes 294920 | tf_op jit(solution)/shard_map/ppermute | solution.py:437
  25.4 9.1 %collective-permute-start.8 = (bf16[4,96,256]{2,1,0:T(8,128)(2,1)S(1)}, bf16[4,96,256]{2,1,0:T(8,128)(2,1)S(1)}, u32[]{:S(2)}, u32[]{:S(2)}) collective-permute-start(bf16[4,96,256]{2,1,0:T(8,128)(2,1)S(1)} %get-tuple-element.139), channel_id=1, source_target_pairs={{1,4},{5,8},{9,12},{13,0},{4,1},{8,5},{12,9},{0,13},{3,6},{7,10},{... | collective-permute-start | bytes 589832 | tf_op jit(solution)/shard_map/ppermute | solution.py:459
  28.7 1.6 %collective-permute-start.7 = (bf16[4,96,384]{2,1,0:T(8,128)(2,1)S(1)}, bf16[4,96,384]{2,1,0:T(8,128)(2,1)S(1)}, u32[]{:S(2)}, u32[]{:S(2)}) collective-permute-start(bf16[4,96,384]{2,1,0:T(8,128)(2,1)S(1)} %get-tuple-element.136), channel_id=1, source_target_pairs={{0,1},{1,0},{4,5},{5,4},{8,9},{9,8},{12,13},{13,12},{2,3},{3,2},{6... | collective-permute-start | bytes 884744 | tf_op jit(solution)/shard_map/ppermute | solution.py:452
  28.9 6.6 %collective-permute-start.9 = (bf16[4,96,128]{2,1,0:T(8,128)(2,1)S(1)}, bf16[4,96,128]{2,1,0:T(8,128)(2,1)S(1)}, u32[]{:S(2)}, u32[]{:S(2)}) collective-permute-start(bf16[4,96,128]{2,1,0:T(8,128)(2,1)S(1)} %get-tuple-element.145), channel_id=1, source_target_pairs={{1,4},{5,8},{9,12},{13,0},{4,1},{8,5},{12,9},{0,13},{3,6},{7,10},{... | collective-permute-start | bytes 294920 | tf_op jit(solution)/shard_map/ppermute | solution.py:459

commit v5 on v4

--- a/solution.py
+++ b/solution.py
@@ -62,7 +62,7 @@
 
 
 def head(vel0, inv_mass, *refs):
-    *out_b, out_a, low, high, mass, sem = refs
+    out_b, out_a, low, high, mass, sem = refs
     rows, _, lanes = vel0.shape
     end(
         begin(
@@ -78,20 +78,18 @@
     for j in range(HB):
         p = spread(upright, j, lanes) * (0.5 * low[j].astype(jnp.float32))
         q = spread(upright, rows - HB + j, lanes) * (0.5 * high[j].astype(jnp.float32))
-        b = jnp.where(rep == 0, p, q).astype(jnp.bfloat16)
-        for ref, (at, size) in zip(out_b, windows_of(lanes)):
-            ref[j] = b[:, at : at + size]
+        out_b[j] = jnp.where(rep == 0, p, q).astype(jnp.bfloat16)
         out_a[j] = jnp.where(rep == 0, q, p).astype(jnp.bfloat16)
 
 
 def load_all(total, blocks_in, vel0_in, disp0_in, inv_mass, stiff_in, contact_in, mine, cols_in, *refs):
-    halo, blocks, now, disp, vel, mass_b, bent, turned, place_out = refs[:9]
-    vel0, edges, cols, place, mass, stiff, contact, shard, sem = refs[9:]
+    halo, blocks, disp0, now, disp, vel, mass_b, bent, turned, place_out = refs[:10]
+    vel0, cols, place, mass, stiff, contact, shard, sem = refs[10:]
     rows, _, lanes = vel0.shape
     rep = lax.axis_index("rep")
     a_start = (rows - HB) * (1 - rep)
     b_start = (rows - HB) * rep
-    sides = (pl.ds(a_start, HB), pl.ds(b_start, HB))
+    sides = (pl.ds(a_start, HB), pl.ds(b_start, HB), pl.ds(HB, rows - 2 * HB))
     get_cols = begin([pltpu.make_async_copy(cols_in, cols, sem.at[0])])
     small = begin(
         [
@@ -102,16 +100,15 @@
         ]
     )
     get_vel = begin([pltpu.make_async_copy(vel0_in, vel0, sem.at[5])])
-    get_rest = begin(
-        [
-            pltpu.make_async_copy(blocks_in.at[at], blocks.at[at], sem.at[6 + n])
-            for n, at in enumerate(sides)
-        ]
-        + [
-            pltpu.make_async_copy(disp0_in.at[at], edges.at[n], sem.at[8 + n])
-            for n, at in enumerate(sides)
-        ]
-    )
+    get_rest = [
+        begin(
+            [
+                pltpu.make_async_copy(blocks_in.at[at], blocks.at[at], sem.at[6 + 2 * n]),
+                pltpu.make_async_copy(disp0_in.at[at], disp0.at[at], sem.at[7 + 2 * n]),
+            ]
+        )
+        for n, at in enumerate(sides)
+    ]
     now[rows + 2 * HB] = jnp.zeros(now.shape[1:], now.dtype)
     side = (rows + HB) * (1 - rep)
     for j in range(HB):
@@ -140,15 +137,17 @@
         vel[r] = v
         now[r + HB] = (tiled(mass_b[r], lanes) * (0.5 * v)).astype(jnp.bfloat16)
     end(get_place)
-    end(get_rest)
-    for j in range(HB):
-        disp[b_start + j] = edges[1, j].astype(jnp.float32)
+    end(get_rest[0])
 
     def one(i):
         r = a_start + i
-        disp[r] = edges[0, i].astype(jnp.float32) - product(blocks, now, place, r)
+        disp[r] = disp0[r].astype(jnp.float32) - product(blocks, now, place, r)
 
     each(HB, one)
+    end(get_rest[1])
+    for j in range(HB):
+        disp[b_start + j] = disp0[b_start + j].astype(jnp.float32)
+    end(get_rest[2])
 
 
 def finish_row(r, image, later, disp, vel, mass_b, window=None):
@@ -163,10 +162,13 @@
         return p
 
 
-def joint(step, r, now, coeff, window=None):
-    at = slice(None) if window is None else pl.ds(*window)
-    own = now[r + HB, :, at].astype(jnp.float32)
-    return tiled(coeff[step, r], own.shape[1]) * own
+def joint(r, now, coeff):
+    return tiled(coeff[r], now.shape[2]) * now[r + HB].astype(jnp.float32)
+
+
+def spread_rows(matrix, out):
+    for r in range(out.shape[0]):
+        out[r] = spread(matrix, r, 128)
 
 
 def coefficients(pieces, *refs):
@@ -181,83 +183,48 @@
             source = lax.rem(me + 1 + j, pieces)
             turned[s, pl.ds(pl.multiple_of(source * part, 8), part), :] = piece[s].T
         turned[s] = bent[s] * turned[s] * turned[s]
-    full = turned[last]
-    for r in range(rows):
-        coeff[last, r] = spread(full, r, 128)
+    spread_rows(turned[last], coeff)
     later[rows + 2 * HB] = jnp.zeros(later.shape[1:], later.dtype)
     start = (rows - HB) * (1 - lax.axis_index("rep"))
 
     def one(i):
         r = start + i
-        out_a[i] = finish_row(r, joint(last, r, now, coeff), later, disp, vel, mass_b)
+        out_a[i] = finish_row(r, joint(r, now, coeff), later, disp, vel, mass_b)
 
     each(HB, one)
 
 
-def first_edge(window, *refs):
-    place, blocks, now, disp, vel, mass_b, coeff, halo, later, out = refs[-10:]
-    rows = disp.shape[0]
-    rep = lax.axis_index("rep")
-    at = pl.ds(*window)
-    for j in range(HB):
-        now[(rows + HB) * rep + j, :, at] = halo[j]
-    start = (rows - HB) * rep
+def first_interior(*refs):
+    place, blocks, disp0, now, later, disp, vel, mass_b, coeff, dense = refs[-10:]
+    rows, width, _ = disp.shape
+    slots = blocks.shape[2] // width
+    side = lax.axis_index("rep")
+    shape = (width, HB * width)
+    ahead = lax.broadcasted_iota(jnp.int32, shape, 1) - lax.broadcasted_iota(jnp.int32, shape, 0)
+    for i in range(HB):
+        r = (rows - HB) * side + i
+        chosen = []
+        for k in range(slots):
+            j = place[k, r] - (rows + HB) * side
+            inside = jnp.logical_and(j >= 0, j < HB)
+            at = jnp.where(inside, j * width, -width)
+            chosen.append(jnp.where(ahead == at, 1.0, 0.0).astype(jnp.bfloat16))
+        picked = jnp.dot(
+            blocks[r], jnp.concatenate(chosen, axis=0), preferred_element_type=jnp.float32
+        )
+        dense[pl.ds(i * width, width), :] = picked.astype(jnp.bfloat16)
 
     def one(i):
-        r = start + i
-        image = product(blocks, now, place, r, window)
-        image = image + joint(WINDOW - 1, r, now, coeff, window)
-        out[i] = finish_row(r, image, later, disp, vel, mass_b, window)
-
-    each(HB, one)
-
-
-def first_interior(*refs):
-    blocks_in, disp0_in, place = refs[8:11]
-    blocks, now, later, disp, vel, mass_b, turned, coeff, dense, wide, disp0, sem = refs[11:]
-    rows, width, lanes = disp.shape
-    slots = blocks.shape[2] // width
-    loads = []
-    for g in range(1, rows // HB - 1):
-        at = pl.ds(g * HB, HB)
-        loads.append(
-            begin(
-                [
-                    pltpu.make_async_copy(blocks_in.at[at], blocks.at[at], sem.at[0, g]),
-                    pltpu.make_async_copy(disp0_in.at[at], disp0.at[at], sem.at[1, g]),
-                ]
-            )
-        )
-    for s in range(WINDOW - 1):
-        full = turned[s]
-        for r in range(rows):
-            coeff[s, r] = spread(full, r, 128)
-    rep = lax.axis_index("rep")
-    wide[...] = jnp.zeros_like(wide)
-    for i in range(HB):
-        r = (rows - HB) * rep + i
-        block = blocks[r].astype(jnp.float32)
-        for k in range(slots):
-            j = place[k, r] - (rows + HB) * rep
-            inside = jnp.logical_and(j >= 0, j < HB)
-
-            @pl.when(inside)
-            def _():
-                at = pl.ds(i * width, width)
-                wide[j, at, pl.ds(0, width)] += block[:, k * width : (k + 1) * width]
-
-    dense[...] = jnp.concatenate([wide[j, :, :width] for j in range(HB)], axis=1).astype(
-        jnp.bfloat16
-    )
-    for g, load in enumerate(loads, 1):
-        end(load)
-        for r in range(g * HB, (g + 1) * HB):
-            disp[r] = disp0[r].astype(jnp.float32)
-            image = product(blocks, now, place, r) + joint(WINDOW - 1, r, now, coeff)
-            finish_row(r, image, later, disp, vel, mass_b)
-
-
-def near_part(step, i, blocks, now, place, coeff, disp):
+        r = HB + i
+        disp[r] = disp0[r].astype(jnp.float32)
+        image = product(blocks, now, place, r) + joint(r, now, coeff)
+        finish_row(r, image, later, disp, vel, mass_b)
+
+    each(rows - 2 * HB, one)
+    each(HB, lambda i: near_part(i, blocks, now, place, coeff, disp))
+
+
+def near_part(i, blocks, now, place, coeff, disp):
     rows = disp.shape[0]
     rep = lax.axis_index("rep")
     r = (rows - HB) * rep + i
@@ -271,12 +238,13 @@
     image = jnp.dot(
         blocks[r], jnp.concatenate(picked, axis=0), preferred_element_type=jnp.float32
     )
-    disp[r] = disp[r] - (image + joint(step, r, now, coeff))
+    disp[r] = disp[r] - (image + joint(r, now, coeff))
 
 
 def main_rows(step, *refs):
-    place, blocks, now, disp, vel, mass_b, coeff, halo, later, out = refs[-10:]
+    place, blocks, now, disp, vel, mass_b, turned, coeff, halo, later, out = refs[-11:]
     rows = disp.shape[0]
+    spread_rows(turned[step], coeff)
     side = 1 - lax.axis_index("rep")
     for j in range(HB):
         now[(rows + HB) * side + j] = halo[j]
@@ -284,26 +252,27 @@
 
     def one(i):
         r = start + i
-        image = product(blocks, now, place, r) + joint(step, r, now, coeff)
+        image = product(blocks, now, place, r) + joint(r, now, coeff)
         finish_row(r, image, later, disp, vel, mass_b)
 
     each(rows - HB, one)
     for j in range(HB):
         out[j] = later[(rows - HB) * side + HB + j]
-    each(HB, lambda i: near_part(step, i, blocks, now, place, coeff, disp))
-
-
-def far_part(dense, halo):
+    each(HB, lambda i: near_part(i, blocks, now, place, coeff, disp))
+
+
+def far_part(dense, halo, window):
     rows, width, lanes = halo.shape
-    return jnp.dot(
-        dense[...], halo[...].reshape(rows * width, lanes), preferred_element_type=jnp.float32
-    )
+    start, size = window
+    start = start if lanes > size else 0
+    seen = halo[:, :, start : start + size].reshape(rows * width, size)
+    return jnp.dot(dense[...], seen, preferred_element_type=jnp.float32)
 
 
 def edge_rows(window, *refs):
     dense, disp, vel, mass_b, halo, later, out = refs[-7:]
     rows, width, _ = disp.shape
-    image = far_part(dense, halo)
+    image = far_part(dense, halo, window)
     start = (rows - HB) * lax.axis_index("rep")
     for i in range(HB):
         part = image[i * width : (i + 1) * width]
@@ -319,8 +288,9 @@
 
 
 def main_last(*refs):
-    place, blocks, now, disp, vel, coeff, halo, disp_out, vel_out, sem = refs[-10:]
+    place, blocks, now, disp, vel, turned, coeff, halo, disp_out, vel_out, sem = refs[-11:]
     rows = disp.shape[0]
+    spread_rows(turned[0], coeff)
     side = 1 - lax.axis_index("rep")
     for j in range(HB):
         now[(rows + HB) * side + j] = halo[j]
@@ -330,20 +300,20 @@
 
         def one(i):
             r = start + i
-            image = product(blocks, now, place, r) + joint(0, r, now, coeff)
+            image = product(blocks, now, place, r) + joint(r, now, coeff)
             finish_row(r, image, None, disp, vel, None)
 
         each(HB, one)
         copies = row_copies(disp, vel, disp_out, vel_out, sem, start, HB, g, (0, disp.shape[2]))
         sent += begin(copies)
-    each(HB, lambda i: near_part(0, i, blocks, now, place, coeff, disp))
+    each(HB, lambda i: near_part(i, blocks, now, place, coeff, disp))
     end(sent)
 
 
 def edge_last(window, *refs):
     dense, disp, vel, halo, disp_out, vel_out, sem = refs[-7:]
     rows, width, _ = disp.shape
-    image = far_part(dense, halo)
+    image = far_part(dense, halo, window)
     start = (rows - HB) * lax.axis_index("rep")
     sent = []
     for i in range(HB):
@@ -395,72 +365,68 @@
     windows = windows_of(lanes)
     edges_t = [pltpu.VMEM((HB, width, size), bf16) for _, size in windows]
 
-    *out_b, out_a = call(
-        head, "head", [], [adj_vel, inv_mass], [hbm] * 2,
-        edges_t + [edge_t], [vm] * (len(windows) + 1), [edge_t, edge_t, table, dma((3,))],
+    out_b, out_a = call(
+        head, "head", [], [adj_vel, inv_mass], [hbm] * 2, [edge_t] * 2, [vm] * 2,
+        [edge_t, edge_t, table, dma((3,))],
     )
     states_late, out_a = lax.optimization_barrier((states, out_a))
     halo_a = lax.ppermute(out_a, RING, inner)
-    halo_b = [lax.ppermute(a, RING, outer) for a in out_b]
+    whole_b = lax.ppermute(out_b, RING, outer)
+    halo_b = [whole_b] * len(windows)
     others = [
         lax.ppermute(states_late, "ckpt", [((i + j) % pieces, i) for i in range(pieces)])
         for j in range(1, pieces)
     ]
 
-    _, blocks, now, disp, vel, mass_b, bent, turned, place = call(
+    _, blocks, disp0, now, disp, vel, mass_b, bent, turned, place = call(
         lambda *refs: load_all(total, *refs[1:9], refs[0], *refs[10:]), "load_all",
         [halo_a],
         [tangent_blocks, adj_vel, adj_disp, inv_mass, joint_stiff, contact, mine, cols], [hbm] * 8,
         [
-            like(tangent_blocks), ext, full, full, pltpu.VMEM((rows, width, 128), f32),
-            upright, upright, like(cols),
+            like(tangent_blocks), like(adj_disp), ext, full, full,
+            pltpu.VMEM((rows, width, 128), f32), upright, upright, like(cols),
         ],
-        [vm] * 8,
+        [vm] * 9,
         [
-            like(adj_vel), pltpu.VMEM((2, HB, width, lanes), bf16), like(cols),
-            pltpu.SMEM(cols.shape, jnp.int32), table, table,
-            pltpu.VMEM(contact.shape, jnp.int32), pltpu.VMEM(states.shape, f32), dma((10,)),
+            like(adj_vel), like(cols), pltpu.SMEM(cols.shape, jnp.int32), table, table,
+            pltpu.VMEM(contact.shape, jnp.int32), pltpu.VMEM(states.shape, f32), dma((12,)),
         ],
     )
     now, disp, vel, mass_b, _, turned, *_, later, coeff, out_a = call(
         functools.partial(coefficients, pieces), "coefficients",
         [now, disp, vel, mass_b, bent, turned] + others, [], [],
-        [ext, pltpu.VMEM((WINDOW, rows, width, 128), f32), edge_t], [vm] * 3,
+        [ext, like(mass_b), edge_t], [vm] * 3,
     )
     halo_a = lax.ppermute(out_a, RING, inner)
-    for n, window in enumerate(windows):
-        blocks, now, disp, vel, mass_b, coeff, _, later, out = call(
-            functools.partial(first_edge, window), "first_edge",
-            [blocks, now, disp, vel, mass_b, coeff, halo_b[n], later], [place], [sm],
-            [edges_t[n]], [vm], (), heavy if n else light,
-        )
-        halo_b[n] = lax.ppermute(out, RING, outer)
-    blocks, now, later, disp, vel, mass_b, _, coeff, dense = call(
+    blocks, _, now, later, disp, vel, mass_b, coeff, dense = call(
         first_interior, "first_interior",
-        [blocks, now, later, disp, vel, mass_b, turned, coeff],
-        [tangent_blocks, adj_disp, place], [hbm, hbm, sm],
+        [blocks, disp0, now, later, disp, vel, mass_b, coeff], [place], [sm],
         [pltpu.VMEM((HB * width, HB * width), bf16)], [vm],
-        [pltpu.VMEM((HB, HB * width, 128), f32), like(adj_disp), dma((2, rows // HB))],
-    )
-    for step in range(WINDOW - 2, 0, -1):
-        blocks, later, disp, vel, mass_b, coeff, _, now, out_a = call(
-            functools.partial(main_rows, step), "main_rows",
-            [blocks, later, disp, vel, mass_b, coeff, halo_a, now], [place], [sm],
-            [edge_t], [vm],
-        )
-        now, later = later, now
-        halo_a = lax.ppermute(out_a, RING, inner)
+    )
+    for step in range(WINDOW - 1, 0, -1):
+        if step < WINDOW - 1:
+            blocks, later, disp, vel, mass_b, turned, coeff, _, now, out_a = call(
+                functools.partial(main_rows, step), "main_rows",
+                [blocks, later, disp, vel, mass_b, turned, coeff, halo_a, now], [place], [sm],
+                [edge_t], [vm],
+            )
+            now, later = later, now
+            halo_a = lax.ppermute(out_a, RING, inner)
+        sent = []
         for n, window in enumerate(windows):
-            dense, disp, vel, mass_b, _, later, out = call(
+            dense, disp, vel, mass_b, halo, later, out = call(
                 functools.partial(edge_rows, window), "edge_rows",
                 [dense, disp, vel, mass_b, halo_b[n], later], [], [], [edges_t[n]], [vm],
                 (), heavy if n else light,
             )
-            halo_b[n] = lax.ppermute(out, RING, outer)
+            sent.append(lax.ppermute(out, RING, outer))
+            if step == WINDOW - 1:
+                halo_b = [halo] * len(windows)
+        halo_b = sent
 
     shape = jax.ShapeDtypeStruct((rows, width, lanes), f32)
-    *_, disp, vel, _, _, disp_out, vel_out = call(
-        main_last, "main_last", [blocks, later, disp, vel, coeff, halo_a], [place], [sm],
+    *_, disp, vel, _, _, _, disp_out, vel_out = call(
+        main_last, "main_last", [blocks, later, disp, vel, turned, coeff, halo_a], [place], [sm],
         [shape] * 2, [hbm] * 2, [dma((2, rows // HB - 1))],
     )
     for n, window in enumerate(windows):

time: 36.8 us -> 34.5 us (0.938)
  Pallas kernels: 20.3 us -> 18 us
    pallas_call x10, Pallas kernels: 18.1 us -> 15.9 us  [call(): pl.pallas_call(kernel, name=name, out_shape=tuple((like(a) for a in held)...]
    ppermute x6 -> x5, waiting for transfers between devices: 0.39 us -> 1.66 us  [the longest x4 1.66 us: body(): sent.append(lax.ppermute(out, RING, outer))]
    ppermute x3, waiting for transfers between devices: 0.96 us -> 0.01 us  [body(): halo_a = lax.ppermute(out_a, RING, inner)]
    ppermute x6 -> x5, starting transfers between devices: 12.1 us -> 11.8 us  [the longest x4 7.1 us: body(): sent.append(lax.ppermute(out, RING, outer))]
  transfers between devices with their start and end apart: 10 -> 9, of which waited for: 3 -> 3; matrix products, arithmetic and copies ran while one was open for 0% -> 0% of each run, Pallas kernels for 49% -> 45%
where the time goes in v5:
time: 34.5 us; the launch traced here: 34.3 us
  Pallas kernels  18 us (52%)
  starting transfers between devices  13.8 us (40%)
  waiting for transfers between devices  1.67 us (5%)
  between operations  0.74 us (2%)
    pallas_call x10, Pallas kernels, call(): pl.pallas_call(kernel, name=name, out_shape=tuple((like(a) for a in held)...  15.9 us
    ppermute x4, starting transfers between devices, body(): sent.append(lax.ppermute(out, RING, outer))  7.1 us
    ppermute x1, starting transfers between devices, body(): whole_b = lax.ppermute(out_b, RING, outer)  4.71 us
    pallas_call x2, Pallas kernels, body(): pl.pallas_call(functools.partial(edge_last, window), name='edge_last', ou...  2.13 us
    ppermute x4, waiting for transfers between devices, body(): sent.append(lax.ppermute(out, RING, outer))  1.66 us
    ppermute x1, starting transfers between devices, body(): lax.ppermute(states_late, 'ckpt', [((i + j) % pieces, i) for i in range(p...  1.49 us
  transfers between devices with their start and end apart: 9, of which 3 were waited for; matrix products, arithmetic and copies ran while one was open for 0% of the time, Pallas kernels for 45%

profile of v5, /device:TPU:0, one launch (start us, length us, event | category | flops | bytes accessed | tf_op | source)
XLA Modules:
  0.0 34.3 jit_solution(4162992057335324695)
XLA Ops:
  0.6 1.4 %head.1 = (bf16[4,96,384]{2,1,0:T(8,128)(2,1)S(1)}, bf16[4,96,384]{2,1,0:T(8,128)(2,1)S(1)}) custom-call(bf16[20,96,384]{2,1,0:T(8,128)(2,1)} %refs_2_.1, f32[20,96]{1,0:T(8,128)} %refs_4_.1), custom_call_target="tpu_custom_call" | custom-call | flops 1000 | bytes 1000 | tf_op jit(solution)/shard_map/head/pallas_call | solution.py:353
  2.0 0.5 %collective-permute-start = (bf16[4,96,384]{2,1,0:T(8,128)(2,1)S(1)}, bf16[4,96,384]{2,1,0:T(8,128)(2,1)S(1)}, u32[]{:S(2)}, u32[]{:S(2)}) collective-permute-start(bf16[4,96,384]{2,1,0:T(8,128)(2,1)S(1)} %get-tuple-element.75), channel_id=1, source_target_pairs={{0,1},{1,0},{4,5},{5,4},{8,9},{9,8},{12,13},{13,12},{2,3},{3,2},{6... | collective-permute-start | bytes 884744 | tf_op jit(solution)/shard_map/ppermute | solution.py:373
  2.6 4.7 %collective-permute-start.2 = (bf16[4,96,384]{2,1,0:T(8,128)(2,1)S(1)}, bf16[4,96,384]{2,1,0:T(8,128)(2,1)S(1)}, u32[]{:S(2)}, u32[]{:S(2)}) collective-permute-start(bf16[4,96,384]{2,1,0:T(8,128)(2,1)S(1)} %get-tuple-element.96), channel_id=1, source_target_pairs={{1,4},{5,8},{9,12},{13,0},{4,1},{8,5},{12,9},{0,13},{3,6},{7,10},{... | collective-permute-start | bytes 884744 | tf_op jit(solution)/shard_map/ppermute | solution.py:374
  7.3 1.5 %collective-permute-start.1 = (f32[3,20,48]{2,1,0:T(8,128)}, f32[3,20,48]{2,1,0:T(8,128)S(1)}, u32[]{:S(2)}, u32[]{:S(2)}) collective-permute-start(f32[3,20,48]{2,1,0:T(8,128)} %refs_7_.1), channel_id=1, source_target_pairs={{2,0},{0,2},{3,1},{1,3},{6,4},{4,6},{7,5},{5,7},{10,8},{8,10},{11,... | collective-permute-start | bytes 34568 | tf_op jit(solution)/shard_map/ppermute | solution.py:377
  8.8 0.0 collective-permute-done.refs_0_
  8.8 2.9 %load_all.1 = (bf16[4,96,384]{2,1,0:T(8,128)(2,1)S(1)}, bf16[20,96,768]{2,1,0:T(8,128)(2,1)S(1)}, bf16[20,96,384]{2,1,0:T(8,128)(2,1)S(1)}, bf16[29,96,384]{2,1,...) custom-call(bf16[4,96,384]{2,1,0:T(8,128)(2,1)S(1)} %collective-perm, ...), custom_call_target="tpu_custom_call", output_to_operand_aliasing={{0}: (0, {})} | custom-call | flops 1000 | bytes 1000 | tf_op jit(solution)/shard_map/load_all/pallas_call | solution.py:353
  11.6 0.0 collective-permute-done.1.refs_6_
  11.6 0.6 %coefficients.1 = (bf16[29,96,384]{2,1,0:T(8,128)(2,1)S(1)}, f32[20,96,384]{2,1,0:T(8,128)S(1)}, f32[20,96,384]{2,1,0:T(8,128)S(1)}, f32[20,96,128]{2,1,0:T(8,12...) custom-call(bf16[29,96,384]{2,1,0:T(8,128)(2,1)S(1)} %get-tuple-elem, ...), custom_call_target="tpu_custom_call", output_to_operand_aliasing={{0}: (0, {}), {1}: (1, {}), {2}: (2, {}), {3}: (3, {}), {4}... | custom-call | flops 1000 | bytes 1000 | tf_op jit(solution)/shard_map/coefficients/pallas_call | solution.py:353
  12.2 2.9 %first_interior.1 = (bf16[20,96,768]{2,1,0:T(8,128)(2,1)S(1)}, bf16[20,96,384]{2,1,0:T(8,128)(2,1)S(1)}, bf16[29,96,384]{2,1,0:T(8,128)(2,1)S(1)}, bf16[29,96,38...) custom-call(bf16[20,96,768]{2,1,0:T(8,128)(2,1)S(1)} %get-tuple-elem, ...), custom_call_target="tpu_custom_call", output_to_operand_aliasing={{0}: (0, {}), {1}: (1, {}), {2}: (2, {}), {3}: (3, {}), {4}... | custom-call | flops 1000 | bytes 1000 | tf_op jit(solution)/shard_map/first_interior/pallas_call | solution.py:353
  15.2 0.0 collective-permute-done.2.refs_4_
  15.2 0.3 edge_rows.4
  15.5 0.7 %collective-permute-start.4 = (bf16[4,96,256]{2,1,0:T(8,128)(2,1)S(1)}, bf16[4,96,256]{2,1,0:T(8,128)(2,1)S(1)}, u32[]{:S(2)}, u32[]{:S(2)}) collective-permute-start(bf16[4,96,256]{2,1,0:T(8,128)(2,1)S(1)} %get-tuple-element.117), channel_id=1, source_target_pairs={{1,4},{5,8},{9,12},{13,0},{4,1},{8,5},{12,9},{0,13},{3,6},{7,10},{... | collective-permute-start | bytes 589832 | tf_op jit(solution)/shard_map/ppermute | solution.py:422
  16.2 0.0 collective-permute-start.3
  16.2 0.2 edge_rows.5
  16.5 2.9 %collective-permute-start.5 = (bf16[4,96,128]{2,1,0:T(8,128)(2,1)S(1)}, bf16[4,96,128]{2,1,0:T(8,128)(2,1)S(1)}, u32[]{:S(2)}, u32[]{:S(2)}) collective-permute-start(bf16[4,96,128]{2,1,0:T(8,128)(2,1)S(1)} %get-tuple-element.123), channel_id=1, source_target_pairs={{1,4},{5,8},{9,12},{13,0},{4,1},{8,5},{12,9},{0,13},{3,6},{7,10},{... | collective-permute-start | bytes 294920 | tf_op jit(solution)/shard_map/ppermute | solution.py:422
  19.4 0.0 collective-permute-done.3.refs_7_
  19.4 3.2 %main_rows.1 = (bf16[20,96,768]{2,1,0:T(8,128)(2,1)S(1)}, bf16[29,96,384]{2,1,0:T(8,128)(2,1)S(1)}, f32[20,96,384]{2,1,0:T(8,128)S(1)}, f32[20,96,384]{2,1,0:T(8...) custom-call(bf16[20,96,768]{2,1,0:T(8,128)(2,1)S(1)} %get-tuple-elem, ...), custom_call_target="tpu_custom_call", output_to_operand_aliasing={{0}: (0, {}), {1}: (1, {}), {2}: (2, {}), {3}: (3, {}), {4}... | custom-call | flops 1000 | bytes 1000 | tf_op jit(solution)/shard_map/main_rows/pallas_call | solution.py:353
  22.7 1.1 %collective-permute-done.4.refs_4_ = bf16[4,96,256]{2,1,0:T(8,128)(2,1)S(1)} collective-permute-done((bf16[4,96,256]{2,1,0:T(8,128)(2,1)S(1)}, bf16[4,96,256]{2,1,0:T(8,128)(2,1)S(1)}, u32[]{:S(2)}, u32[]{:S(2)}) %collective-permute-start.4) | collective-permute-done | bytes 196640 | tf_op jit(solution)/shard_map/ppermute | solution.py:422
  23.8 0.3 edge_rows.6
  24.1 0.5 %collective-permute-start.7 = (bf16[4,96,256]{2,1,0:T(8,128)(2,1)S(1)}, bf16[4,96,256]{2,1,0:T(8,128)(2,1)S(1)}, u32[]{:S(2)}, u32[]{:S(2)}) collective-permute-start(bf16[4,96,256]{2,1,0:T(8,128)(2,1)S(1)} %get-tuple-element.135), channel_id=1, source_target_pairs={{1,4},{5,8},{9,12},{13,0},{4,1},{8,5},{12,9},{0,13},{3,6},{7,10},{... | collective-permute-start | bytes 589832 | tf_op jit(solution)/shard_map/ppermute | solution.py:422
  24.6 0.0 collective-permute-start.6
  24.6 0.3 collective-permute-done.5.refs_4_
  24.9 0.3 edge_rows.7
  25.1 2.9 %collective-permute-start.8 = (bf16[4,96,128]{2,1,0:T(8,128)(2,1)S(1)}, bf16[4,96,128]{2,1,0:T(8,128)(2,1)S(1)}, u32[]{:S(2)}, u32[]{:S(2)}) collective-permute-start(bf16[4,96,128]{2,1,0:T(8,128)(2,1)S(1)} %get-tuple-element.141), channel_id=1, source_target_pairs={{1,4},{5,8},{9,12},{13,0},{4,1},{8,5},{12,9},{0,13},{3,6},{7,10},{... | collective-permute-start | bytes 294920 | tf_op jit(solution)/shard_map/ppermute | solution.py:422
  28.0 0.0 collective-permute-done.6.refs_6_
  28.0 3.8 %main_last.1 = (bf16[20,96,768]{2,1,0:T(8,128)(2,1)S(1)}, bf16[29,96,384]{2,1,0:T(8,128)(2,1)S(1)}, f32[20,96,384]{2,1,0:T(8,128)S(1)}, f32[20,96,384]{2,1,0:T(8...) custom-call(bf16[20,96,768]{2,1,0:T(8,128)(2,1)S(1)} %get-tuple-elem, ...), custom_call_target="tpu_custom_call", output_to_operand_aliasing={{0}: (0, {}), {1}: (1, {}), {2}: (2, {}), {3}: (3, {}), {4}... | custom-call | flops 1000 | bytes 1000 | tf_op jit(solution)/shard_map/main_last/pallas_call | solution.py:353
  31.8 0.3 collective-permute-done.7.refs_3_
  32.1 1.1 %edge_last.2 = (bf16[384,384]{1,0:T(8,128)(2,1)S(1)}, f32[20,96,384]{2,1,0:T(8,128)S(1)}, f32[20,96,384]{2,1,0:T(8,128)S(1)}, bf16[4,96,256]{2,1,0:T(8,128)(2,1)...) custom-call(bf16[384,384]{1,0:T(8,128)(2,1)S(1)} %get-tuple-element., ...), custom_call_target="tpu_custom_call", output_to_operand_aliasing={{0}: (0, {}), {1}: (1, {}), {2}: (2, {}), {3}: (3, {}), {4}... | custom-call | flops 1000 | bytes 1000 | tf_op jit(solution)/shard_map/edge_last/pallas_call | solution.py:433
  33.2 0.0 collective-permute-done.8.refs_3_
  33.2 1.0 %edge_last.3 = (bf16[384,384]{1,0:T(8,128)(2,1)S(1)}, f32[20,96,384]{2,1,0:T(8,128)S(1)}, f32[20,96,384]{2,1,0:T(8,128)S(1)}, bf16[4,96,128]{2,1,0:T(8,128)(2,1)...) custom-call(bf16[384,384]{1,0:T(8,128)(2,1)S(1)} %get-tuple-element., ...), custom_call_target="tpu_custom_call", output_to_operand_aliasing={{0}: (0, {}), {1}: (1, {}), {2}: (2, {}), {3}: (3, {}), {4}... | custom-call | flops 1000 | bytes 1000 | tf_op jit(solution)/shard_map/edge_last/pallas_call | solution.py:433
Async XLA Ops:
  2.0 6.7 %collective-permute-start = (bf16[4,96,384]{2,1,0:T(8,128)(2,1)S(1)}, bf16[4,96,384]{2,1,0:T(8,128)(2,1)S(1)}, u32[]{:S(2)}, u32[]{:S(2)}) collective-permute-start(bf16[4,96,384]{2,1,0:T(8,128)(2,1)S(1)} %get-tuple-element.75), channel_id=1, source_target_pairs={{0,1},{1,0},{4,5},{5,4},{8,9},{9,8},{12,13},{13,12},{2,3},{3,2},{6... | collective-permute-start | bytes 884744 | tf_op jit(solution)/shard_map/ppermute | solution.py:373
  2.6 12.6 %collective-permute-start.2 = (bf16[4,96,384]{2,1,0:T(8,128)(2,1)S(1)}, bf16[4,96,384]{2,1,0:T(8,128)(2,1)S(1)}, u32[]{:S(2)}, u32[]{:S(2)}) collective-permute-start(bf16[4,96,384]{2,1,0:T(8,128)(2,1)S(1)} %get-tuple-element.96), channel_id=1, source_target_pairs={{1,4},{5,8},{9,12},{13,0},{4,1},{8,5},{12,9},{0,13},{3,6},{7,10},{... | collective-permute-start | bytes 884744 | tf_op jit(solution)/shard_map/ppermute | solution.py:374
  7.3 4.4 %collective-permute-start.1 = (f32[3,20,48]{2,1,0:T(8,128)}, f32[3,20,48]{2,1,0:T(8,128)S(1)}, u32[]{:S(2)}, u32[]{:S(2)}) collective-permute-start(f32[3,20,48]{2,1,0:T(8,128)} %refs_7_.1), channel_id=1, source_target_pairs={{2,0},{0,2},{3,1},{1,3},{6,4},{4,6},{7,5},{5,7},{10,8},{8,10},{11,... | collective-permute-start | bytes 34568 | tf_op jit(solution)/shard_map/ppermute | solution.py:377
  15.5 8.3 %collective-permute-start.4 = (bf16[4,96,256]{2,1,0:T(8,128)(2,1)S(1)}, bf16[4,96,256]{2,1,0:T(8,128)(2,1)S(1)}, u32[]{:S(2)}, u32[]{:S(2)}) collective-permute-start(bf16[4,96,256]{2,1,0:T(8,128)(2,1)S(1)} %get-tuple-element.117), channel_id=1, source_target_pairs={{1,4},{5,8},{9,12},{13,0},{4,1},{8,5},{12,9},{0,13},{3,6},{7,10},{... | collective-permute-start | bytes 589832 | tf_op jit(solution)/shard_map/ppermute | solution.py:422
  16.2 3.2 %collective-permute-start.3 = (bf16[4,96,384]{2,1,0:T(8,128)(2,1)S(1)}, bf16[4,96,384]{2,1,0:T(8,128)(2,1)S(1)}, u32[]{:S(2)}, u32[]{:S(2)}) collective-permute-start(bf16[4,96,384]{2,1,0:T(8,128)(2,1)S(1)} %get-tuple-element.112), channel_id=1, source_target_pairs={{0,1},{1,0},{4,5},{5,4},{8,9},{9,8},{12,13},{13,12},{2,3},{3,2},{6... | collective-permute-start | bytes 884744 | tf_op jit(solution)/shard_map/ppermute | solution.py:400
  16.5 8.4 %collective-permute-start.5 = (bf16[4,96,128]{2,1,0:T(8,128)(2,1)S(1)}, bf16[4,96,128]{2,1,0:T(8,128)(2,1)S(1)}, u32[]{:S(2)}, u32[]{:S(2)}) collective-permute-start(bf16[4,96,128]{2,1,0:T(8,128)(2,1)S(1)} %get-tuple-element.123), channel_id=1, source_target_pairs={{1,4},{5,8},{9,12},{13,0},{4,1},{8,5},{12,9},{0,13},{3,6},{7,10},{... | collective-permute-start | bytes 294920 | tf_op jit(solution)/shard_map/ppermute | solution.py:422
  24.1 8.0 %collective-permute-start.7 = (bf16[4,96,256]{2,1,0:T(8,128)(2,1)S(1)}, bf16[4,96,256]{2,1,0:T(8,128)(2,1)S(1)}, u32[]{:S(2)}, u32[]{:S(2)}) collective-permute-start(bf16[4,96,256]{2,1,0:T(8,128)(2,1)S(1)} %get-tuple-element.135), channel_id=1, source_target_pairs={{1,4},{5,8},{9,12},{13,0},{4,1},{8,5},{12,9},{0,13},{3,6},{7,10},{... | collective-permute-start | bytes 589832 | tf_op jit(solution)/shard_map/ppermute | solution.py:422
  24.6 3.4 %collective-permute-start.6 = (bf16[4,96,384]{2,1,0:T(8,128)(2,1)S(1)}, bf16[4,96,384]{2,1,0:T(8,128)(2,1)S(1)}, u32[]{:S(2)}, u32[]{:S(2)}) collective-permute-start(bf16[4,96,384]{2,1,0:T(8,128)(2,1)S(1)} %get-tuple-element.132), channel_id=1, source_target_pairs={{0,1},{1,0},{4,5},{5,4},{8,9},{9,8},{12,13},{13,12},{2,3},{3,2},{6... | collective-permute-start | bytes 884744 | tf_op jit(solution)/shard_map/ppermute | solution.py:414
  25.1 8.1 %collective-permute-start.8 = (bf16[4,96,128]{2,1,0:T(8,128)(2,1)S(1)}, bf16[4,96,128]{2,1,0:T(8,128)(2,1)S(1)}, u32[]{:S(2)}, u32[]{:S(2)}) collective-permute-start(bf16[4,96,128]{2,1,0:T(8,128)(2,1)S(1)} %get-tuple-element.141), channel_id=1, source_target_pairs={{1,4},{5,8},{9,12},{13,0},{4,1},{8,5},{12,9},{0,13},{3,6},{7,10},{... | collective-permute-start | bytes 294920 | tf_op jit(solution)/shard_map/ppermute | solution.py:422

commit v6 on v5

--- a/solution.py
+++ b/solution.py
@@ -10,6 +10,7 @@
 WINDOW = 3
 RING = ("space", "rep")
 VMEM_LIMIT = 24 * 1024 * 1024
+LATE = 8
 
 
 def ring_pairs(ring):
@@ -62,7 +63,7 @@
 
 
 def head(vel0, inv_mass, *refs):
-    out_b, out_a, low, high, mass, sem = refs
+    out_b, *out_a, low, high, mass, sem = refs
     rows, _, lanes = vel0.shape
     end(
         begin(
@@ -79,17 +80,18 @@
         p = spread(upright, j, lanes) * (0.5 * low[j].astype(jnp.float32))
         q = spread(upright, rows - HB + j, lanes) * (0.5 * high[j].astype(jnp.float32))
         out_b[j] = jnp.where(rep == 0, p, q).astype(jnp.bfloat16)
-        out_a[j] = jnp.where(rep == 0, q, p).astype(jnp.bfloat16)
+        a = jnp.where(rep == 0, q, p).astype(jnp.bfloat16)
+        for ref, (at, size) in zip(out_a, windows_of(lanes)):
+            ref[j] = a[:, at : at + size]
 
 
 def load_all(total, blocks_in, vel0_in, disp0_in, inv_mass, stiff_in, contact_in, mine, cols_in, *refs):
-    halo, blocks, disp0, now, disp, vel, mass_b, bent, turned, place_out = refs[:10]
+    blocks, disp0, now, disp, vel, mass_b, bent, turned, place_out, dense = refs[:10]
     vel0, cols, place, mass, stiff, contact, shard, sem = refs[10:]
-    rows, _, lanes = vel0.shape
+    rows, width, lanes = vel0.shape
     rep = lax.axis_index("rep")
-    a_start = (rows - HB) * (1 - rep)
     b_start = (rows - HB) * rep
-    sides = (pl.ds(a_start, HB), pl.ds(b_start, HB), pl.ds(HB, rows - 2 * HB))
+    sides = (pl.ds(b_start, HB), pl.ds(HB, rows - 2 * HB), pl.ds((rows - HB) * (1 - rep), HB))
     get_cols = begin([pltpu.make_async_copy(cols_in, cols, sem.at[0])])
     small = begin(
         [
@@ -110,9 +112,6 @@
         for n, at in enumerate(sides)
     ]
     now[rows + 2 * HB] = jnp.zeros(now.shape[1:], now.dtype)
-    side = (rows + HB) * (1 - rep)
-    for j in range(HB):
-        now[side + j] = halo[j]
     end(get_cols)
     first = (lax.axis_index("space") * 2 + rep) * rows
     row = lax.broadcasted_iota(jnp.int32, cols.shape, 1)
@@ -138,15 +137,25 @@
         now[r + HB] = (tiled(mass_b[r], lanes) * (0.5 * v)).astype(jnp.bfloat16)
     end(get_place)
     end(get_rest[0])
-
-    def one(i):
-        r = a_start + i
-        disp[r] = disp0[r].astype(jnp.float32) - product(blocks, now, place, r)
-
-    each(HB, one)
+    slots = blocks.shape[2] // width
+    shape = (width, HB * width)
+    ahead = lax.broadcasted_iota(jnp.int32, shape, 1) - lax.broadcasted_iota(jnp.int32, shape, 0)
+    for i in range(HB):
+        r = b_start + i
+        chosen = []
+        for k in range(slots):
+            j = place[k, r] - (rows + HB) * rep
+            inside = jnp.logical_and(j >= 0, j < HB)
+            at = jnp.where(inside, j * width, -width)
+            chosen.append(jnp.where(ahead == at, 1.0, 0.0).astype(jnp.bfloat16))
+        picked = jnp.dot(
+            blocks[r], jnp.concatenate(chosen, axis=0), preferred_element_type=jnp.float32
+        )
+        dense[pl.ds(i * width, width), :] = picked.astype(jnp.bfloat16)
+    for i in range(HB):
+        r = b_start + i
+        disp[r] = disp0[r].astype(jnp.float32) - near_product(i, blocks, now, place)
     end(get_rest[1])
-    for j in range(HB):
-        disp[b_start + j] = disp0[b_start + j].astype(jnp.float32)
     end(get_rest[2])
 
 
@@ -171,61 +180,8 @@
         out[r] = spread(matrix, r, 128)
 
 
-def coefficients(pieces, *refs):
-    now, disp, vel, mass_b, bent, turned, *others = refs[5 + pieces : 10 + 2 * pieces]
-    later, coeff, out_a = refs[10 + 2 * pieces :]
-    rows, _, lanes = disp.shape
-    part = turned.shape[1] // pieces
-    me = lax.axis_index("ckpt")
-    last = WINDOW - 1
-    for s in range(WINDOW):
-        for j, piece in enumerate(others):
-            source = lax.rem(me + 1 + j, pieces)
-            turned[s, pl.ds(pl.multiple_of(source * part, 8), part), :] = piece[s].T
-        turned[s] = bent[s] * turned[s] * turned[s]
-    spread_rows(turned[last], coeff)
-    later[rows + 2 * HB] = jnp.zeros(later.shape[1:], later.dtype)
-    start = (rows - HB) * (1 - lax.axis_index("rep"))
-
-    def one(i):
-        r = start + i
-        out_a[i] = finish_row(r, joint(r, now, coeff), later, disp, vel, mass_b)
-
-    each(HB, one)
-
-
-def first_interior(*refs):
-    place, blocks, disp0, now, later, disp, vel, mass_b, coeff, dense = refs[-10:]
-    rows, width, _ = disp.shape
-    slots = blocks.shape[2] // width
-    side = lax.axis_index("rep")
-    shape = (width, HB * width)
-    ahead = lax.broadcasted_iota(jnp.int32, shape, 1) - lax.broadcasted_iota(jnp.int32, shape, 0)
-    for i in range(HB):
-        r = (rows - HB) * side + i
-        chosen = []
-        for k in range(slots):
-            j = place[k, r] - (rows + HB) * side
-            inside = jnp.logical_and(j >= 0, j < HB)
-            at = jnp.where(inside, j * width, -width)
-            chosen.append(jnp.where(ahead == at, 1.0, 0.0).astype(jnp.bfloat16))
-        picked = jnp.dot(
-            blocks[r], jnp.concatenate(chosen, axis=0), preferred_element_type=jnp.float32
-        )
-        dense[pl.ds(i * width, width), :] = picked.astype(jnp.bfloat16)
-
-    def one(i):
-        r = HB + i
-        disp[r] = disp0[r].astype(jnp.float32)
-        image = product(blocks, now, place, r) + joint(r, now, coeff)
-        finish_row(r, image, later, disp, vel, mass_b)
-
-    each(rows - 2 * HB, one)
-    each(HB, lambda i: near_part(i, blocks, now, place, coeff, disp))
-
-
-def near_part(i, blocks, now, place, coeff, disp):
-    rows = disp.shape[0]
+def near_product(i, blocks, now, place):
+    rows = blocks.shape[0]
     rep = lax.axis_index("rep")
     r = (rows - HB) * rep + i
     low = (rows + HB) * rep
@@ -235,27 +191,73 @@
         p = place[k, r]
         inside = jnp.logical_and(p >= low, p < low + HB)
         picked.append(now[jnp.where(inside, rows + 2 * HB, p)])
-    image = jnp.dot(
+    return jnp.dot(
         blocks[r], jnp.concatenate(picked, axis=0), preferred_element_type=jnp.float32
     )
-    disp[r] = disp[r] - (image + joint(r, now, coeff))
+
+
+def near_part(i, blocks, now, place, coeff, disp):
+    rows = disp.shape[0]
+    r = (rows - HB) * lax.axis_index("rep") + i
+    disp[r] = disp[r] - (near_product(i, blocks, now, place) + joint(r, now, coeff))
+
+
+def full_rows(start, count, blocks, now, later, disp_old, disp, vel, mass_b, coeff, place, out=None):
+    def one(i):
+        r = start + i
+        if disp_old is not None:
+            disp[r] = disp_old[r].astype(jnp.float32)
+        image = product(blocks, now, place, r) + joint(r, now, coeff)
+        p = finish_row(r, image, later, disp, vel, mass_b)
+        if out is not None:
+            out[i] = p
+
+    each(count, one)
+
+
+def first_step(pieces, *refs):
+    held = (len(refs) - 4) // 2
+    place = refs[held]
+    blocks, disp0, now, disp, vel, mass_b, bent, turned, *halo = refs[held + 1 : -3 - (pieces - 1)]
+    others = refs[-3 - (pieces - 1) : -3]
+    later, coeff, out_a = refs[-3:]
+    rows = disp.shape[0]
+    part = turned.shape[1] // pieces
+    me = lax.axis_index("ckpt")
+    rep = lax.axis_index("rep")
+    for s in range(WINDOW):
+        for j, piece in enumerate(others):
+            source = lax.rem(me + 1 + j, pieces)
+            turned[s, pl.ds(pl.multiple_of(source * part, 8), part), :] = piece[s].T
+        turned[s] = bent[s] * turned[s] * turned[s]
+    spread_rows(turned[WINDOW - 1], coeff)
+    later[rows + 2 * HB] = jnp.zeros(later.shape[1:], later.dtype)
+    for j in range(HB):
+        for ref, window in zip(halo, windows_of(now.shape[2])):
+            now[(rows + HB) * (1 - rep) + j, :, pl.ds(*window)] = ref[j]
+    state = (blocks, now, later, disp0, disp, vel, mass_b, coeff, place)
+    full_rows((rows - HB) * (1 - rep), HB, *state, out_a)
+    full_rows(HB, rows - 2 * HB - min(LATE, rows - 2 * HB), *state)
+    for i in range(HB):
+        r = (rows - HB) * rep + i
+        disp[r] = disp[r] - joint(r, now, coeff)
 
 
 def main_rows(step, *refs):
-    place, blocks, now, disp, vel, mass_b, turned, coeff, halo, later, out = refs[-11:]
+    place, blocks, now, disp, vel, mass_b, turned, coeff, halo, later, *disp0, out = refs[
+        -11 - (step == WINDOW - 2) :
+    ]
     rows = disp.shape[0]
+    late = min(LATE, rows - 2 * HB)
+    if disp0:
+        first = (later, now, disp0[0], disp, vel, mass_b, coeff, place)
+        full_rows(rows - HB - late, late, blocks, *first)
     spread_rows(turned[step], coeff)
     side = 1 - lax.axis_index("rep")
     for j in range(HB):
         now[(rows + HB) * side + j] = halo[j]
-    start = HB * side
-
-    def one(i):
-        r = start + i
-        image = product(blocks, now, place, r) + joint(r, now, coeff)
-        finish_row(r, image, later, disp, vel, mass_b)
-
-    each(rows - HB, one)
+    state = (blocks, now, later, None, disp, vel, mass_b, coeff, place)
+    full_rows(HB * side, rows - HB, *state)
     for j in range(HB):
         out[j] = later[(rows - HB) * side + HB + j]
     each(HB, lambda i: near_part(i, blocks, now, place, coeff, disp))
@@ -310,12 +312,25 @@
     end(sent)
 
 
+def edge_compute(window, *refs):
+    dense, disp, vel, halo = refs[-4:]
+    rows, width, _ = disp.shape
+    image = far_part(dense, halo, window)
+    start = (rows - HB) * lax.axis_index("rep")
+    for i in range(HB):
+        part = image[i * width : (i + 1) * width]
+        finish_row(start + i, part, None, disp, vel, None, window)
+
+
 def edge_last(window, *refs):
     dense, disp, vel, halo, disp_out, vel_out, sem = refs[-7:]
     rows, width, _ = disp.shape
+    start = (rows - HB) * lax.axis_index("rep")
+    before = (0, window[0])
+    sent = []
+    if window[0]:
+        sent += begin(row_copies(disp, vel, disp_out, vel_out, sem, start, HB, HB, before))
     image = far_part(dense, halo, window)
-    start = (rows - HB) * lax.axis_index("rep")
-    sent = []
     for i in range(HB):
         part = image[i * width : (i + 1) * width]
         finish_row(start + i, part, None, disp, vel, None, window)
@@ -365,12 +380,12 @@
     windows = windows_of(lanes)
     edges_t = [pltpu.VMEM((HB, width, size), bf16) for _, size in windows]
 
-    out_b, out_a = call(
-        head, "head", [], [adj_vel, inv_mass], [hbm] * 2, [edge_t] * 2, [vm] * 2,
-        [edge_t, edge_t, table, dma((3,))],
+    out_b, *out_a = call(
+        head, "head", [], [adj_vel, inv_mass], [hbm] * 2, [edge_t] + edges_t,
+        [vm] * (len(windows) + 1), [edge_t, edge_t, table, dma((3,))],
     )
     states_late, out_a = lax.optimization_barrier((states, out_a))
-    halo_a = lax.ppermute(out_a, RING, inner)
+    halo_a = [lax.ppermute(a, RING, inner) for a in out_a]
     whole_b = lax.ppermute(out_b, RING, outer)
     halo_b = [whole_b] * len(windows)
     others = [
@@ -378,37 +393,33 @@
         for j in range(1, pieces)
     ]
 
-    _, blocks, disp0, now, disp, vel, mass_b, bent, turned, place = call(
-        lambda *refs: load_all(total, *refs[1:9], refs[0], *refs[10:]), "load_all",
-        [halo_a],
+    blocks, disp0, now, disp, vel, mass_b, bent, turned, place, dense = call(
+        functools.partial(load_all, total), "load_all", [],
         [tangent_blocks, adj_vel, adj_disp, inv_mass, joint_stiff, contact, mine, cols], [hbm] * 8,
         [
             like(tangent_blocks), like(adj_disp), ext, full, full,
             pltpu.VMEM((rows, width, 128), f32), upright, upright, like(cols),
+            pltpu.VMEM((HB * width, HB * width), bf16),
         ],
-        [vm] * 9,
+        [vm] * 10,
         [
             like(adj_vel), like(cols), pltpu.SMEM(cols.shape, jnp.int32), table, table,
             pltpu.VMEM(contact.shape, jnp.int32), pltpu.VMEM(states.shape, f32), dma((12,)),
         ],
     )
-    now, disp, vel, mass_b, _, turned, *_, later, coeff, out_a = call(
-        functools.partial(coefficients, pieces), "coefficients",
-        [now, disp, vel, mass_b, bent, turned] + others, [], [],
+    blocks, disp0, now, disp, vel, mass_b, _, turned, *_, later, coeff, out_a = call(
+        functools.partial(first_step, pieces), "first_step",
+        [blocks, disp0, now, disp, vel, mass_b, bent, turned] + halo_a + others, [place], [sm],
         [ext, like(mass_b), edge_t], [vm] * 3,
     )
     halo_a = lax.ppermute(out_a, RING, inner)
-    blocks, _, now, later, disp, vel, mass_b, coeff, dense = call(
-        first_interior, "first_interior",
-        [blocks, disp0, now, later, disp, vel, mass_b, coeff], [place], [sm],
-        [pltpu.VMEM((HB * width, HB * width), bf16)], [vm],
-    )
     for step in range(WINDOW - 1, 0, -1):
         if step < WINDOW - 1:
-            blocks, later, disp, vel, mass_b, turned, coeff, _, now, out_a = call(
+            old = [disp0] if step == WINDOW - 2 else []
+            blocks, later, disp, vel, mass_b, turned, coeff, _, now, *_, out_a = call(
                 functools.partial(main_rows, step), "main_rows",
-                [blocks, later, disp, vel, mass_b, turned, coeff, halo_a, now], [place], [sm],
-                [edge_t], [vm],
+                [blocks, later, disp, vel, mass_b, turned, coeff, halo_a, now] + old,
+                [place], [sm], [edge_t], [vm],
             )
             now, later = later, now
             halo_a = lax.ppermute(out_a, RING, inner)
@@ -429,19 +440,23 @@
         main_last, "main_last", [blocks, later, disp, vel, turned, coeff, halo_a], [place], [sm],
         [shape] * 2, [hbm] * 2, [dma((2, rows // HB - 1))],
     )
-    for n, window in enumerate(windows):
-        dense, disp, vel, _, disp_out, vel_out = pl.pallas_call(
-            functools.partial(edge_last, window),
-            name="edge_last",
-            out_shape=tuple(like(a) for a in (dense, disp, vel, halo_b[n])) + (shape,) * 2,
-            in_specs=[vm] * 4 + [hbm] * 2,
-            out_specs=(vm,) * 4 + (hbm,) * 2,
-            input_output_aliases={i: i for i in range(6)},
-            scratch_shapes=[dma((2, HB))],
-            compiler_params=pltpu.CompilerParams(vmem_limit_bytes=VMEM_LIMIT),
-            cost_estimate=light,
-        )(dense, disp, vel, halo_b[n], disp_out, vel_out)
-    return disp_out, vel_out
+    for window, halo in zip(windows[:-1], halo_b):
+        dense, disp, vel, _ = call(
+            functools.partial(edge_compute, window), "edge_compute",
+            [dense, disp, vel, halo], [], [], [], [],
+        )
+    held = [dense, disp, vel, halo_b[-1]]
+    return pl.pallas_call(
+        functools.partial(edge_last, windows[-1]),
+        name="edge_last",
+        out_shape=tuple(like(a) for a in held) + (shape,) * 2,
+        in_specs=[vm] * 4 + [hbm] * 2,
+        out_specs=(vm,) * 4 + (hbm,) * 2,
+        input_output_aliases={i: i for i in range(6)},
+        scratch_shapes=[dma((2, HB + 1))],
+        compiler_params=pltpu.CompilerParams(vmem_limit_bytes=VMEM_LIMIT),
+        cost_estimate=light,
+    )(*held, disp_out, vel_out)[-2:]
 
 
 def solution(mesh):

time: 34.5 us -> 33.6 us (0.974)
  Pallas kernels: 18 us -> 16.7 us
    pallas_call x2 -> x1, Pallas kernels: 2.13 us -> 1.12 us  [body(): pl.pallas_call(functools.partial(edge_last, windows[-1]), name='edge_last...]
    ppermute x0 -> x2, starting transfers between devices: none -> 0.51 us  [body(): halo_a = [lax.ppermute(a, RING, inner) for a in out_a]]
    ppermute x3 -> x2, starting transfers between devices: 0.52 us -> 0.07 us  [body(): halo_a = lax.ppermute(out_a, RING, inner)]
  transfers between devices with their start and end apart: 9 -> 10, of which waited for: 3 -> 4; matrix products, arithmetic and copies ran while one was open for 0% -> 0% of each run, Pallas kernels for 45% -> 43%
where the time goes in v6:
time: 33.6 us; the launch traced here: 33.3 us
  Pallas kernels  16.7 us (50%)
  starting transfers between devices  13.9 us (41%)
  waiting for transfers between devices  1.98 us (6%)
  between operations  0.75 us (2%)
    pallas_call x10, Pallas kernels, call(): pl.pallas_call(kernel, name=name, out_shape=tuple((like(a) for a in held)...  15.6 us
    ppermute x4, starting transfers between devices, body(): sent.append(lax.ppermute(out, RING, outer))  7.26 us
    ppermute x1, starting transfers between devices, body(): whole_b = lax.ppermute(out_b, RING, outer)  4.55 us
    ppermute x4, waiting for transfers between devices, body(): sent.append(lax.ppermute(out, RING, outer))  1.96 us
    ppermute x1, starting transfers between devices, body(): lax.ppermute(states_late, 'ckpt', [((i + j) % pieces, i) for i in range(p...  1.49 us
    pallas_call x1, Pallas kernels, body(): pl.pallas_call(functools.partial(edge_last, windows[-1]), name='edge_last...  1.12 us
  transfers between devices with their start and end apart: 10, of which 4 were waited for; matrix products, arithmetic and copies ran while one was open for 0% of the time, Pallas kernels for 43%

profile of v6, /device:TPU:0, one launch (start us, length us, event | category | flops | bytes accessed | tf_op | source)
XLA Modules:
  0.0 33.3 jit_solution(16354263272806497804)
XLA Ops:
  0.6 1.4 %head.1 = (bf16[4,96,384]{2,1,0:T(8,128)(2,1)S(1)}, bf16[4,96,256]{2,1,0:T(8,128)(2,1)S(1)}, bf16[4,96,128]{2,1,0:T(8,128)(2,1)S(1)}) custom-call(bf16[20,96,384]{2,1,0:T(8,128)(2,1)} %vel0.1, f32[20,96]{1,0:T(8,128)} %inv_mass.3), custom_call_target="tpu_custom_call" | custom-call | flops 1000 | bytes 1000 | tf_op jit(solution)/shard_map/head/pallas_call | solution.py:368
  2.0 4.6 %collective-permute-start.3 = (bf16[4,96,384]{2,1,0:T(8,128)(2,1)S(1)}, bf16[4,96,384]{2,1,0:T(8,128)(2,1)S(1)}, u32[]{:S(2)}, u32[]{:S(2)}) collective-permute-start(bf16[4,96,384]{2,1,0:T(8,128)(2,1)S(1)} %get-tuple-element.87), channel_id=1, source_target_pairs={{1,4},{5,8},{9,12},{13,0},{4,1},{8,5},{12,9},{0,13},{3,6},{7,10},{... | collective-permute-start | bytes 884744 | tf_op jit(solution)/shard_map/ppermute | solution.py:389
  6.6 0.0 collective-permute-start
  6.6 0.5 %collective-permute-start.1 = (bf16[4,96,128]{2,1,0:T(8,128)(2,1)S(1)}, bf16[4,96,128]{2,1,0:T(8,128)(2,1)S(1)}, u32[]{:S(2)}, u32[]{:S(2)}) collective-permute-start(bf16[4,96,128]{2,1,0:T(8,128)(2,1)S(1)} %get-tuple-element.81), channel_id=1, source_target_pairs={{0,1},{1,0},{4,5},{5,4},{8,9},{9,8},{12,13},{13,12},{2,3},{3,2},{6... | collective-permute-start | bytes 294920 | tf_op jit(solution)/shard_map/ppermute | solution.py:388
  7.1 1.5 %collective-permute-start.2 = (f32[3,20,48]{2,1,0:T(8,128)}, f32[3,20,48]{2,1,0:T(8,128)S(1)}, u32[]{:S(2)}, u32[]{:S(2)}) collective-permute-start(f32[3,20,48]{2,1,0:T(8,128)} %mine.1), channel_id=1, source_target_pairs={{2,0},{0,2},{3,1},{1,3},{6,4},{4,6},{7,5},{5,7},{10,8},{8,10},{11,... | collective-permute-start | bytes 34568 | tf_op jit(solution)/shard_map/ppermute | solution.py:392
  8.6 2.9 %load_all.1 = (bf16[20,96,768]{2,1,0:T(8,128)(2,1)S(1)}, bf16[20,96,384]{2,1,0:T(8,128)(2,1)S(1)}, bf16[29,96,384]{2,1,0:T(8,128)(2,1)S(1)}, f32[20,96,384]{2,1,...) custom-call(bf16[20,96,768]{2,1,0:T(8,128)(2,1)} %blocks_in.1, ...), custom_call_target="tpu_custom_call" | custom-call | flops 1000 | bytes 1000 | tf_op jit(solution)/shard_map/load_all/pallas_call | solution.py:368
  11.5 0.0 collective-permute-done.2.refs_10_
  11.5 0.0 collective-permute-done.1.refs_9_
  11.5 0.0 collective-permute-done.refs_8_
  11.5 2.0 %first_step.1 = (bf16[20,96,768]{2,1,0:T(8,128)(2,1)S(1)}, bf16[20,96,384]{2,1,0:T(8,128)(2,1)S(1)}, bf16[29,96,384]{2,1,0:T(8,128)(2,1)S(1)}, f32[20,96,384]{2,...) custom-call(bf16[20,96,768]{2,1,0:T(8,128)(2,1)S(1)} %get-tuple-elem, ...), custom_call_target="tpu_custom_call", output_to_operand_aliasing={{0}: (0, {}), {1}: (1, {}), {2}: (2, {}), {3}: (3, {}), {4}... | custom-call | flops 1000 | bytes 1000 | tf_op jit(solution)/shard_map/first_step/pallas_call | solution.py:368
  13.5 0.1 collective-permute-start.4
  13.5 0.0 collective-permute-done.3.refs_4_
  13.5 0.3 edge_rows.4
  13.8 2.3 %collective-permute-start.5 = (bf16[4,96,256]{2,1,0:T(8,128)(2,1)S(1)}, bf16[4,96,256]{2,1,0:T(8,128)(2,1)S(1)}, u32[]{:S(2)}, u32[]{:S(2)}) collective-permute-start(bf16[4,96,256]{2,1,0:T(8,128)(2,1)S(1)} %get-tuple-element.109), channel_id=1, source_target_pairs={{1,4},{5,8},{9,12},{13,0},{4,1},{8,5},{12,9},{0,13},{3,6},{7,10},{... | collective-permute-start | bytes 589832 | tf_op jit(solution)/shard_map/ppermute | solution.py:433
  16.2 0.2 edge_rows.5
  16.4 1.3 %collective-permute-start.6 = (bf16[4,96,128]{2,1,0:T(8,128)(2,1)S(1)}, bf16[4,96,128]{2,1,0:T(8,128)(2,1)S(1)}, u32[]{:S(2)}, u32[]{:S(2)}) collective-permute-start(bf16[4,96,128]{2,1,0:T(8,128)(2,1)S(1)} %get-tuple-element.115), channel_id=1, source_target_pairs={{1,4},{5,8},{9,12},{13,0},{4,1},{8,5},{12,9},{0,13},{3,6},{7,10},{... | collective-permute-start | bytes 294920 | tf_op jit(solution)/shard_map/ppermute | solution.py:433
  17.7 0.0 collective-permute-done.4.refs_7_
  17.7 4.4 %main_rows.1 = (bf16[20,96,768]{2,1,0:T(8,128)(2,1)S(1)}, bf16[29,96,384]{2,1,0:T(8,128)(2,1)S(1)}, f32[20,96,384]{2,1,0:T(8,128)S(1)}, f32[20,96,384]{2,1,0:T(8...) custom-call(bf16[20,96,768]{2,1,0:T(8,128)(2,1)S(1)} %get-tuple-elem, ...), custom_call_target="tpu_custom_call", output_to_operand_aliasing={{0}: (0, {}), {1}: (1, {}), {2}: (2, {}), {3}: (3, {}), {4}... | custom-call | flops 1000 | bytes 1000 | tf_op jit(solution)/shard_map/main_rows/pallas_call | solution.py:368
  22.1 0.8 %collective-permute-done.5.refs_4_ = bf16[4,96,256]{2,1,0:T(8,128)(2,1)S(1)} collective-permute-done((bf16[4,96,256]{2,1,0:T(8,128)(2,1)S(1)}, bf16[4,96,256]{2,1,0:T(8,128)(2,1)S(1)}, u32[]{:S(2)}, u32[]{:S(2)}) %collective-permute-start.5) | collective-permute-done | bytes 196640 | tf_op jit(solution)/shard_map/ppermute | solution.py:433
  22.9 0.3 edge_rows.6
  23.1 1.6 %collective-permute-start.8 = (bf16[4,96,256]{2,1,0:T(8,128)(2,1)S(1)}, bf16[4,96,256]{2,1,0:T(8,128)(2,1)S(1)}, u32[]{:S(2)}, u32[]{:S(2)}) collective-permute-start(bf16[4,96,256]{2,1,0:T(8,128)(2,1)S(1)} %get-tuple-element.127), channel_id=1, source_target_pairs={{1,4},{5,8},{9,12},{13,0},{4,1},{8,5},{12,9},{0,13},{3,6},{7,10},{... | collective-permute-start | bytes 589832 | tf_op jit(solution)/shard_map/ppermute | solution.py:433
  24.8 0.0 collective-permute-start.7
  24.8 0.1 collective-permute-done.6.refs_4_
  24.9 0.2 edge_rows.7
  25.1 2.0 %collective-permute-start.9 = (bf16[4,96,128]{2,1,0:T(8,128)(2,1)S(1)}, bf16[4,96,128]{2,1,0:T(8,128)(2,1)S(1)}, u32[]{:S(2)}, u32[]{:S(2)}) collective-permute-start(bf16[4,96,128]{2,1,0:T(8,128)(2,1)S(1)} %get-tuple-element.131), channel_id=1, source_target_pairs={{1,4},{5,8},{9,12},{13,0},{4,1},{8,5},{12,9},{0,13},{3,6},{7,10},{... | collective-permute-start | bytes 294920 | tf_op jit(solution)/shard_map/ppermute | solution.py:433
  27.1 0.0 collective-permute-done.7.refs_6_
  27.1 3.7 %main_last.1 = (bf16[20,96,768]{2,1,0:T(8,128)(2,1)S(1)}, bf16[29,96,384]{2,1,0:T(8,128)(2,1)S(1)}, f32[20,96,384]{2,1,0:T(8,128)S(1)}, f32[20,96,384]{2,1,0:T(8...) custom-call(bf16[20,96,768]{2,1,0:T(8,128)(2,1)S(1)} %get-tuple-elem, ...), custom_call_target="tpu_custom_call", output_to_operand_aliasing={{0}: (0, {}), {1}: (1, {}), {2}: (2, {}), {3}: (3, {}), {4}... | custom-call | flops 1000 | bytes 1000 | tf_op jit(solution)/shard_map/main_last/pallas_call | solution.py:368
  30.8 0.3 %collective-permute-done.8.refs_3_ = bf16[4,96,256]{2,1,0:T(8,128)(2,1)S(1)} collective-permute-done((bf16[4,96,256]{2,1,0:T(8,128)(2,1)S(1)}, bf16[4,96,256]{2,1,0:T(8,128)(2,1)S(1)}, u32[]{:S(2)}, u32[]{:S(2)}) %collective-permute-start.8) | collective-permute-done | bytes 196640 | tf_op jit(solution)/shard_map/ppermute | solution.py:433
  31.2 0.3 edge_compute.1
  31.4 0.8 %collective-permute-done.9.refs_3_ = bf16[4,96,128]{2,1,0:T(8,128)(2,1)S(1)} collective-permute-done((bf16[4,96,128]{2,1,0:T(8,128)(2,1)S(1)}, bf16[4,96,128]{2,1,0:T(8,128)(2,1)S(1)}, u32[]{:S(2)}, u32[]{:S(2)}) %collective-permute-start.9) | collective-permute-done | bytes 98336 | tf_op jit(solution)/shard_map/ppermute | solution.py:433
  32.2 1.1 %edge_last.1 = (bf16[384,384]{1,0:T(8,128)(2,1)S(1)}, f32[20,96,384]{2,1,0:T(8,128)S(1)}, f32[20,96,384]{2,1,0:T(8,128)S(1)}, bf16[4,96,128]{2,1,0:T(8,128)(2,1)...) custom-call(bf16[384,384]{1,0:T(8,128)(2,1)S(1)} %get-tuple-element., ...), custom_call_target="tpu_custom_call", output_to_operand_aliasing={{0}: (0, {}), {1}: (1, {}), {2}: (2, {}), {3}: (3, {}), {4}... | custom-call | flops 1000 | bytes 1000 | tf_op jit(solution)/shard_map/edge_last/pallas_call | solution.py:449
Async XLA Ops:
  2.0 11.5 %collective-permute-start.3 = (bf16[4,96,384]{2,1,0:T(8,128)(2,1)S(1)}, bf16[4,96,384]{2,1,0:T(8,128)(2,1)S(1)}, u32[]{:S(2)}, u32[]{:S(2)}) collective-permute-start(bf16[4,96,384]{2,1,0:T(8,128)(2,1)S(1)} %get-tuple-element.87), channel_id=1, source_target_pairs={{1,4},{5,8},{9,12},{13,0},{4,1},{8,5},{12,9},{0,13},{3,6},{7,10},{... | collective-permute-start | bytes 884744 | tf_op jit(solution)/shard_map/ppermute | solution.py:389
  6.6 4.9 %collective-permute-start = (bf16[4,96,256]{2,1,0:T(8,128)(2,1)S(1)}, bf16[4,96,256]{2,1,0:T(8,128)(2,1)S(1)}, u32[]{:S(2)}, u32[]{:S(2)}) collective-permute-start(bf16[4,96,256]{2,1,0:T(8,128)(2,1)S(1)} %get-tuple-element.80), channel_id=1, source_target_pairs={{0,1},{1,0},{4,5},{5,4},{8,9},{9,8},{12,13},{13,12},{2,3},{3,2},{6... | collective-permute-start | bytes 589832 | tf_op jit(solution)/shard_map/ppermute | solution.py:388
  6.6 4.9 %collective-permute-start.1 = (bf16[4,96,128]{2,1,0:T(8,128)(2,1)S(1)}, bf16[4,96,128]{2,1,0:T(8,128)(2,1)S(1)}, u32[]{:S(2)}, u32[]{:S(2)}) collective-permute-start(bf16[4,96,128]{2,1,0:T(8,128)(2,1)S(1)} %get-tuple-element.81), channel_id=1, source_target_pairs={{0,1},{1,0},{4,5},{5,4},{8,9},{9,8},{12,13},{13,12},{2,3},{3,2},{6... | collective-permute-start | bytes 294920 | tf_op jit(solution)/shard_map/ppermute | solution.py:388
  7.1 4.4 %collective-permute-start.2 = (f32[3,20,48]{2,1,0:T(8,128)}, f32[3,20,48]{2,1,0:T(8,128)S(1)}, u32[]{:S(2)}, u32[]{:S(2)}) collective-permute-start(f32[3,20,48]{2,1,0:T(8,128)} %mine.1), channel_id=1, source_target_pairs={{2,0},{0,2},{3,1},{1,3},{6,4},{4,6},{7,5},{5,7},{10,8},{8,10},{11,... | collective-permute-start | bytes 34568 | tf_op jit(solution)/shard_map/ppermute | solution.py:392
  13.5 4.3 %collective-permute-start.4 = (bf16[4,96,384]{2,1,0:T(8,128)(2,1)S(1)}, bf16[4,96,384]{2,1,0:T(8,128)(2,1)S(1)}, u32[]{:S(2)}, u32[]{:S(2)}) collective-permute-start(bf16[4,96,384]{2,1,0:T(8,128)(2,1)S(1)} %get-tuple-element.103), channel_id=1, source_target_pairs={{0,1},{1,0},{4,5},{5,4},{8,9},{9,8},{12,13},{13,12},{2,3},{3,2},{6... | collective-permute-start | bytes 884744 | tf_op jit(solution)/shard_map/ppermute | solution.py:415
  13.8 9.1 %collective-permute-start.5 = (bf16[4,96,256]{2,1,0:T(8,128)(2,1)S(1)}, bf16[4,96,256]{2,1,0:T(8,128)(2,1)S(1)}, u32[]{:S(2)}, u32[]{:S(2)}) collective-permute-start(bf16[4,96,256]{2,1,0:T(8,128)(2,1)S(1)} %get-tuple-element.109), channel_id=1, source_target_pairs={{1,4},{5,8},{9,12},{13,0},{4,1},{8,5},{12,9},{0,13},{3,6},{7,10},{... | collective-permute-start | bytes 589832 | tf_op jit(solution)/shard_map/ppermute | solution.py:433
  16.4 8.5 %collective-permute-start.6 = (bf16[4,96,128]{2,1,0:T(8,128)(2,1)S(1)}, bf16[4,96,128]{2,1,0:T(8,128)(2,1)S(1)}, u32[]{:S(2)}, u32[]{:S(2)}) collective-permute-start(bf16[4,96,128]{2,1,0:T(8,128)(2,1)S(1)} %get-tuple-element.115), channel_id=1, source_target_pairs={{1,4},{5,8},{9,12},{13,0},{4,1},{8,5},{12,9},{0,13},{3,6},{7,10},{... | collective-permute-start | bytes 294920 | tf_op jit(solution)/shard_map/ppermute | solution.py:433
  23.1 8.0 %collective-permute-start.8 = (bf16[4,96,256]{2,1,0:T(8,128)(2,1)S(1)}, bf16[4,96,256]{2,1,0:T(8,128)(2,1)S(1)}, u32[]{:S(2)}, u32[]{:S(2)}) collective-permute-start(bf16[4,96,256]{2,1,0:T(8,128)(2,1)S(1)} %get-tuple-element.127), channel_id=1, source_target_pairs={{1,4},{5,8},{9,12},{13,0},{4,1},{8,5},{12,9},{0,13},{3,6},{7,10},{... | collective-permute-start | bytes 589832 | tf_op jit(solution)/shard_map/ppermute | solution.py:433
  24.8 2.3 %collective-permute-start.7 = (bf16[4,96,384]{2,1,0:T(8,128)(2,1)S(1)}, bf16[4,96,384]{2,1,0:T(8,128)(2,1)S(1)}, u32[]{:S(2)}, u32[]{:S(2)}) collective-permute-start(bf16[4,96,384]{2,1,0:T(8,128)(2,1)S(1)} %get-tuple-element.124), channel_id=1, source_target_pairs={{0,1},{1,0},{4,5},{5,4},{8,9},{9,8},{12,13},{13,12},{2,3},{3,2},{6... | collective-permute-start | bytes 884744 | tf_op jit(solution)/shard_map/ppermute | solution.py:425
  25.1 7.1 %collective-permute-start.9 = (bf16[4,96,128]{2,1,0:T(8,128)(2,1)S(1)}, bf16[4,96,128]{2,1,0:T(8,128)(2,1)S(1)}, u32[]{:S(2)}, u32[]{:S(2)}) collective-permute-start(bf16[4,96,128]{2,1,0:T(8,128)(2,1)S(1)} %get-tuple-element.131), channel_id=1, source_target_pairs={{1,4},{5,8},{9,12},{13,0},{4,1},{8,5},{12,9},{0,13},{3,6},{7,10},{... | collective-permute-start | bytes 294920 | tf_op jit(solution)/shard_map/ppermute | solution.py:433

commit v7 on v6

--- a/solution.py
+++ b/solution.py
@@ -65,22 +65,24 @@
 def head(vel0, inv_mass, *refs):
     out_b, *out_a, low, high, mass, sem = refs
     rows, _, lanes = vel0.shape
-    end(
-        begin(
-            [
-                pltpu.make_async_copy(inv_mass, mass, sem.at[0]),
-                pltpu.make_async_copy(vel0.at[pl.ds(0, HB)], low, sem.at[1]),
-                pltpu.make_async_copy(vel0.at[pl.ds(rows - HB, HB)], high, sem.at[2]),
-            ]
-        )
-    )
     rep = lax.axis_index("rep")
-    upright = mass[...].T
+    loads = begin(
+        [
+            pltpu.make_async_copy(inv_mass, mass, sem.at[0]),
+            pltpu.make_async_copy(vel0.at[pl.ds((rows - HB) * rep, HB)], low, sem.at[1]),
+            pltpu.make_async_copy(vel0.at[pl.ds((rows - HB) * (1 - rep), HB)], high, sem.at[2]),
+        ]
+    )
+    end(loads[:1])
+    upright = 0.5 * mass[...].T
+    first = [spread(upright, j, 128) for j in range(HB)]
+    last = [spread(upright, rows - HB + j, 128) for j in range(HB)]
+    mass_b = [jnp.where(rep == 0, p, q) for p, q in zip(first, last)]
+    mass_a = [jnp.where(rep == 0, q, p) for p, q in zip(first, last)]
+    end(loads[1:])
     for j in range(HB):
-        p = spread(upright, j, lanes) * (0.5 * low[j].astype(jnp.float32))
-        q = spread(upright, rows - HB + j, lanes) * (0.5 * high[j].astype(jnp.float32))
-        out_b[j] = jnp.where(rep == 0, p, q).astype(jnp.bfloat16)
-        a = jnp.where(rep == 0, q, p).astype(jnp.bfloat16)
+        out_b[j] = (tiled(mass_b[j], lanes) * low[j].astype(jnp.float32)).astype(jnp.bfloat16)
+        a = (tiled(mass_a[j], lanes) * high[j].astype(jnp.float32)).astype(jnp.bfloat16)
         for ref, (at, size) in zip(out_a, windows_of(lanes)):
             ref[j] = a[:, at : at + size]
 
@@ -243,15 +245,17 @@
         disp[r] = disp[r] - joint(r, now, coeff)
 
 
-def main_rows(step, *refs):
-    place, blocks, now, disp, vel, mass_b, turned, coeff, halo, later, *disp0, out = refs[
-        -11 - (step == WINDOW - 2) :
-    ]
+def late_rows(*refs):
+    place, blocks, disp0, now, later, disp, vel, mass_b, coeff = refs[-9:]
     rows = disp.shape[0]
     late = min(LATE, rows - 2 * HB)
-    if disp0:
-        first = (later, now, disp0[0], disp, vel, mass_b, coeff, place)
-        full_rows(rows - HB - late, late, blocks, *first)
+    state = (blocks, now, later, disp0, disp, vel, mass_b, coeff, place)
+    full_rows(rows - HB - late, late, *state)
+
+
+def main_rows(step, *refs):
+    place, blocks, now, disp, vel, mass_b, turned, coeff, halo, later, out = refs[-11:]
+    rows = disp.shape[0]
     spread_rows(turned[step], coeff)
     side = 1 - lax.axis_index("rep")
     for j in range(HB):
@@ -312,25 +316,12 @@
     end(sent)
 
 
-def edge_compute(window, *refs):
-    dense, disp, vel, halo = refs[-4:]
-    rows, width, _ = disp.shape
-    image = far_part(dense, halo, window)
-    start = (rows - HB) * lax.axis_index("rep")
-    for i in range(HB):
-        part = image[i * width : (i + 1) * width]
-        finish_row(start + i, part, None, disp, vel, None, window)
-
-
 def edge_last(window, *refs):
     dense, disp, vel, halo, disp_out, vel_out, sem = refs[-7:]
     rows, width, _ = disp.shape
     start = (rows - HB) * lax.axis_index("rep")
-    before = (0, window[0])
+    image = far_part(dense, halo, window)
     sent = []
-    if window[0]:
-        sent += begin(row_copies(disp, vel, disp_out, vel_out, sem, start, HB, HB, before))
-    image = far_part(dense, halo, window)
     for i in range(HB):
         part = image[i * width : (i + 1) * width]
         finish_row(start + i, part, None, disp, vel, None, window)
@@ -415,10 +406,9 @@
     halo_a = lax.ppermute(out_a, RING, inner)
     for step in range(WINDOW - 1, 0, -1):
         if step < WINDOW - 1:
-            old = [disp0] if step == WINDOW - 2 else []
-            blocks, later, disp, vel, mass_b, turned, coeff, _, now, *_, out_a = call(
+            blocks, later, disp, vel, mass_b, turned, coeff, _, now, out_a = call(
                 functools.partial(main_rows, step), "main_rows",
-                [blocks, later, disp, vel, mass_b, turned, coeff, halo_a, now] + old,
+                [blocks, later, disp, vel, mass_b, turned, coeff, halo_a, now],
                 [place], [sm], [edge_t], [vm],
             )
             now, later = later, now
@@ -433,6 +423,12 @@
             sent.append(lax.ppermute(out, RING, outer))
             if step == WINDOW - 1:
                 halo_b = [halo] * len(windows)
+                if n == 0:
+                    blocks, _, now, later, disp, vel, mass_b, coeff = call(
+                        late_rows, "late_rows",
+                        [blocks, disp0, now, later, disp, vel, mass_b, coeff], [place], [sm],
+                        [], [],
+                    )
         halo_b = sent
 
     shape = jax.ShapeDtypeStruct((rows, width, lanes), f32)
@@ -440,23 +436,20 @@
         main_last, "main_last", [blocks, later, disp, vel, turned, coeff, halo_a], [place], [sm],
         [shape] * 2, [hbm] * 2, [dma((2, rows // HB - 1))],
     )
-    for window, halo in zip(windows[:-1], halo_b):
-        dense, disp, vel, _ = call(
-            functools.partial(edge_compute, window), "edge_compute",
-            [dense, disp, vel, halo], [], [], [], [],
-        )
-    held = [dense, disp, vel, halo_b[-1]]
-    return pl.pallas_call(
-        functools.partial(edge_last, windows[-1]),
-        name="edge_last",
-        out_shape=tuple(like(a) for a in held) + (shape,) * 2,
-        in_specs=[vm] * 4 + [hbm] * 2,
-        out_specs=(vm,) * 4 + (hbm,) * 2,
-        input_output_aliases={i: i for i in range(6)},
-        scratch_shapes=[dma((2, HB + 1))],
-        compiler_params=pltpu.CompilerParams(vmem_limit_bytes=VMEM_LIMIT),
-        cost_estimate=light,
-    )(*held, disp_out, vel_out)[-2:]
+    for window, halo in zip(windows, halo_b):
+        held = [dense, disp, vel, halo]
+        dense, disp, vel, _, disp_out, vel_out = pl.pallas_call(
+            functools.partial(edge_last, window),
+            name="edge_last",
+            out_shape=tuple(like(a) for a in held) + (shape,) * 2,
+            in_specs=[vm] * 4 + [hbm] * 2,
+            out_specs=(vm,) * 4 + (hbm,) * 2,
+            input_output_aliases={i: i for i in range(6)},
+            scratch_shapes=[dma((2, HB))],
+            compiler_params=pltpu.CompilerParams(vmem_limit_bytes=VMEM_LIMIT),
+            cost_estimate=light,
+        )(*held, disp_out, vel_out)
+    return disp_out, vel_out
 
 
 def solution(mesh):

time: 33.6 us -> 33.4 us (level)
  waiting for transfers between devices: 1.98 us -> 0.73 us
  Pallas kernels: 16.7 us -> 17.7 us
    ppermute x4, waiting for transfers between devices: 1.96 us -> 0.71 us  [body(): sent.append(lax.ppermute(out, RING, outer))]
    pallas_call x1 -> x2, Pallas kernels: 1.12 us -> 2.13 us  [body(): pl.pallas_call(functools.partial(edge_last, window), name='edge_last', ou...]
  transfers between devices with their start and end apart: 10 -> 10, of which waited for: 4 -> 2; matrix products, arithmetic and copies ran while one was open for 0% -> 0% of each run, Pallas kernels for 43% -> 47%
where the time goes in v7:
time: 33.4 us; the launch traced here: 33.2 us
  Pallas kernels  17.7 us (53%)
  starting transfers between devices  14 us (42%)
  between operations  0.77 us (2%)
  waiting for transfers between devices  0.73 us (2%)
    pallas_call x10, Pallas kernels, call(): pl.pallas_call(kernel, name=name, out_shape=tuple((like(a) for a in held)...  15.6 us
    ppermute x4, starting transfers between devices, body(): sent.append(lax.ppermute(out, RING, outer))  7.36 us
    ppermute x1, starting transfers between devices, body(): whole_b = lax.ppermute(out_b, RING, outer)  4.55 us
    pallas_call x2, Pallas kernels, body(): pl.pallas_call(functools.partial(edge_last, window), name='edge_last', ou...  2.13 us
    ppermute x1, starting transfers between devices, body(): lax.ppermute(states_late, 'ckpt', [((i + j) % pieces, i) for i in range(p...  1.49 us
    ppermute x4, waiting for transfers between devices, body(): sent.append(lax.ppermute(out, RING, outer))  0.71 us
  transfers between devices with their start and end apart: 10, of which 2 were waited for; matrix products, arithmetic and copies ran while one was open for 0% of the time, Pallas kernels for 47%

profile of v7, /device:TPU:0, one launch (start us, length us, event | category | flops | bytes accessed | tf_op | source)
XLA Modules:
  0.0 33.2 jit_solution(17484325380320962558)
XLA Ops:
  0.6 1.2 %head.1 = (bf16[4,96,384]{2,1,0:T(8,128)(2,1)S(1)}, bf16[4,96,256]{2,1,0:T(8,128)(2,1)S(1)}, bf16[4,96,128]{2,1,0:T(8,128)(2,1)S(1)}) custom-call(bf16[20,96,384]{2,1,0:T(8,128)(2,1)} %vel0.1, f32[20,96]{1,0:T(8,128)} %inv_mass.3), custom_call_target="tpu_custom_call" | custom-call | flops 1000 | bytes 1000 | tf_op jit(solution)/shard_map/head/pallas_call | solution.py:359
  1.8 4.6 %collective-permute-start.3 = (bf16[4,96,384]{2,1,0:T(8,128)(2,1)S(1)}, bf16[4,96,384]{2,1,0:T(8,128)(2,1)S(1)}, u32[]{:S(2)}, u32[]{:S(2)}) collective-permute-start(bf16[4,96,384]{2,1,0:T(8,128)(2,1)S(1)} %get-tuple-element.96), channel_id=1, source_target_pairs={{1,4},{5,8},{9,12},{13,0},{4,1},{8,5},{12,9},{0,13},{3,6},{7,10},{... | collective-permute-start | bytes 884744 | tf_op jit(solution)/shard_map/ppermute | solution.py:380
  6.4 0.0 collective-permute-start
  6.4 0.5 %collective-permute-start.1 = (bf16[4,96,128]{2,1,0:T(8,128)(2,1)S(1)}, bf16[4,96,128]{2,1,0:T(8,128)(2,1)S(1)}, u32[]{:S(2)}, u32[]{:S(2)}) collective-permute-start(bf16[4,96,128]{2,1,0:T(8,128)(2,1)S(1)} %get-tuple-element.90), channel_id=1, source_target_pairs={{0,1},{1,0},{4,5},{5,4},{8,9},{9,8},{12,13},{13,12},{2,3},{3,2},{6... | collective-permute-start | bytes 294920 | tf_op jit(solution)/shard_map/ppermute | solution.py:379
  6.9 1.5 %collective-permute-start.2 = (f32[3,20,48]{2,1,0:T(8,128)}, f32[3,20,48]{2,1,0:T(8,128)S(1)}, u32[]{:S(2)}, u32[]{:S(2)}) collective-permute-start(f32[3,20,48]{2,1,0:T(8,128)} %mine.1), channel_id=1, source_target_pairs={{2,0},{0,2},{3,1},{1,3},{6,4},{4,6},{7,5},{5,7},{10,8},{8,10},{11,... | collective-permute-start | bytes 34568 | tf_op jit(solution)/shard_map/ppermute | solution.py:383
  8.4 2.9 %load_all.1 = (bf16[20,96,768]{2,1,0:T(8,128)(2,1)S(1)}, bf16[20,96,384]{2,1,0:T(8,128)(2,1)S(1)}, bf16[29,96,384]{2,1,0:T(8,128)(2,1)S(1)}, f32[20,96,384]{2,1,...) custom-call(bf16[20,96,768]{2,1,0:T(8,128)(2,1)} %blocks_in.1, ...), custom_call_target="tpu_custom_call" | custom-call | flops 1000 | bytes 1000 | tf_op jit(solution)/shard_map/load_all/pallas_call | solution.py:359
  11.3 0.0 collective-permute-done.2.refs_10_
  11.3 0.0 collective-permute-done.1.refs_9_
  11.3 0.0 collective-permute-done.refs_8_
  11.3 2.0 %first_step.1 = (bf16[20,96,768]{2,1,0:T(8,128)(2,1)S(1)}, bf16[20,96,384]{2,1,0:T(8,128)(2,1)S(1)}, bf16[29,96,384]{2,1,0:T(8,128)(2,1)S(1)}, f32[20,96,384]{2,...) custom-call(bf16[20,96,768]{2,1,0:T(8,128)(2,1)S(1)} %get-tuple-elem, ...), custom_call_target="tpu_custom_call", output_to_operand_aliasing={{0}: (0, {}), {1}: (1, {}), {2}: (2, {}), {3}: (3, {}), {4}... | custom-call | flops 1000 | bytes 1000 | tf_op jit(solution)/shard_map/first_step/pallas_call | solution.py:359
  13.3 0.1 collective-permute-start.4
  13.3 0.0 collective-permute-done.3.refs_4_
  13.4 0.3 edge_rows.4
  13.6 2.3 %collective-permute-start.5 = (bf16[4,96,256]{2,1,0:T(8,128)(2,1)S(1)}, bf16[4,96,256]{2,1,0:T(8,128)(2,1)S(1)}, u32[]{:S(2)}, u32[]{:S(2)}) collective-permute-start(bf16[4,96,256]{2,1,0:T(8,128)(2,1)S(1)} %get-tuple-element.125), channel_id=1, source_target_pairs={{1,4},{5,8},{9,12},{13,0},{4,1},{8,5},{12,9},{0,13},{3,6},{7,10},{... | collective-permute-start | bytes 589832 | tf_op jit(solution)/shard_map/ppermute | solution.py:423
  15.9 1.6 %late_rows.1 = (bf16[20,96,768]{2,1,0:T(8,128)(2,1)S(1)}, bf16[20,96,384]{2,1,0:T(8,128)(2,1)S(1)}, bf16[29,96,384]{2,1,0:T(8,128)(2,1)S(1)}, bf16[29,96,384]{2,...) custom-call(bf16[20,96,768]{2,1,0:T(8,128)(2,1)S(1)} %get-tuple-elem, ...), custom_call_target="tpu_custom_call", output_to_operand_aliasing={{0}: (0, {}), {1}: (1, {}), {2}: (2, {}), {3}: (3, {}), {4}... | custom-call | flops 1000 | bytes 1000 | tf_op jit(solution)/shard_map/late_rows/pallas_call | solution.py:359
  17.6 0.2 edge_rows.5
  17.8 1.4 %collective-permute-start.6 = (bf16[4,96,128]{2,1,0:T(8,128)(2,1)S(1)}, bf16[4,96,128]{2,1,0:T(8,128)(2,1)S(1)}, u32[]{:S(2)}, u32[]{:S(2)}) collective-permute-start(bf16[4,96,128]{2,1,0:T(8,128)(2,1)S(1)} %get-tuple-element.131), channel_id=1, source_target_pairs={{1,4},{5,8},{9,12},{13,0},{4,1},{8,5},{12,9},{0,13},{3,6},{7,10},{... | collective-permute-start | bytes 294920 | tf_op jit(solution)/shard_map/ppermute | solution.py:423
  19.2 0.0 collective-permute-done.4.refs_7_
  19.2 3.2 %main_rows.1 = (bf16[20,96,768]{2,1,0:T(8,128)(2,1)S(1)}, bf16[29,96,384]{2,1,0:T(8,128)(2,1)S(1)}, f32[20,96,384]{2,1,0:T(8,128)S(1)}, f32[20,96,384]{2,1,0:T(8...) custom-call(bf16[20,96,768]{2,1,0:T(8,128)(2,1)S(1)} %get-tuple-elem, ...), custom_call_target="tpu_custom_call", output_to_operand_aliasing={{0}: (0, {}), {1}: (1, {}), {2}: (2, {}), {3}: (3, {}), {4}... | custom-call | flops 1000 | bytes 1000 | tf_op jit(solution)/shard_map/main_rows/pallas_call | solution.py:359
  22.4 0.2 collective-permute-done.5.refs_4_
  22.6 0.3 edge_rows.6
  22.9 2.1 %collective-permute-start.8 = (bf16[4,96,256]{2,1,0:T(8,128)(2,1)S(1)}, bf16[4,96,256]{2,1,0:T(8,128)(2,1)S(1)}, u32[]{:S(2)}, u32[]{:S(2)}) collective-permute-start(bf16[4,96,256]{2,1,0:T(8,128)(2,1)S(1)} %get-tuple-element.143), channel_id=1, source_target_pairs={{1,4},{5,8},{9,12},{13,0},{4,1},{8,5},{12,9},{0,13},{3,6},{7,10},{... | collective-permute-start | bytes 589832 | tf_op jit(solution)/shard_map/ppermute | solution.py:423
  25.0 0.0 collective-permute-start.7
  25.0 0.0 collective-permute-done.6.refs_4_
  25.0 0.2 edge_rows.7
  25.2 1.6 %collective-permute-start.9 = (bf16[4,96,128]{2,1,0:T(8,128)(2,1)S(1)}, bf16[4,96,128]{2,1,0:T(8,128)(2,1)S(1)}, u32[]{:S(2)}, u32[]{:S(2)}) collective-permute-start(bf16[4,96,128]{2,1,0:T(8,128)(2,1)S(1)} %get-tuple-element.149), channel_id=1, source_target_pairs={{1,4},{5,8},{9,12},{13,0},{4,1},{8,5},{12,9},{0,13},{3,6},{7,10},{... | collective-permute-start | bytes 294920 | tf_op jit(solution)/shard_map/ppermute | solution.py:423
  26.8 0.0 collective-permute-done.7.refs_6_
  26.8 3.8 %main_last.1 = (bf16[20,96,768]{2,1,0:T(8,128)(2,1)S(1)}, bf16[29,96,384]{2,1,0:T(8,128)(2,1)S(1)}, f32[20,96,384]{2,1,0:T(8,128)S(1)}, f32[20,96,384]{2,1,0:T(8...) custom-call(bf16[20,96,768]{2,1,0:T(8,128)(2,1)S(1)} %get-tuple-elem, ...), custom_call_target="tpu_custom_call", output_to_operand_aliasing={{0}: (0, {}), {1}: (1, {}), {2}: (2, {}), {3}: (3, {}), {4}... | custom-call | flops 1000 | bytes 1000 | tf_op jit(solution)/shard_map/main_last/pallas_call | solution.py:359
  30.6 0.5 %collective-permute-done.8.refs_3_ = bf16[4,96,256]{2,1,0:T(8,128)(2,1)S(1)} collective-permute-done((bf16[4,96,256]{2,1,0:T(8,128)(2,1)S(1)}, bf16[4,96,256]{2,1,0:T(8,128)(2,1)S(1)}, u32[]{:S(2)}, u32[]{:S(2)}) %collective-permute-start.8) | collective-permute-done | bytes 196640 | tf_op jit(solution)/shard_map/ppermute | solution.py:423
  31.1 1.1 %edge_last.2 = (bf16[384,384]{1,0:T(8,128)(2,1)S(1)}, f32[20,96,384]{2,1,0:T(8,128)S(1)}, f32[20,96,384]{2,1,0:T(8,128)S(1)}, bf16[4,96,256]{2,1,0:T(8,128)(2,1)...) custom-call(bf16[384,384]{1,0:T(8,128)(2,1)S(1)} %get-tuple-element., ...), custom_call_target="tpu_custom_call", output_to_operand_aliasing={{0}: (0, {}), {1}: (1, {}), {2}: (2, {}), {3}: (3, {}), {4}... | custom-call | flops 1000 | bytes 1000 | tf_op jit(solution)/shard_map/edge_last/pallas_call | solution.py:441
  32.2 0.0 collective-permute-done.9.refs_3_
  32.2 1.0 %edge_last.3 = (bf16[384,384]{1,0:T(8,128)(2,1)S(1)}, f32[20,96,384]{2,1,0:T(8,128)S(1)}, f32[20,96,384]{2,1,0:T(8,128)S(1)}, bf16[4,96,128]{2,1,0:T(8,128)(2,1)...) custom-call(bf16[384,384]{1,0:T(8,128)(2,1)S(1)} %get-tuple-element., ...), custom_call_target="tpu_custom_call", output_to_operand_aliasing={{0}: (0, {}), {1}: (1, {}), {2}: (2, {}), {3}: (3, {}), {4}... | custom-call | flops 1000 | bytes 1000 | tf_op jit(solution)/shard_map/edge_last/pallas_call | solution.py:441
Async XLA Ops:
  1.8 11.5 %collective-permute-start.3 = (bf16[4,96,384]{2,1,0:T(8,128)(2,1)S(1)}, bf16[4,96,384]{2,1,0:T(8,128)(2,1)S(1)}, u32[]{:S(2)}, u32[]{:S(2)}) collective-permute-start(bf16[4,96,384]{2,1,0:T(8,128)(2,1)S(1)} %get-tuple-element.96), channel_id=1, source_target_pairs={{1,4},{5,8},{9,12},{13,0},{4,1},{8,5},{12,9},{0,13},{3,6},{7,10},{... | collective-permute-start | bytes 884744 | tf_op jit(solution)/shard_map/ppermute | solution.py:380
  6.4 4.9 %collective-permute-start = (bf16[4,96,256]{2,1,0:T(8,128)(2,1)S(1)}, bf16[4,96,256]{2,1,0:T(8,128)(2,1)S(1)}, u32[]{:S(2)}, u32[]{:S(2)}) collective-permute-start(bf16[4,96,256]{2,1,0:T(8,128)(2,1)S(1)} %get-tuple-element.89), channel_id=1, source_target_pairs={{0,1},{1,0},{4,5},{5,4},{8,9},{9,8},{12,13},{13,12},{2,3},{3,2},{6... | collective-permute-start | bytes 589832 | tf_op jit(solution)/shard_map/ppermute | solution.py:379
  6.4 4.9 %collective-permute-start.1 = (bf16[4,96,128]{2,1,0:T(8,128)(2,1)S(1)}, bf16[4,96,128]{2,1,0:T(8,128)(2,1)S(1)}, u32[]{:S(2)}, u32[]{:S(2)}) collective-permute-start(bf16[4,96,128]{2,1,0:T(8,128)(2,1)S(1)} %get-tuple-element.90), channel_id=1, source_target_pairs={{0,1},{1,0},{4,5},{5,4},{8,9},{9,8},{12,13},{13,12},{2,3},{3,2},{6... | collective-permute-start | bytes 294920 | tf_op jit(solution)/shard_map/ppermute | solution.py:379
  6.9 4.4 %collective-permute-start.2 = (f32[3,20,48]{2,1,0:T(8,128)}, f32[3,20,48]{2,1,0:T(8,128)S(1)}, u32[]{:S(2)}, u32[]{:S(2)}) collective-permute-start(f32[3,20,48]{2,1,0:T(8,128)} %mine.1), channel_id=1, source_target_pairs={{2,0},{0,2},{3,1},{1,3},{6,4},{4,6},{7,5},{5,7},{10,8},{8,10},{11,... | collective-permute-start | bytes 34568 | tf_op jit(solution)/shard_map/ppermute | solution.py:383
  13.3 5.9 %collective-permute-start.4 = (bf16[4,96,384]{2,1,0:T(8,128)(2,1)S(1)}, bf16[4,96,384]{2,1,0:T(8,128)(2,1)S(1)}, u32[]{:S(2)}, u32[]{:S(2)}) collective-permute-start(bf16[4,96,384]{2,1,0:T(8,128)(2,1)S(1)} %get-tuple-element.120), channel_id=1, source_target_pairs={{0,1},{1,0},{4,5},{5,4},{8,9},{9,8},{12,13},{13,12},{2,3},{3,2},{6... | collective-permute-start | bytes 884744 | tf_op jit(solution)/shard_map/ppermute | solution.py:406
  13.6 9.0 %collective-permute-start.5 = (bf16[4,96,256]{2,1,0:T(8,128)(2,1)S(1)}, bf16[4,96,256]{2,1,0:T(8,128)(2,1)S(1)}, u32[]{:S(2)}, u32[]{:S(2)}) collective-permute-start(bf16[4,96,256]{2,1,0:T(8,128)(2,1)S(1)} %get-tuple-element.125), channel_id=1, source_target_pairs={{1,4},{5,8},{9,12},{13,0},{4,1},{8,5},{12,9},{0,13},{3,6},{7,10},{... | collective-permute-start | bytes 589832 | tf_op jit(solution)/shard_map/ppermute | solution.py:423
  17.8 7.1 %collective-permute-start.6 = (bf16[4,96,128]{2,1,0:T(8,128)(2,1)S(1)}, bf16[4,96,128]{2,1,0:T(8,128)(2,1)S(1)}, u32[]{:S(2)}, u32[]{:S(2)}) collective-permute-start(bf16[4,96,128]{2,1,0:T(8,128)(2,1)S(1)} %get-tuple-element.131), channel_id=1, source_target_pairs={{1,4},{5,8},{9,12},{13,0},{4,1},{8,5},{12,9},{0,13},{3,6},{7,10},{... | collective-permute-start | bytes 294920 | tf_op jit(solution)/shard_map/ppermute | solution.py:423
  22.9 8.2 %collective-permute-start.8 = (bf16[4,96,256]{2,1,0:T(8,128)(2,1)S(1)}, bf16[4,96,256]{2,1,0:T(8,128)(2,1)S(1)}, u32[]{:S(2)}, u32[]{:S(2)}) collective-permute-start(bf16[4,96,256]{2,1,0:T(8,128)(2,1)S(1)} %get-tuple-element.143), channel_id=1, source_target_pairs={{1,4},{5,8},{9,12},{13,0},{4,1},{8,5},{12,9},{0,13},{3,6},{7,10},{... | collective-permute-start | bytes 589832 | tf_op jit(solution)/shard_map/ppermute | solution.py:423
  25.0 1.8 %collective-permute-start.7 = (bf16[4,96,384]{2,1,0:T(8,128)(2,1)S(1)}, bf16[4,96,384]{2,1,0:T(8,128)(2,1)S(1)}, u32[]{:S(2)}, u32[]{:S(2)}) collective-permute-start(bf16[4,96,384]{2,1,0:T(8,128)(2,1)S(1)} %get-tuple-element.140), channel_id=1, source_target_pairs={{0,1},{1,0},{4,5},{5,4},{8,9},{9,8},{12,13},{13,12},{2,3},{3,2},{6... | collective-permute-start | bytes 884744 | tf_op jit(solution)/shard_map/ppermute | solution.py:415
  25.2 7.0 %collective-permute-start.9 = (bf16[4,96,128]{2,1,0:T(8,128)(2,1)S(1)}, bf16[4,96,128]{2,1,0:T(8,128)(2,1)S(1)}, u32[]{:S(2)}, u32[]{:S(2)}) collective-permute-start(bf16[4,96,128]{2,1,0:T(8,128)(2,1)S(1)} %get-tuple-element.149), channel_id=1, source_target_pairs={{1,4},{5,8},{9,12},{13,0},{4,1},{8,5},{12,9},{0,13},{3,6},{7,10},{... | collective-permute-start | bytes 294920 | tf_op jit(solution)/shard_map/ppermute | solution.py:423

commit v8 on v7

--- a/solution.py
+++ b/solution.py
@@ -10,7 +10,7 @@
 WINDOW = 3
 RING = ("space", "rep")
 VMEM_LIMIT = 24 * 1024 * 1024
-LATE = 8
+LATE = 10
 
 
 def ring_pairs(ring):
@@ -232,7 +232,9 @@
             source = lax.rem(me + 1 + j, pieces)
             turned[s, pl.ds(pl.multiple_of(source * part, 8), part), :] = piece[s].T
         turned[s] = bent[s] * turned[s] * turned[s]
-    spread_rows(turned[WINDOW - 1], coeff)
+    for s in range(WINDOW):
+        spread_rows(turned[s], coeff.at[s])
+    coeff = coeff.at[WINDOW - 1]
     later[rows + 2 * HB] = jnp.zeros(later.shape[1:], later.dtype)
     for j in range(HB):
         for ref, window in zip(halo, windows_of(now.shape[2])):
@@ -249,14 +251,14 @@
     place, blocks, disp0, now, later, disp, vel, mass_b, coeff = refs[-9:]
     rows = disp.shape[0]
     late = min(LATE, rows - 2 * HB)
-    state = (blocks, now, later, disp0, disp, vel, mass_b, coeff, place)
+    state = (blocks, now, later, disp0, disp, vel, mass_b, coeff.at[WINDOW - 1], place)
     full_rows(rows - HB - late, late, *state)
 
 
 def main_rows(step, *refs):
     place, blocks, now, disp, vel, mass_b, turned, coeff, halo, later, out = refs[-11:]
     rows = disp.shape[0]
-    spread_rows(turned[step], coeff)
+    coeff = coeff.at[step]
     side = 1 - lax.axis_index("rep")
     for j in range(HB):
         now[(rows + HB) * side + j] = halo[j]
@@ -296,7 +298,7 @@
 def main_last(*refs):
     place, blocks, now, disp, vel, turned, coeff, halo, disp_out, vel_out, sem = refs[-11:]
     rows = disp.shape[0]
-    spread_rows(turned[0], coeff)
+    coeff = coeff.at[0]
     side = 1 - lax.axis_index("rep")
     for j in range(HB):
         now[(rows + HB) * side + j] = halo[j]
@@ -401,7 +403,7 @@
     blocks, disp0, now, disp, vel, mass_b, _, turned, *_, later, coeff, out_a = call(
         functools.partial(first_step, pieces), "first_step",
         [blocks, disp0, now, disp, vel, mass_b, bent, turned] + halo_a + others, [place], [sm],
-        [ext, like(mass_b), edge_t], [vm] * 3,
+        [ext, pltpu.VMEM((WINDOW, rows, width, 128), f32), edge_t], [vm] * 3,
     )
     halo_a = lax.ppermute(out_a, RING, inner)
     for step in range(WINDOW - 1, 0, -1):

time: 33.4 us -> 33.5 us (level)
  Pallas kernels: 17.7 us -> 18.1 us
  transfers between devices with their start and end apart: 10 -> 10, of which waited for: 2 -> 1; matrix products, arithmetic and copies ran while one was open for 0% -> 0% of each run, Pallas kernels for 47% -> 48%
where the time goes in v8:
time: 33.5 us; the launch traced here: 33.2 us
  Pallas kernels  18.1 us (54%)
  starting transfers between devices  14 us (42%)
  between operations  0.77 us (2%)
  waiting for transfers between devices  0.43 us (1%)
    pallas_call x10, Pallas kernels, call(): pl.pallas_call(kernel, name=name, out_shape=tuple((like(a) for a in held)...  15.9 us
    ppermute x4, starting transfers between devices, body(): sent.append(lax.ppermute(out, RING, outer))  7.33 us
    ppermute x1, starting transfers between devices, body(): whole_b = lax.ppermute(out_b, RING, outer)  4.55 us
    pallas_call x2, Pallas kernels, body(): pl.pallas_call(functools.partial(edge_last, window), name='edge_last', ou...  2.13 us
    ppermute x1, starting transfers between devices, body(): lax.ppermute(states_late, 'ckpt', [((i + j) % pieces, i) for i in range(p...  1.49 us
  transfers between devices with their start and end apart: 10, of which 1 were waited for; matrix products, arithmetic and copies ran while one was open for 0% of the time, Pallas kernels for 48%

profile of v8, /device:TPU:0, one launch (start us, length us, event | category | flops | bytes accessed | tf_op | source)
XLA Modules:
  0.0 33.2 jit_solution(9033012492530009265)
XLA Ops:
  0.6 1.2 %head.1 = (bf16[4,96,384]{2,1,0:T(8,128)(2,1)S(1)}, bf16[4,96,256]{2,1,0:T(8,128)(2,1)S(1)}, bf16[4,96,128]{2,1,0:T(8,128)(2,1)S(1)}) custom-call(bf16[20,96,384]{2,1,0:T(8,128)(2,1)} %vel0.1, f32[20,96]{1,0:T(8,128)} %inv_mass.3), custom_call_target="tpu_custom_call" | custom-call | flops 1000 | bytes 1000 | tf_op jit(solution)/shard_map/head/pallas_call | solution.py:361
  1.8 4.6 %collective-permute-start.3 = (bf16[4,96,384]{2,1,0:T(8,128)(2,1)S(1)}, bf16[4,96,384]{2,1,0:T(8,128)(2,1)S(1)}, u32[]{:S(2)}, u32[]{:S(2)}) collective-permute-start(bf16[4,96,384]{2,1,0:T(8,128)(2,1)S(1)} %get-tuple-element.96), channel_id=1, source_target_pairs={{1,4},{5,8},{9,12},{13,0},{4,1},{8,5},{12,9},{0,13},{3,6},{7,10},{... | collective-permute-start | bytes 884744 | tf_op jit(solution)/shard_map/ppermute | solution.py:382
  6.4 0.0 collective-permute-start
  6.4 0.5 %collective-permute-start.1 = (bf16[4,96,128]{2,1,0:T(8,128)(2,1)S(1)}, bf16[4,96,128]{2,1,0:T(8,128)(2,1)S(1)}, u32[]{:S(2)}, u32[]{:S(2)}) collective-permute-start(bf16[4,96,128]{2,1,0:T(8,128)(2,1)S(1)} %get-tuple-element.90), channel_id=1, source_target_pairs={{0,1},{1,0},{4,5},{5,4},{8,9},{9,8},{12,13},{13,12},{2,3},{3,2},{6... | collective-permute-start | bytes 294920 | tf_op jit(solution)/shard_map/ppermute | solution.py:381
  6.9 1.5 %collective-permute-start.2 = (f32[3,20,48]{2,1,0:T(8,128)}, f32[3,20,48]{2,1,0:T(8,128)S(1)}, u32[]{:S(2)}, u32[]{:S(2)}) collective-permute-start(f32[3,20,48]{2,1,0:T(8,128)} %mine.1), channel_id=1, source_target_pairs={{2,0},{0,2},{3,1},{1,3},{6,4},{4,6},{7,5},{5,7},{10,8},{8,10},{11,... | collective-permute-start | bytes 34568 | tf_op jit(solution)/shard_map/ppermute | solution.py:385
  8.4 2.9 %load_all.1 = (bf16[20,96,768]{2,1,0:T(8,128)(2,1)S(1)}, bf16[20,96,384]{2,1,0:T(8,128)(2,1)S(1)}, bf16[29,96,384]{2,1,0:T(8,128)(2,1)S(1)}, f32[20,96,384]{2,1,...) custom-call(bf16[20,96,768]{2,1,0:T(8,128)(2,1)} %blocks_in.1, ...), custom_call_target="tpu_custom_call" | custom-call | flops 1000 | bytes 1000 | tf_op jit(solution)/shard_map/load_all/pallas_call | solution.py:361
  11.3 0.0 collective-permute-done.2.refs_10_
  11.3 0.0 collective-permute-done.1.refs_9_
  11.3 0.0 collective-permute-done.refs_8_
  11.3 2.1 %first_step.1 = (bf16[20,96,768]{2,1,0:T(8,128)(2,1)S(1)}, bf16[20,96,384]{2,1,0:T(8,128)(2,1)S(1)}, bf16[29,96,384]{2,1,0:T(8,128)(2,1)S(1)}, f32[20,96,384]{2,...) custom-call(bf16[20,96,768]{2,1,0:T(8,128)(2,1)S(1)} %get-tuple-elem, ...), custom_call_target="tpu_custom_call", output_to_operand_aliasing={{0}: (0, {}), {1}: (1, {}), {2}: (2, {}), {3}: (3, {}), {4}... | custom-call | flops 1000 | bytes 1000 | tf_op jit(solution)/shard_map/first_step/pallas_call | solution.py:361
  13.4 0.1 collective-permute-start.4
  13.5 0.0 collective-permute-done.3.refs_4_
  13.5 0.3 edge_rows.4
  13.8 2.2 %collective-permute-start.5 = (bf16[4,96,256]{2,1,0:T(8,128)(2,1)S(1)}, bf16[4,96,256]{2,1,0:T(8,128)(2,1)S(1)}, u32[]{:S(2)}, u32[]{:S(2)}) collective-permute-start(bf16[4,96,256]{2,1,0:T(8,128)(2,1)S(1)} %get-tuple-element.125), channel_id=1, source_target_pairs={{1,4},{5,8},{9,12},{13,0},{4,1},{8,5},{12,9},{0,13},{3,6},{7,10},{... | collective-permute-start | bytes 589832 | tf_op jit(solution)/shard_map/ppermute | solution.py:425
  15.9 1.9 %late_rows.1 = (bf16[20,96,768]{2,1,0:T(8,128)(2,1)S(1)}, bf16[20,96,384]{2,1,0:T(8,128)(2,1)S(1)}, bf16[29,96,384]{2,1,0:T(8,128)(2,1)S(1)}, bf16[29,96,384]{2,...) custom-call(bf16[20,96,768]{2,1,0:T(8,128)(2,1)S(1)} %get-tuple-elem, ...), custom_call_target="tpu_custom_call", output_to_operand_aliasing={{0}: (0, {}), {1}: (1, {}), {2}: (2, {}), {3}: (3, {}), {4}... | custom-call | flops 1000 | bytes 1000 | tf_op jit(solution)/shard_map/late_rows/pallas_call | solution.py:361
  17.8 0.3 edge_rows.5
  18.1 1.5 %collective-permute-start.6 = (bf16[4,96,128]{2,1,0:T(8,128)(2,1)S(1)}, bf16[4,96,128]{2,1,0:T(8,128)(2,1)S(1)}, u32[]{:S(2)}, u32[]{:S(2)}) collective-permute-start(bf16[4,96,128]{2,1,0:T(8,128)(2,1)S(1)} %get-tuple-element.131), channel_id=1, source_target_pairs={{1,4},{5,8},{9,12},{13,0},{4,1},{8,5},{12,9},{0,13},{3,6},{7,10},{... | collective-permute-start | bytes 294920 | tf_op jit(solution)/shard_map/ppermute | solution.py:425
  19.6 0.0 collective-permute-done.4.refs_7_
  19.6 3.1 %main_rows.1 = (bf16[20,96,768]{2,1,0:T(8,128)(2,1)S(1)}, bf16[29,96,384]{2,1,0:T(8,128)(2,1)S(1)}, f32[20,96,384]{2,1,0:T(8,128)S(1)}, f32[20,96,384]{2,1,0:T(8...) custom-call(bf16[20,96,768]{2,1,0:T(8,128)(2,1)S(1)} %get-tuple-elem, ...), custom_call_target="tpu_custom_call", output_to_operand_aliasing={{0}: (0, {}), {1}: (1, {}), {2}: (2, {}), {3}: (3, {}), {4}... | custom-call | flops 1000 | bytes 1000 | tf_op jit(solution)/shard_map/main_rows/pallas_call | solution.py:361
  22.7 0.0 collective-permute-done.5.refs_4_
  22.7 0.3 edge_rows.6
  23.0 2.1 %collective-permute-start.8 = (bf16[4,96,256]{2,1,0:T(8,128)(2,1)S(1)}, bf16[4,96,256]{2,1,0:T(8,128)(2,1)S(1)}, u32[]{:S(2)}, u32[]{:S(2)}) collective-permute-start(bf16[4,96,256]{2,1,0:T(8,128)(2,1)S(1)} %get-tuple-element.143), channel_id=1, source_target_pairs={{1,4},{5,8},{9,12},{13,0},{4,1},{8,5},{12,9},{0,13},{3,6},{7,10},{... | collective-permute-start | bytes 589832 | tf_op jit(solution)/shard_map/ppermute | solution.py:425
  25.1 0.0 collective-permute-start.7
  25.1 0.0 collective-permute-done.6.refs_4_
  25.1 0.2 edge_rows.7
  25.4 1.5 %collective-permute-start.9 = (bf16[4,96,128]{2,1,0:T(8,128)(2,1)S(1)}, bf16[4,96,128]{2,1,0:T(8,128)(2,1)S(1)}, u32[]{:S(2)}, u32[]{:S(2)}) collective-permute-start(bf16[4,96,128]{2,1,0:T(8,128)(2,1)S(1)} %get-tuple-element.149), channel_id=1, source_target_pairs={{1,4},{5,8},{9,12},{13,0},{4,1},{8,5},{12,9},{0,13},{3,6},{7,10},{... | collective-permute-start | bytes 294920 | tf_op jit(solution)/shard_map/ppermute | solution.py:425
  26.9 0.0 collective-permute-done.7.refs_6_
  26.9 3.8 %main_last.1 = (bf16[20,96,768]{2,1,0:T(8,128)(2,1)S(1)}, bf16[29,96,384]{2,1,0:T(8,128)(2,1)S(1)}, f32[20,96,384]{2,1,0:T(8,128)S(1)}, f32[20,96,384]{2,1,0:T(8...) custom-call(bf16[20,96,768]{2,1,0:T(8,128)(2,1)S(1)} %get-tuple-elem, ...), custom_call_target="tpu_custom_call", output_to_operand_aliasing={{0}: (0, {}), {1}: (1, {}), {2}: (2, {}), {3}: (3, {}), {4}... | custom-call | flops 1000 | bytes 1000 | tf_op jit(solution)/shard_map/main_last/pallas_call | solution.py:361
  30.7 0.4 %collective-permute-done.8.refs_3_ = bf16[4,96,256]{2,1,0:T(8,128)(2,1)S(1)} collective-permute-done((bf16[4,96,256]{2,1,0:T(8,128)(2,1)S(1)}, bf16[4,96,256]{2,1,0:T(8,128)(2,1)S(1)}, u32[]{:S(2)}, u32[]{:S(2)}) %collective-permute-start.8) | collective-permute-done | bytes 196640 | tf_op jit(solution)/shard_map/ppermute | solution.py:425
  31.1 1.1 %edge_last.2 = (bf16[384,384]{1,0:T(8,128)(2,1)S(1)}, f32[20,96,384]{2,1,0:T(8,128)S(1)}, f32[20,96,384]{2,1,0:T(8,128)S(1)}, bf16[4,96,256]{2,1,0:T(8,128)(2,1)...) custom-call(bf16[384,384]{1,0:T(8,128)(2,1)S(1)} %get-tuple-element., ...), custom_call_target="tpu_custom_call", output_to_operand_aliasing={{0}: (0, {}), {1}: (1, {}), {2}: (2, {}), {3}: (3, {}), {4}... | custom-call | flops 1000 | bytes 1000 | tf_op jit(solution)/shard_map/edge_last/pallas_call | solution.py:443
  32.2 0.0 collective-permute-done.9.refs_3_
  32.2 1.0 %edge_last.3 = (bf16[384,384]{1,0:T(8,128)(2,1)S(1)}, f32[20,96,384]{2,1,0:T(8,128)S(1)}, f32[20,96,384]{2,1,0:T(8,128)S(1)}, bf16[4,96,128]{2,1,0:T(8,128)(2,1)...) custom-call(bf16[384,384]{1,0:T(8,128)(2,1)S(1)} %get-tuple-element., ...), custom_call_target="tpu_custom_call", output_to_operand_aliasing={{0}: (0, {}), {1}: (1, {}), {2}: (2, {}), {3}: (3, {}), {4}... | custom-call | flops 1000 | bytes 1000 | tf_op jit(solution)/shard_map/edge_last/pallas_call | solution.py:443
Async XLA Ops:
  1.8 11.7 %collective-permute-start.3 = (bf16[4,96,384]{2,1,0:T(8,128)(2,1)S(1)}, bf16[4,96,384]{2,1,0:T(8,128)(2,1)S(1)}, u32[]{:S(2)}, u32[]{:S(2)}) collective-permute-start(bf16[4,96,384]{2,1,0:T(8,128)(2,1)S(1)} %get-tuple-element.96), channel_id=1, source_target_pairs={{1,4},{5,8},{9,12},{13,0},{4,1},{8,5},{12,9},{0,13},{3,6},{7,10},{... | collective-permute-start | bytes 884744 | tf_op jit(solution)/shard_map/ppermute | solution.py:382
  6.4 4.9 %collective-permute-start = (bf16[4,96,256]{2,1,0:T(8,128)(2,1)S(1)}, bf16[4,96,256]{2,1,0:T(8,128)(2,1)S(1)}, u32[]{:S(2)}, u32[]{:S(2)}) collective-permute-start(bf16[4,96,256]{2,1,0:T(8,128)(2,1)S(1)} %get-tuple-element.89), channel_id=1, source_target_pairs={{0,1},{1,0},{4,5},{5,4},{8,9},{9,8},{12,13},{13,12},{2,3},{3,2},{6... | collective-permute-start | bytes 589832 | tf_op jit(solution)/shard_map/ppermute | solution.py:381
  6.4 4.9 %collective-permute-start.1 = (bf16[4,96,128]{2,1,0:T(8,128)(2,1)S(1)}, bf16[4,96,128]{2,1,0:T(8,128)(2,1)S(1)}, u32[]{:S(2)}, u32[]{:S(2)}) collective-permute-start(bf16[4,96,128]{2,1,0:T(8,128)(2,1)S(1)} %get-tuple-element.90), channel_id=1, source_target_pairs={{0,1},{1,0},{4,5},{5,4},{8,9},{9,8},{12,13},{13,12},{2,3},{3,2},{6... | collective-permute-start | bytes 294920 | tf_op jit(solution)/shard_map/ppermute | solution.py:381
  6.9 4.4 %collective-permute-start.2 = (f32[3,20,48]{2,1,0:T(8,128)}, f32[3,20,48]{2,1,0:T(8,128)S(1)}, u32[]{:S(2)}, u32[]{:S(2)}) collective-permute-start(f32[3,20,48]{2,1,0:T(8,128)} %mine.1), channel_id=1, source_target_pairs={{2,0},{0,2},{3,1},{1,3},{6,4},{4,6},{7,5},{5,7},{10,8},{8,10},{11,... | collective-permute-start | bytes 34568 | tf_op jit(solution)/shard_map/ppermute | solution.py:385
  13.4 6.2 %collective-permute-start.4 = (bf16[4,96,384]{2,1,0:T(8,128)(2,1)S(1)}, bf16[4,96,384]{2,1,0:T(8,128)(2,1)S(1)}, u32[]{:S(2)}, u32[]{:S(2)}) collective-permute-start(bf16[4,96,384]{2,1,0:T(8,128)(2,1)S(1)} %get-tuple-element.120), channel_id=1, source_target_pairs={{0,1},{1,0},{4,5},{5,4},{8,9},{9,8},{12,13},{13,12},{2,3},{3,2},{6... | collective-permute-start | bytes 884744 | tf_op jit(solution)/shard_map/ppermute | solution.py:408
  13.8 8.9 %collective-permute-start.5 = (bf16[4,96,256]{2,1,0:T(8,128)(2,1)S(1)}, bf16[4,96,256]{2,1,0:T(8,128)(2,1)S(1)}, u32[]{:S(2)}, u32[]{:S(2)}) collective-permute-start(bf16[4,96,256]{2,1,0:T(8,128)(2,1)S(1)} %get-tuple-element.125), channel_id=1, source_target_pairs={{1,4},{5,8},{9,12},{13,0},{4,1},{8,5},{12,9},{0,13},{3,6},{7,10},{... | collective-permute-start | bytes 589832 | tf_op jit(solution)/shard_map/ppermute | solution.py:425
  18.1 7.0 %collective-permute-start.6 = (bf16[4,96,128]{2,1,0:T(8,128)(2,1)S(1)}, bf16[4,96,128]{2,1,0:T(8,128)(2,1)S(1)}, u32[]{:S(2)}, u32[]{:S(2)}) collective-permute-start(bf16[4,96,128]{2,1,0:T(8,128)(2,1)S(1)} %get-tuple-element.131), channel_id=1, source_target_pairs={{1,4},{5,8},{9,12},{13,0},{4,1},{8,5},{12,9},{0,13},{3,6},{7,10},{... | collective-permute-start | bytes 294920 | tf_op jit(solution)/shard_map/ppermute | solution.py:425
  23.0 8.1 %collective-permute-start.8 = (bf16[4,96,256]{2,1,0:T(8,128)(2,1)S(1)}, bf16[4,96,256]{2,1,0:T(8,128)(2,1)S(1)}, u32[]{:S(2)}, u32[]{:S(2)}) collective-permute-start(bf16[4,96,256]{2,1,0:T(8,128)(2,1)S(1)} %get-tuple-element.143), channel_id=1, source_target_pairs={{1,4},{5,8},{9,12},{13,0},{4,1},{8,5},{12,9},{0,13},{3,6},{7,10},{... | collective-permute-start | bytes 589832 | tf_op jit(solution)/shard_map/ppermute | solution.py:425
  25.1 1.8 %collective-permute-start.7 = (bf16[4,96,384]{2,1,0:T(8,128)(2,1)S(1)}, bf16[4,96,384]{2,1,0:T(8,128)(2,1)S(1)}, u32[]{:S(2)}, u32[]{:S(2)}) collective-permute-start(bf16[4,96,384]{2,1,0:T(8,128)(2,1)S(1)} %get-tuple-element.140), channel_id=1, source_target_pairs={{0,1},{1,0},{4,5},{5,4},{8,9},{9,8},{12,13},{13,12},{2,3},{3,2},{6... | collective-permute-start | bytes 884744 | tf_op jit(solution)/shard_map/ppermute | solution.py:417
  25.4 6.8 %collective-permute-start.9 = (bf16[4,96,128]{2,1,0:T(8,128)(2,1)S(1)}, bf16[4,96,128]{2,1,0:T(8,128)(2,1)S(1)}, u32[]{:S(2)}, u32[]{:S(2)}) collective-permute-start(bf16[4,96,128]{2,1,0:T(8,128)(2,1)S(1)} %get-tuple-element.149), channel_id=1, source_target_pairs={{1,4},{5,8},{9,12},{13,0},{4,1},{8,5},{12,9},{0,13},{3,6},{7,10},{... | collective-permute-start | bytes 294920 | tf_op jit(solution)/shard_map/ppermute | solution.py:425

commit v9 on v8

--- a/solution.py
+++ b/solution.py
@@ -323,12 +323,10 @@
     rows, width, _ = disp.shape
     start = (rows - HB) * lax.axis_index("rep")
     image = far_part(dense, halo, window)
-    sent = []
     for i in range(HB):
         part = image[i * width : (i + 1) * width]
         finish_row(start + i, part, None, disp, vel, None, window)
-        sent += begin(row_copies(disp, vel, disp_out, vel_out, sem, start + i, 1, i, window))
-    end(sent)
+    end(begin(row_copies(disp, vel, disp_out, vel_out, sem, start, HB, 0, window)))
 
 
 def body(adj_disp, adj_vel, tangent_blocks, block_cols, inv_mass, joint_stiff, contact, states):

time: 33.5 us -> 33.6 us (level)
  no operation moved by 1% of the time
where the time goes in v9:
time: 33.6 us; the launch traced here: 33.3 us
  Pallas kernels  18.2 us (54%)
  starting transfers between devices  14 us (42%)
  between operations  0.77 us (2%)
  waiting for transfers between devices  0.44 us (1%)
    pallas_call x10, Pallas kernels, call(): pl.pallas_call(kernel, name=name, out_shape=tuple((like(a) for a in held)...  15.9 us
    ppermute x4, starting transfers between devices, body(): sent.append(lax.ppermute(out, RING, outer))  7.34 us
    ppermute x1, starting transfers between devices, body(): whole_b = lax.ppermute(out_b, RING, outer)  4.55 us
    pallas_call x2, Pallas kernels, body(): pl.pallas_call(functools.partial(edge_last, window), name='edge_last', ou...  2.26 us
    ppermute x1, starting transfers between devices, body(): lax.ppermute(states_late, 'ckpt', [((i + j) % pieces, i) for i in range(p...  1.49 us
  transfers between devices with their start and end apart: 10, of which 1 were waited for; matrix products, arithmetic and copies ran while one was open for 0% of the time, Pallas kernels for 48%

profile of v9, /device:TPU:0, one launch (start us, length us, event | category | flops | bytes accessed | tf_op | source)
XLA Modules:
  0.0 33.3 jit_solution(341867625312761687)
XLA Ops:
  0.6 1.2 %head.1 = (bf16[4,96,384]{2,1,0:T(8,128)(2,1)S(1)}, bf16[4,96,256]{2,1,0:T(8,128)(2,1)S(1)}, bf16[4,96,128]{2,1,0:T(8,128)(2,1)S(1)}) custom-call(bf16[20,96,384]{2,1,0:T(8,128)(2,1)} %vel0.1, f32[20,96]{1,0:T(8,128)} %inv_mass.3), custom_call_target="tpu_custom_call" | custom-call | flops 1000 | bytes 1000 | tf_op jit(solution)/shard_map/head/pallas_call | solution.py:359
  1.8 4.6 %collective-permute-start.3 = (bf16[4,96,384]{2,1,0:T(8,128)(2,1)S(1)}, bf16[4,96,384]{2,1,0:T(8,128)(2,1)S(1)}, u32[]{:S(2)}, u32[]{:S(2)}) collective-permute-start(bf16[4,96,384]{2,1,0:T(8,128)(2,1)S(1)} %get-tuple-element.96), channel_id=1, source_target_pairs={{1,4},{5,8},{9,12},{13,0},{4,1},{8,5},{12,9},{0,13},{3,6},{7,10},{... | collective-permute-start | bytes 884744 | tf_op jit(solution)/shard_map/ppermute | solution.py:380
  6.4 0.0 collective-permute-start
  6.4 0.5 %collective-permute-start.1 = (bf16[4,96,128]{2,1,0:T(8,128)(2,1)S(1)}, bf16[4,96,128]{2,1,0:T(8,128)(2,1)S(1)}, u32[]{:S(2)}, u32[]{:S(2)}) collective-permute-start(bf16[4,96,128]{2,1,0:T(8,128)(2,1)S(1)} %get-tuple-element.90), channel_id=1, source_target_pairs={{0,1},{1,0},{4,5},{5,4},{8,9},{9,8},{12,13},{13,12},{2,3},{3,2},{6... | collective-permute-start | bytes 294920 | tf_op jit(solution)/shard_map/ppermute | solution.py:379
  6.9 1.5 %collective-permute-start.2 = (f32[3,20,48]{2,1,0:T(8,128)}, f32[3,20,48]{2,1,0:T(8,128)S(1)}, u32[]{:S(2)}, u32[]{:S(2)}) collective-permute-start(f32[3,20,48]{2,1,0:T(8,128)} %mine.1), channel_id=1, source_target_pairs={{2,0},{0,2},{3,1},{1,3},{6,4},{4,6},{7,5},{5,7},{10,8},{8,10},{11,... | collective-permute-start | bytes 34568 | tf_op jit(solution)/shard_map/ppermute | solution.py:383
  8.4 2.9 %load_all.1 = (bf16[20,96,768]{2,1,0:T(8,128)(2,1)S(1)}, bf16[20,96,384]{2,1,0:T(8,128)(2,1)S(1)}, bf16[29,96,384]{2,1,0:T(8,128)(2,1)S(1)}, f32[20,96,384]{2,1,...) custom-call(bf16[20,96,768]{2,1,0:T(8,128)(2,1)} %blocks_in.1, ...), custom_call_target="tpu_custom_call" | custom-call | flops 1000 | bytes 1000 | tf_op jit(solution)/shard_map/load_all/pallas_call | solution.py:359
  11.3 0.0 collective-permute-done.2.refs_10_
  11.3 0.0 collective-permute-done.1.refs_9_
  11.3 0.0 collective-permute-done.refs_8_
  11.3 2.1 %first_step.1 = (bf16[20,96,768]{2,1,0:T(8,128)(2,1)S(1)}, bf16[20,96,384]{2,1,0:T(8,128)(2,1)S(1)}, bf16[29,96,384]{2,1,0:T(8,128)(2,1)S(1)}, f32[20,96,384]{2,...) custom-call(bf16[20,96,768]{2,1,0:T(8,128)(2,1)S(1)} %get-tuple-elem, ...), custom_call_target="tpu_custom_call", output_to_operand_aliasing={{0}: (0, {}), {1}: (1, {}), {2}: (2, {}), {3}: (3, {}), {4}... | custom-call | flops 1000 | bytes 1000 | tf_op jit(solution)/shard_map/first_step/pallas_call | solution.py:359
  13.4 0.1 collective-permute-start.4
  13.5 0.0 collective-permute-done.3.refs_4_
  13.5 0.3 edge_rows.4
  13.8 2.2 %collective-permute-start.5 = (bf16[4,96,256]{2,1,0:T(8,128)(2,1)S(1)}, bf16[4,96,256]{2,1,0:T(8,128)(2,1)S(1)}, u32[]{:S(2)}, u32[]{:S(2)}) collective-permute-start(bf16[4,96,256]{2,1,0:T(8,128)(2,1)S(1)} %get-tuple-element.125), channel_id=1, source_target_pairs={{1,4},{5,8},{9,12},{13,0},{4,1},{8,5},{12,9},{0,13},{3,6},{7,10},{... | collective-permute-start | bytes 589832 | tf_op jit(solution)/shard_map/ppermute | solution.py:423
  15.9 1.9 %late_rows.1 = (bf16[20,96,768]{2,1,0:T(8,128)(2,1)S(1)}, bf16[20,96,384]{2,1,0:T(8,128)(2,1)S(1)}, bf16[29,96,384]{2,1,0:T(8,128)(2,1)S(1)}, bf16[29,96,384]{2,...) custom-call(bf16[20,96,768]{2,1,0:T(8,128)(2,1)S(1)} %get-tuple-elem, ...), custom_call_target="tpu_custom_call", output_to_operand_aliasing={{0}: (0, {}), {1}: (1, {}), {2}: (2, {}), {3}: (3, {}), {4}... | custom-call | flops 1000 | bytes 1000 | tf_op jit(solution)/shard_map/late_rows/pallas_call | solution.py:359
  17.8 0.3 edge_rows.5
  18.1 1.5 %collective-permute-start.6 = (bf16[4,96,128]{2,1,0:T(8,128)(2,1)S(1)}, bf16[4,96,128]{2,1,0:T(8,128)(2,1)S(1)}, u32[]{:S(2)}, u32[]{:S(2)}) collective-permute-start(bf16[4,96,128]{2,1,0:T(8,128)(2,1)S(1)} %get-tuple-element.131), channel_id=1, source_target_pairs={{1,4},{5,8},{9,12},{13,0},{4,1},{8,5},{12,9},{0,13},{3,6},{7,10},{... | collective-permute-start | bytes 294920 | tf_op jit(solution)/shard_map/ppermute | solution.py:423
  19.5 0.0 collective-permute-done.4.refs_7_
  19.5 3.1 %main_rows.1 = (bf16[20,96,768]{2,1,0:T(8,128)(2,1)S(1)}, bf16[29,96,384]{2,1,0:T(8,128)(2,1)S(1)}, f32[20,96,384]{2,1,0:T(8,128)S(1)}, f32[20,96,384]{2,1,0:T(8...) custom-call(bf16[20,96,768]{2,1,0:T(8,128)(2,1)S(1)} %get-tuple-elem, ...), custom_call_target="tpu_custom_call", output_to_operand_aliasing={{0}: (0, {}), {1}: (1, {}), {2}: (2, {}), {3}: (3, {}), {4}... | custom-call | flops 1000 | bytes 1000 | tf_op jit(solution)/shard_map/main_rows/pallas_call | solution.py:359
  22.7 0.0 collective-permute-done.5.refs_4_
  22.7 0.3 edge_rows.6
  22.9 2.2 %collective-permute-start.8 = (bf16[4,96,256]{2,1,0:T(8,128)(2,1)S(1)}, bf16[4,96,256]{2,1,0:T(8,128)(2,1)S(1)}, u32[]{:S(2)}, u32[]{:S(2)}) collective-permute-start(bf16[4,96,256]{2,1,0:T(8,128)(2,1)S(1)} %get-tuple-element.143), channel_id=1, source_target_pairs={{1,4},{5,8},{9,12},{13,0},{4,1},{8,5},{12,9},{0,13},{3,6},{7,10},{... | collective-permute-start | bytes 589832 | tf_op jit(solution)/shard_map/ppermute | solution.py:423
  25.1 0.0 collective-permute-start.7
  25.1 0.0 collective-permute-done.6.refs_4_
  25.1 0.2 edge_rows.7
  25.4 1.5 %collective-permute-start.9 = (bf16[4,96,128]{2,1,0:T(8,128)(2,1)S(1)}, bf16[4,96,128]{2,1,0:T(8,128)(2,1)S(1)}, u32[]{:S(2)}, u32[]{:S(2)}) collective-permute-start(bf16[4,96,128]{2,1,0:T(8,128)(2,1)S(1)} %get-tuple-element.149), channel_id=1, source_target_pairs={{1,4},{5,8},{9,12},{13,0},{4,1},{8,5},{12,9},{0,13},{3,6},{7,10},{... | collective-permute-start | bytes 294920 | tf_op jit(solution)/shard_map/ppermute | solution.py:423
  26.9 0.0 collective-permute-done.7.refs_6_
  26.9 3.7 %main_last.1 = (bf16[20,96,768]{2,1,0:T(8,128)(2,1)S(1)}, bf16[29,96,384]{2,1,0:T(8,128)(2,1)S(1)}, f32[20,96,384]{2,1,0:T(8,128)S(1)}, f32[20,96,384]{2,1,0:T(8...) custom-call(bf16[20,96,768]{2,1,0:T(8,128)(2,1)S(1)} %get-tuple-elem, ...), custom_call_target="tpu_custom_call", output_to_operand_aliasing={{0}: (0, {}), {1}: (1, {}), {2}: (2, {}), {3}: (3, {}), {4}... | custom-call | flops 1000 | bytes 1000 | tf_op jit(solution)/shard_map/main_last/pallas_call | solution.py:359
  30.6 0.4 %collective-permute-done.8.refs_3_ = bf16[4,96,256]{2,1,0:T(8,128)(2,1)S(1)} collective-permute-done((bf16[4,96,256]{2,1,0:T(8,128)(2,1)S(1)}, bf16[4,96,256]{2,1,0:T(8,128)(2,1)S(1)}, u32[]{:S(2)}, u32[]{:S(2)}) %collective-permute-start.8) | collective-permute-done | bytes 196640 | tf_op jit(solution)/shard_map/ppermute | solution.py:423
  31.1 1.2 %edge_last.2 = (bf16[384,384]{1,0:T(8,128)(2,1)S(1)}, f32[20,96,384]{2,1,0:T(8,128)S(1)}, f32[20,96,384]{2,1,0:T(8,128)S(1)}, bf16[4,96,256]{2,1,0:T(8,128)(2,1)...) custom-call(bf16[384,384]{1,0:T(8,128)(2,1)S(1)} %get-tuple-element., ...), custom_call_target="tpu_custom_call", output_to_operand_aliasing={{0}: (0, {}), {1}: (1, {}), {2}: (2, {}), {3}: (3, {}), {4}... | custom-call | flops 1000 | bytes 1000 | tf_op jit(solution)/shard_map/edge_last/pallas_call | solution.py:441
  32.3 0.0 collective-permute-done.9.refs_3_
  32.3 1.1 %edge_last.3 = (bf16[384,384]{1,0:T(8,128)(2,1)S(1)}, f32[20,96,384]{2,1,0:T(8,128)S(1)}, f32[20,96,384]{2,1,0:T(8,128)S(1)}, bf16[4,96,128]{2,1,0:T(8,128)(2,1)...) custom-call(bf16[384,384]{1,0:T(8,128)(2,1)S(1)} %get-tuple-element., ...), custom_call_target="tpu_custom_call", output_to_operand_aliasing={{0}: (0, {}), {1}: (1, {}), {2}: (2, {}), {3}: (3, {}), {4}... | custom-call | flops 1000 | bytes 1000 | tf_op jit(solution)/shard_map/edge_last/pallas_call | solution.py:441
Async XLA Ops:
  1.8 11.6 %collective-permute-start.3 = (bf16[4,96,384]{2,1,0:T(8,128)(2,1)S(1)}, bf16[4,96,384]{2,1,0:T(8,128)(2,1)S(1)}, u32[]{:S(2)}, u32[]{:S(2)}) collective-permute-start(bf16[4,96,384]{2,1,0:T(8,128)(2,1)S(1)} %get-tuple-element.96), channel_id=1, source_target_pairs={{1,4},{5,8},{9,12},{13,0},{4,1},{8,5},{12,9},{0,13},{3,6},{7,10},{... | collective-permute-start | bytes 884744 | tf_op jit(solution)/shard_map/ppermute | solution.py:380
  6.4 4.9 %collective-permute-start = (bf16[4,96,256]{2,1,0:T(8,128)(2,1)S(1)}, bf16[4,96,256]{2,1,0:T(8,128)(2,1)S(1)}, u32[]{:S(2)}, u32[]{:S(2)}) collective-permute-start(bf16[4,96,256]{2,1,0:T(8,128)(2,1)S(1)} %get-tuple-element.89), channel_id=1, source_target_pairs={{0,1},{1,0},{4,5},{5,4},{8,9},{9,8},{12,13},{13,12},{2,3},{3,2},{6... | collective-permute-start | bytes 589832 | tf_op jit(solution)/shard_map/ppermute | solution.py:379
  6.4 4.9 %collective-permute-start.1 = (bf16[4,96,128]{2,1,0:T(8,128)(2,1)S(1)}, bf16[4,96,128]{2,1,0:T(8,128)(2,1)S(1)}, u32[]{:S(2)}, u32[]{:S(2)}) collective-permute-start(bf16[4,96,128]{2,1,0:T(8,128)(2,1)S(1)} %get-tuple-element.90), channel_id=1, source_target_pairs={{0,1},{1,0},{4,5},{5,4},{8,9},{9,8},{12,13},{13,12},{2,3},{3,2},{6... | collective-permute-start | bytes 294920 | tf_op jit(solution)/shard_map/ppermute | solution.py:379
  6.9 4.4 %collective-permute-start.2 = (f32[3,20,48]{2,1,0:T(8,128)}, f32[3,20,48]{2,1,0:T(8,128)S(1)}, u32[]{:S(2)}, u32[]{:S(2)}) collective-permute-start(f32[3,20,48]{2,1,0:T(8,128)} %mine.1), channel_id=1, source_target_pairs={{2,0},{0,2},{3,1},{1,3},{6,4},{4,6},{7,5},{5,7},{10,8},{8,10},{11,... | collective-permute-start | bytes 34568 | tf_op jit(solution)/shard_map/ppermute | solution.py:383
  13.4 6.1 %collective-permute-start.4 = (bf16[4,96,384]{2,1,0:T(8,128)(2,1)S(1)}, bf16[4,96,384]{2,1,0:T(8,128)(2,1)S(1)}, u32[]{:S(2)}, u32[]{:S(2)}) collective-permute-start(bf16[4,96,384]{2,1,0:T(8,128)(2,1)S(1)} %get-tuple-element.120), channel_id=1, source_target_pairs={{0,1},{1,0},{4,5},{5,4},{8,9},{9,8},{12,13},{13,12},{2,3},{3,2},{6... | collective-permute-start | bytes 884744 | tf_op jit(solution)/shard_map/ppermute | solution.py:406
  13.8 8.9 %collective-permute-start.5 = (bf16[4,96,256]{2,1,0:T(8,128)(2,1)S(1)}, bf16[4,96,256]{2,1,0:T(8,128)(2,1)S(1)}, u32[]{:S(2)}, u32[]{:S(2)}) collective-permute-start(bf16[4,96,256]{2,1,0:T(8,128)(2,1)S(1)} %get-tuple-element.125), channel_id=1, source_target_pairs={{1,4},{5,8},{9,12},{13,0},{4,1},{8,5},{12,9},{0,13},{3,6},{7,10},{... | collective-permute-start | bytes 589832 | tf_op jit(solution)/shard_map/ppermute | solution.py:423
  18.1 7.0 %collective-permute-start.6 = (bf16[4,96,128]{2,1,0:T(8,128)(2,1)S(1)}, bf16[4,96,128]{2,1,0:T(8,128)(2,1)S(1)}, u32[]{:S(2)}, u32[]{:S(2)}) collective-permute-start(bf16[4,96,128]{2,1,0:T(8,128)(2,1)S(1)} %get-tuple-element.131), channel_id=1, source_target_pairs={{1,4},{5,8},{9,12},{13,0},{4,1},{8,5},{12,9},{0,13},{3,6},{7,10},{... | collective-permute-start | bytes 294920 | tf_op jit(solution)/shard_map/ppermute | solution.py:423
  22.9 8.1 %collective-permute-start.8 = (bf16[4,96,256]{2,1,0:T(8,128)(2,1)S(1)}, bf16[4,96,256]{2,1,0:T(8,128)(2,1)S(1)}, u32[]{:S(2)}, u32[]{:S(2)}) collective-permute-start(bf16[4,96,256]{2,1,0:T(8,128)(2,1)S(1)} %get-tuple-element.143), channel_id=1, source_target_pairs={{1,4},{5,8},{9,12},{13,0},{4,1},{8,5},{12,9},{0,13},{3,6},{7,10},{... | collective-permute-start | bytes 589832 | tf_op jit(solution)/shard_map/ppermute | solution.py:423
  25.1 1.8 %collective-permute-start.7 = (bf16[4,96,384]{2,1,0:T(8,128)(2,1)S(1)}, bf16[4,96,384]{2,1,0:T(8,128)(2,1)S(1)}, u32[]{:S(2)}, u32[]{:S(2)}) collective-permute-start(bf16[4,96,384]{2,1,0:T(8,128)(2,1)S(1)} %get-tuple-element.140), channel_id=1, source_target_pairs={{0,1},{1,0},{4,5},{5,4},{8,9},{9,8},{12,13},{13,12},{2,3},{3,2},{6... | collective-permute-start | bytes 884744 | tf_op jit(solution)/shard_map/ppermute | solution.py:415
  25.4 6.9 %collective-permute-start.9 = (bf16[4,96,128]{2,1,0:T(8,128)(2,1)S(1)}, bf16[4,96,128]{2,1,0:T(8,128)(2,1)S(1)}, u32[]{:S(2)}, u32[]{:S(2)}) collective-permute-start(bf16[4,96,128]{2,1,0:T(8,128)(2,1)S(1)} %get-tuple-element.149), channel_id=1, source_target_pairs={{1,4},{5,8},{9,12},{13,0},{4,1},{8,5},{12,9},{0,13},{3,6},{7,10},{... | collective-permute-start | bytes 294920 | tf_op jit(solution)/shard_map/ppermute | solution.py:423
